TPU v7x, 256 devices: a whole 4x4x8 slice. The times are simulated.
256 devices in a mesh: dp: 8 (over z_lo, x), ctx: 32 (over z_hi, y, core).
Axes of the slice: x: 4, y: 4, z: 8 (z_hi: 4, z_lo: 2; z = z_hi * 2 + z_lo), core: 2. Of those that a mesh axis runs over, the one named last changes fastest.
Arguments:
- tokens: bfloat16 [8, 4096, 4096], P('dp', 'ctx'), may hold values from -6 to 6
- proj_weight: bfloat16 [4096, 512], P('dp'), may hold values from -0.09375 to 0.09375
- values: bfloat16 [8, 4096, 2048], P('dp', 'ctx'), may hold values from -60 to 60
- grad_out: bfloat16 [8, 4096, 2048], P('dp', 'ctx'), may hold values from -6 to 6
Outputs:
- attended: bfloat16 [8, 4096, 2048], P('dp', 'ctx')
- grad_tokens: bfloat16 [8, 4096, 4096], P('dp', 'ctx')
- grad_values: bfloat16 [8, 4096, 2048], P('dp', 'ctx')
- grad_proj: float32 [4096, 512], P(('dp', 'ctx'))
All inputs are finite; a program needn't handle non-finite values.
Results may differ from a plain program's by a relative error of at most 0.0049.
Values may be sent and summed in bfloat16 or wider, within the bound.
A program may use at most 192 MiB of HBM per device.

v0:
```python
import jax
import jax.numpy as jnp
from jax import lax
from jax.sharding import PartitionSpec as P

H = 16
F = 16
DH = 128


HIGHEST = lax.Precision.HIGHEST
QUAD_SCALE = 0.17677669529663687
EPSILON = 1e-05


def features(inputs):
    count_heads, count_rows, count_feat = inputs.shape
    linear = jnp.swapaxes(inputs, 1, 2) * 0.5
    square = (inputs[:, :, :, None] * inputs[:, :, None, :]).reshape(
        count_heads, count_rows, count_feat * count_feat
    )
    square = jnp.swapaxes(square, 1, 2) * QUAD_SCALE
    constant_row = jnp.ones((count_heads, 1, count_rows), inputs.dtype)
    return jnp.concatenate([constant_row, linear, square], axis=1)


def block_kernel(query_part, key_part):
    count_rows = query_part.shape[1]
    causal = lax.broadcasted_iota(jnp.int32, (count_rows, count_rows), 0) >= lax.broadcasted_iota(
        jnp.int32, (count_rows, count_rows), 1
    )
    scores = jnp.einsum("htf,hsf->hts", query_part, key_part, precision=HIGHEST) * 0.25
    kernel = jnp.where(causal, 1.0 + scores + 0.5 * scores * scores, 0.0)
    return (causal, scores, kernel)


def normalize(numerator):
    inv_rms = lax.rsqrt(jnp.mean(numerator * numerator, axis=-1, keepdims=True) + EPSILON)
    return (inv_rms, numerator * inv_rms)


def grad_normalize(inv_rms, normed, upstream):
    return inv_rms * (upstream - normed * jnp.mean(normed * upstream, axis=-1, keepdims=True))


def local_backward(
    query_part,
    key_part,
    value_part,
    grad_num,
    causal,
    scores,
    kernel,
    pull_query,
    pull_key,
    feat_key,
    prefix,
    suffix,
):
    mixing = jnp.where(
        causal, jnp.einsum("htd,hsd->hts", grad_num, value_part, precision=HIGHEST), 0.0
    )
    slope = mixing * (1.0 + scores)
    grad_query = jnp.einsum("hts,hsf->htf", slope, key_part, precision=HIGHEST) * 0.25
    grad_key = jnp.einsum("hts,htf->hsf", slope, query_part, precision=HIGHEST) * 0.25
    grad_query = (
        grad_query + pull_query(jnp.einsum("hed,htd->het", prefix, grad_num, precision=HIGHEST))[0]
    )
    grad_key = (
        grad_key + pull_key(jnp.einsum("hed,htd->het", suffix, value_part, precision=HIGHEST))[0]
    )
    grad_value = jnp.einsum("hts,htd->hsd", kernel, grad_num, precision=HIGHEST)
    grad_value = grad_value + jnp.einsum("het,hed->htd", feat_key, suffix, precision=HIGHEST)
    return (grad_query, grad_key, grad_value)


def split_heads(matrix, size):
    return jnp.swapaxes(matrix.reshape(matrix.shape[0], -1, size), 0, 1)


def merge_heads(blocked):
    return jnp.swapaxes(blocked, 0, 1).reshape(blocked.shape[1], -1)


def local(tokens, proj_weight, values, grad_out):
    token_rows = tokens[0]
    query_cols = H * F
    projected = jnp.dot(
        token_rows,
        lax.all_gather(proj_weight, "dp", axis=0, tiled=True),
        preferred_element_type=jnp.float32,
    )
    query_part = split_heads(projected[:, :query_cols], F)
    key_part = split_heads(projected[:, query_cols:], F)
    value_part = split_heads(values[0].astype(jnp.float32), DH)
    upstream = split_heads(grad_out[0].astype(jnp.float32), DH)
    feat_query, pull_query = jax.vjp(features, query_part)
    feat_key, pull_key = jax.vjp(features, key_part)
    local_term = jnp.einsum("het,htd->hed", feat_key, value_part, precision=HIGHEST)
    columns_in = lax.all_to_all(
        local_term.reshape(1, -1), "ctx", split_axis=1, concat_axis=0, tiled=True
    )
    shifted = jnp.concatenate([jnp.zeros_like(columns_in[:1]), columns_in[:-1]], axis=0)
    running = jnp.cumsum(shifted, axis=0)
    prefix = lax.all_to_all(running, "ctx", split_axis=0, concat_axis=1, tiled=True).reshape(
        local_term.shape
    )
    causal, scores, kernel = block_kernel(query_part, key_part)
    numerator = jnp.einsum("hts,hsd->htd", kernel, value_part, precision=HIGHEST)
    numerator = numerator + jnp.einsum("het,hed->htd", feat_query, prefix, precision=HIGHEST)
    inv_rms, normed = normalize(numerator)
    attended = merge_heads(normed).astype(jnp.bfloat16)
    grad_num = grad_normalize(inv_rms, normed, upstream)
    carried = jnp.einsum("het,htd->hed", feat_query, grad_num, precision=HIGHEST)
    later_in = lax.all_to_all(
        carried.reshape(1, -1), "ctx", split_axis=1, concat_axis=0, tiled=True
    )
    later_shift = jnp.concatenate([later_in[1:], jnp.zeros_like(later_in[:1])], axis=0)
    later_running = jnp.cumsum(later_shift[::-1], axis=0)[::-1]
    suffix = lax.all_to_all(later_running, "ctx", split_axis=0, concat_axis=1, tiled=True).reshape(
        carried.shape
    )
    grad_query, grad_key, grad_value = local_backward(
        query_part,
        key_part,
        value_part,
        grad_num,
        causal,
        scores,
        kernel,
        pull_query,
        pull_key,
        feat_key,
        prefix,
        suffix,
    )
    grad_proj_rows = jnp.concatenate(
        [merge_heads(grad_query), merge_heads(grad_key)], axis=1
    ).astype(jnp.bfloat16)
    grad_tokens = lax.dot_general(
        grad_proj_rows,
        lax.all_gather(proj_weight, "dp", axis=0, tiled=True),
        (((1,), (1,)), ((), ())),
        preferred_element_type=jnp.float32,
    ).astype(jnp.bfloat16)
    grad_proj = lax.psum_scatter(
        lax.dot_general(
            token_rows, grad_proj_rows, (((0,), (0,)), ((), ())), preferred_element_type=jnp.float32
        ),
        ("dp", "ctx"),
        scatter_dimension=0,
        tiled=True,
    )
    grad_values = merge_heads(grad_value).astype(jnp.bfloat16)
    return (attended[None], grad_tokens[None], grad_values[None], grad_proj)


def solution(mesh):
    return jax.shard_map(
        local,
        mesh=mesh,
        in_specs=(P("dp", "ctx", None), P("dp", None), P("dp", "ctx", None), P("dp", "ctx", None)),
        out_specs=(
            P("dp", "ctx", None),
            P("dp", "ctx", None),
            P("dp", "ctx", None),
            P(("dp", "ctx"), None),
        ),
        check_vma=False,
    )
```

profile of v0, /device:TPU:32, one launch (start us, length us, event | category | flops | bytes accessed | tf_op | source)
XLA Modules:
  0.0 2036.4 jit_solution(6238759362847132041)
XLA Ops:
  7.2 0.7 all-gather.2.cloned.1.call-update
  7.9 1.1 copy.57
  9.1 57.5 %all-gather.2.cloned.1.call-done = bf16[4096,512]{1,0:T(8,128)(2,1)} async-done(((bf16[512,512]{1,0:T(8,128)(2,1)}), bf16[4096,512]{1,0:T(8,128)(2,1)}) %all-gather.2.cloned.1.call-update) | async-done | bytes 4194320 | tf_op jit(solution)/shard_map/all_gather | solution.py:90
  66.6 2.9 fusion.20
  69.5 0.7 fusion.59
  70.3 0.3 multiply_multiply_fusion
  70.6 0.3 copy-done.14
  70.9 1.0 copy-done.3
  71.9 3.5 fusion.3
  75.4 4.0 all_to_all.45
  79.4 65.7 %all_to_all.51 = f32[1,32,17472]{2,0,1:T(1,128)S(1)} all-to-all(f32[1,32,17472]{2,0,1:T(1,128)S(1)} %all_to_all.45), channel_id=1, replica_groups=mesh['dp'=8,'ctx'=32] {'ctx'}, dimensions={1} | all-to-all | bytes 4472832 | tf_op jit(solution)/shard_map/all_to_all | solution.py:100
  145.1 2.6 fusion.1
  147.6 4.2 all-to-all-start.1
  151.9 2.2 copy.39
  154.1 1.7 copy.34
  155.8 1.6 multiply_bitcast_fusion.1
  157.4 3.7 fusion.60
  161.0 2.6 multiply_multiply_fusion.1
  163.6 43.2 %all-to-all-done.1 = f32[32,1,17472]{2,1,0:T(1,128)S(1)} async-done(((f32[32,1,17472]{2,1,0:T(1,128)}), f32[32,1,17472]{2,1,0:T(1,128)S(1)}, u32[]{:S(2)}, u32[]{:S(2)}) %all-to-all-start.1) | async-done | bytes 2236448 | tf_op jit(solution)/shard_map/all_to_all | solution.py:105
  206.8 7.3 reduce
  214.1 2.4 reshape.141
  216.6 7.7 fusion.5
  224.4 1.4 multiply_reduce_fusion.5
  225.8 0.2 multiply_reduce_fusion.4
  226.0 0.8 copy-done.6
  226.8 0.2 subtract_multiply_fusion
  227.0 0.7 copy-done.2
  227.7 5.2 fusion.4
  233.0 5.1 all_to_all.46
  238.1 60.0 %all_to_all.52 = f32[1,32,17472]{2,0,1:T(1,128)S(1)} all-to-all(f32[1,32,17472]{2,0,1:T(1,128)} %all_to_all.46), channel_id=1, replica_groups=mesh['dp'=8,'ctx'=32] {'ctx'}, dimensions={1} | all-to-all | bytes 4472832 | tf_op jit(solution)/shard_map/all_to_all | solution.py:115
  298.0 0.2 slice.24
  298.2 0.2 copy.75
  298.4 1.6 concatenate.16
  299.9 60.9 %rev.6 = f32[32,17472]{1,0:T(8,128)} reverse(f32[32,17472]{1,0:T(8,128)} %concatenate.16), dimensions={0} | reverse | bytes 4472832 | tf_op jit(solution)/shard_map/rev | solution.py:119
  360.8 4.9 reduce_window_sum.21
  365.7 60.9 %rev.7 = f32[32,17472]{1,0:T(8,128)} reverse(f32[32,17472]{1,0:T(8,128)} %reduce_window_sum.21), dimensions={0} | reverse | bytes 4472832 | tf_op jit(solution)/shard_map/rev | solution.py:119
  426.6 5.3 copy.44
  431.9 4.8 all-to-all-start.3
  436.7 0.2 reduce-scatter.4.cloned.1.call-start
  437.0 5.5 fusion.61
  442.5 0.3 slice_multiply_fusion.1
  442.8 0.6 copy-done.13
  443.4 1.1 multiply_reduce_fusion.2
  444.4 0.2 copy-done.5
  444.7 1.0 fusion.6
  445.8 1.0 copy-done.11
  446.7 1.7 fusion.17
  448.5 42.8 %all-to-all-done.3 = f32[32,1,17472]{2,1,0:T(1,128)} async-done(((f32[32,1,17472]{2,1,0:T(1,128)}), f32[32,1,17472]{2,1,0:T(1,128)}, u32[]{:S(2)}, u32[]{:S(2)}) %all-to-all-start.3) | async-done | bytes 2236448 | tf_op jit(solution)/shard_map/all_to_all | solution.py:120
  491.3 8.6 reduce.1
  499.8 3.2 reshape.144
  503.0 3.8 fusion.25
  506.8 0.3 slice_multiply_fusion
  507.1 1.1 multiply_reduce_fusion
  508.1 0.2 copy-done.12
  508.3 1.0 fusion.16
  509.3 4.5 convolution_bitcast_fusion
  513.8 9.2 copy.54
  523.0 2.2 fusion.18
  525.2 2.0 copy.45
  527.3 7.6 fusion.2
  534.8 2.1 fusion.7
  537.0 2.0 copy.46
  539.0 4.7 fusion
  543.7 1485.6 %reduce-scatter.4.cloned.1.call-done = f32[16,512]{1,0:T(8,128)} async-done(((f32[4096,512]{1,0:T(8,128)}), f32[16,512]{1,0:T(8,128)}) %reduce-scatter.4.cloned.1.call-update) | async-done | bytes 32784
  (34 shorter events, 0.4 us)
Async XLA Ops:
  7.2 59.4 %copy-start = (bf16[1,128,4096]{2,1,0:T(8,128)(2,1)S(1)}, bf16[1,128,4096]{2,1,0:T(8,128)(2,1)}, u32[]{:S(2)}) copy-start(bf16[1,128,4096]{2,1,0:T(8,128)(2,1)} %param.4) | copy-start | bytes 3145732
  7.2 59.4 %all-gather.2.cloned.1.call-start = ((), (), s32[]{:S(2)}) async-start(), calls=%async_computation.5 | async-start | bytes 4718592 | tf_op jit(solution)/shard_map/all_gather | solution.py:90
  9.1 61.5 %copy-start.7 = (bf16[16,8,16,128]{3,2,1,0:T(8,128)(2,1)}, bf16[16,8,16,128]{3,2,1,0:T(8,128)(2,1)S(1)}, u32[]{:S(2)}) copy-start(bf16[16,8,16,128]{3,2,1,0:T(8,128)(2,1)S(1)} %copy.57) | copy-start | bytes 1572868
  70.2 0.6 copy-start.14
  70.5 1.3 copy-start.3
  147.6 59.2 %all-to-all-start.1 = ((f32[32,1,17472]{2,1,0:T(1,128)}), f32[32,1,17472]{2,1,0:T(1,128)S(1)}, u32[]{:S(2)}, u32[]{:S(2)}) async-start(f32[32,1,17472]{2,1,0:T(1,128)} %fusion.1), calls=%async_computation.1 | async-start | bytes 4489216 | tf_op jit(solution)/shard_map/all_to_all | solution.py:105
  216.6 7.8 copy-start.1
  216.6 7.8 copy-start.4
  216.6 7.8 copy-start.8
  224.3 1.4 copy-start.10
  225.7 1.1 copy-start.6
  225.8 2.0 copy-start.2
  225.8 1.9 copy-start.16
  431.9 59.3 %all-to-all-start.3 = ((f32[32,1,17472]{2,1,0:T(1,128)}), f32[32,1,17472]{2,1,0:T(1,128)}, u32[]{:S(2)}, u32[]{:S(2)}) async-start(f32[32,1,17472]{2,1,0:T(1,128)} %copy.44), calls=%async_computation.3 | async-start | bytes 4489216 | tf_op jit(solution)/shard_map/all_to_all | solution.py:120
  436.7 1592.6 %reduce-scatter.4.cloned.1.call-start = ((), (), s32[]{:S(2)}) async-start(), calls=%async_computation.6 | async-start | bytes 8421376
  442.5 0.9 copy-start.13
  443.4 1.2 copy-start.5
  443.4 1.4 copy-start.9
  445.8 1.0 copy-start.11
  507.1 1.2 copy-start.12
  523.0 4.2 copy-start.15
Sparse Core Ops, SparseCore 0:
  9.8 56.6 all-gather.1
  523.1 1506.1 reduce-scatter.3
where the time goes:
time: 2050 us; the launch traced here: 2040 us
  waiting for transfers between devices  1630 us (80%)
  local copies, waits for them, and re-layouts  168 us (8%)
  blocking collectives  126 us (6%)
  matrix products  56.2 us (3%)
  other arithmetic  33 us (2%)
    unnamed x3, waiting for transfers between devices  1490 us
    rev x2, local copies, waits for them, and re-layouts, local(): later_running = jnp.cumsum(later_shift[::-1], axis=0)[::-1]  122 us
    all_to_all x1, blocking collectives, local(): lax.all_to_all(local_term.reshape(1, -1), 'ctx', split_axis=1, concat_axi...  65.7 us
    all_to_all x1, blocking collectives, local(): lax.all_to_all(carried.reshape(1, -1), 'ctx', split_axis=1, concat_axis=0...  60 us
    all_gather x1, waiting for transfers between devices, local(): lax.all_gather(proj_weight, 'dp', axis=0, tiled=True)  57.5 us
    all_to_all x1, waiting for transfers between devices, local(): lax.all_to_all(running, 'ctx', split_axis=0, concat_axis=1, tiled=True)  43.2 us
    all_to_all x1, waiting for transfers between devices, local(): lax.all_to_all(later_running, 'ctx', split_axis=0, concat_axis=1, tiled=T...  42.8 us
  transfers between devices with their start and end apart: 4, of which 4 were waited for; matrix products, arithmetic and copies ran while one was open for 2% of the time, Pallas kernels for 0%

commit v1 on v0

--- a/solution.py
+++ b/solution.py
@@ -74,6 +74,14 @@
     return (grad_query, grad_key, grad_value)
 
 
+def exclusive(blocks, later):
+    count = blocks.shape[0]
+    row = lax.broadcasted_iota(jnp.int32, (count, count), 0)
+    col = lax.broadcasted_iota(jnp.int32, (count, count), 1)
+    chosen = (col > row) if later else (col < row)
+    return jnp.dot(chosen.astype(jnp.float32), blocks, precision=HIGHEST)
+
+
 def split_heads(matrix, size):
     return jnp.swapaxes(matrix.reshape(matrix.shape[0], -1, size), 0, 1)
 
@@ -85,6 +93,7 @@
 def local(tokens, proj_weight, values, grad_out):
     token_rows = tokens[0]
     query_cols = H * F
+    tokens_cols = lax.all_to_all(token_rows, "dp", split_axis=1, concat_axis=0, tiled=True)
     projected = jnp.dot(
         token_rows,
         lax.all_gather(proj_weight, "dp", axis=0, tiled=True),
@@ -100,8 +109,7 @@
     columns_in = lax.all_to_all(
         local_term.reshape(1, -1), "ctx", split_axis=1, concat_axis=0, tiled=True
     )
-    shifted = jnp.concatenate([jnp.zeros_like(columns_in[:1]), columns_in[:-1]], axis=0)
-    running = jnp.cumsum(shifted, axis=0)
+    running = exclusive(columns_in, False)
     prefix = lax.all_to_all(running, "ctx", split_axis=0, concat_axis=1, tiled=True).reshape(
         local_term.shape
     )
@@ -115,8 +123,7 @@
     later_in = lax.all_to_all(
         carried.reshape(1, -1), "ctx", split_axis=1, concat_axis=0, tiled=True
     )
-    later_shift = jnp.concatenate([later_in[1:], jnp.zeros_like(later_in[:1])], axis=0)
-    later_running = jnp.cumsum(later_shift[::-1], axis=0)[::-1]
+    later_running = exclusive(later_in, True)
     suffix = lax.all_to_all(later_running, "ctx", split_axis=0, concat_axis=1, tiled=True).reshape(
         carried.shape
     )
@@ -143,11 +150,12 @@
         (((1,), (1,)), ((), ())),
         preferred_element_type=jnp.float32,
     ).astype(jnp.bfloat16)
+    rows_all = lax.all_gather(grad_proj_rows, "dp", axis=0, tiled=True)
     grad_proj = lax.psum_scatter(
         lax.dot_general(
-            token_rows, grad_proj_rows, (((0,), (0,)), ((), ())), preferred_element_type=jnp.float32
+            tokens_cols, rows_all, (((0,), (0,)), ((), ())), preferred_element_type=jnp.float32
         ),
-        ("dp", "ctx"),
+        "ctx",
         scatter_dimension=0,
         tiled=True,
     )

time: 2050 us -> 531 us (0.26)
  the two profiles are of different devices: /device:TPU:32 before, /device:TPU:1 now
where the time goes in v1:
time: 531 us; the launch traced here: 522 us
  waiting for transfers between devices  231 us (44%)
  blocking collectives  122 us (23%)
  matrix products  50.9 us (10%)
  starting transfers between devices  39 us (7%)
  local copies, waits for them, and re-layouts  38.5 us (7%)
  other arithmetic  26.1 us (5%)
  between operations  14.6 us (3%)
    unnamed x4, waiting for transfers between devices  74.7 us
    all_to_all x1, blocking collectives, local(): lax.all_to_all(carried.reshape(1, -1), 'ctx', split_axis=1, concat_axis=0...  62.8 us
    all_gather x1, waiting for transfers between devices, local(): lax.all_gather(proj_weight, 'dp', axis=0, tiled=True)  59.7 us
    all_to_all x1, blocking collectives, local(): lax.all_to_all(local_term.reshape(1, -1), 'ctx', split_axis=1, concat_axi...  59.1 us
    all_to_all x1, waiting for transfers between devices, local(): lax.all_to_all(running, 'ctx', split_axis=0, concat_axis=1, tiled=True)  36.1 us
    all_to_all x1, waiting for transfers between devices, local(): lax.all_to_all(later_running, 'ctx', split_axis=0, concat_axis=1, tiled=T...  30.2 us
    all_gather x1, waiting for transfers between devices, local(): rows_all = lax.all_gather(grad_proj_rows, 'dp', axis=0, tiled=True)  30.1 us
    all_to_all x1, starting transfers between devices, local(): lax.all_to_all(token_rows, 'dp', split_axis=1, concat_axis=0, tiled=True)  15.5 us
  transfers between devices with their start and end apart: 6, of which 5 were waited for; matrix products, arithmetic and copies ran while one was open for 11% of the time, Pallas kernels for 0%

profile of v1, /device:TPU:1, one launch (start us, length us, event | category | flops | bytes accessed | tf_op | source)
XLA Modules:
  0.0 521.9 jit_solution(1464538950625554450)
XLA Ops:
  7.2 0.7 all-gather.3.cloned.1.call-update
  7.9 1.1 copy.72
  9.1 59.7 %all-gather.3.cloned.1.call-done = bf16[4096,512]{1,0:T(8,128)(2,1)} async-done(((bf16[512,512]{1,0:T(8,128)(2,1)}), bf16[4096,512]{1,0:T(8,128)(2,1)}) %all-gather.3.cloned.1.call-update) | async-done | bytes 4194320 | tf_op jit(solution)/shard_map/all_gather | solution.py:99
  68.8 3.2 fusion.22
  72.2 0.3 multiply_multiply_fusion
  72.5 1.4 copy-done.1
  73.9 2.1 fusion.6
  75.9 3.7 all_to_all.72
  79.7 59.1 %all_to_all.79 = f32[1,32,17472]{2,0,1:T(1,128)S(1)} all-to-all(f32[1,32,17472]{2,0,1:T(1,128)} %all_to_all.72), channel_id=1, replica_groups=mesh['dp'=8,'ctx'=32] {'ctx'}, dimensions={1} | all-to-all | bytes 4472832 | tf_op jit(solution)/shard_map/all_to_all | solution.py:109
  138.8 1.2 convolution_bitcast_fusion.1
  140.0 3.7 copy.50
  143.7 10.2 %all-to-all-start.1 = ((f32[32,1,17472]{2,1,0:T(1,128)}), f32[32,1,17472]{2,1,0:T(1,128)S(1)}, u32[]{:S(2)}, u32[]{:S(2)}) async-start(f32[32,1,17472]{2,1,0:T(1,128)} %copy.50), calls=%async_computation.1 | async-start | bytes 4489216 | tf_op jit(solution)/shard_map/all_to_all | solution.py:113
  153.9 1.2 copy.51
  155.3 0.7 multiply_bitcast_fusion.1
  156.0 2.7 fusion.60
  158.7 2.9 multiply_multiply_fusion.1
  161.6 36.1 %all-to-all-done.1 = f32[32,1,17472]{2,1,0:T(1,128)S(1)} async-done(((f32[32,1,17472]{2,1,0:T(1,128)}), f32[32,1,17472]{2,1,0:T(1,128)S(1)}, u32[]{:S(2)}, u32[]{:S(2)}) %all-to-all-start.1) | async-done | bytes 2236448 | tf_op jit(solution)/shard_map/all_to_all | solution.py:113
  197.6 7.3 %reduce = f32[32,17472]{1,0:T(8,128)} reduce(f32[32,1,17472]{2,1,0:T(1,128)S(1)} %all-to-all-done.1, f32[]{:T(128)} %constant.24), dimensions={1}, to_apply=%all_to_all.62.reduce_sub_computation | reduce | bytes 4472836 | tf_op jit(solution)/shard_map/all_to_all | solution.py:113
  205.0 2.4 reshape.143
  207.4 6.9 %fusion.8 = f32[16,128,128]{1,2,0:T(8,128)S(1)} fusion(f32[16,273,128]{2,1,0:T(8,128)S(1)} %reshape.143, f32[16,256,128]{2,1,0:T(8,128)} %bitcast.119, f32[16,16,128]{2,1,0:T(8,128)} %multiply_bitcast_fusion.1, f32[273]{0:T(512)S(1)} %pad.5.clone), kind=kOutput, calls=%fused_computation.21 | convolution fusion | flops 859901952 | bytes 5514308 | tf_op jit(solution)/shard_map/het,hed->htd/dot_general | solution.py:118
  214.4 1.4 multiply_reduce_fusion.5
  215.8 0.7 add_rsqrt_fusion
  216.4 0.2 multiply_reduce_fusion.4
  216.7 0.2 subtract_multiply_fusion
  217.0 1.1 copy-done
  218.0 5.3 %fusion.7 = f32[16,273,128]{2,1,0:T(8,128)} fusion(f32[16,128,128]{1,2,0:T(8,128)S(1)} %subtract_multiply_fusion, f32[16,256,128]{2,1,0:T(8,128)S(1)} %bitcast.120, f32[16,16,128]{2,1,0:T(8,128)S(1)} %copy-done.17, f32[273]{0:T(512)S(1)} %pad.5.clone), kind=kOutput, calls=%fused_computation.20 | convolution fusion | flops 859901952 | bytes 5514308 | tf_op jit(solution)/shard_map/het,htd->hed/dot_general | solution.py:122
  223.3 5.2 %all_to_all.73 = f32[1,32,17472]{2,0,1:T(1,128)} reshape(f32[16,273,128]{2,1,0:T(8,128)} %fusion.7) | data formatting | bytes 4472832 | tf_op jit(solution)/shard_map/all_to_all | solution.py:123
  228.5 62.8 %all_to_all.80 = f32[1,32,17472]{2,0,1:T(1,128)S(1)} all-to-all(f32[1,32,17472]{2,0,1:T(1,128)} %all_to_all.73), channel_id=1, replica_groups=mesh['dp'=8,'ctx'=32] {'ctx'}, dimensions={1} | all-to-all | bytes 4472832 | tf_op jit(solution)/shard_map/all_to_all | solution.py:123
  291.4 1.2 convolution_bitcast_fusion
  292.6 3.8 copy.56
  296.3 12.8 %all-to-all-start.3 = ((f32[32,1,17472]{2,1,0:T(1,128)}), f32[32,1,17472]{2,1,0:T(1,128)}, u32[]{:S(2)}, u32[]{:S(2)}) async-start(f32[32,1,17472]{2,1,0:T(1,128)} %copy.56), calls=%async_computation.3 | async-start | bytes 4489216 | tf_op jit(solution)/shard_map/all_to_all | solution.py:127
  309.1 2.3 copy.57
  311.4 3.9 fusion.61
  315.3 0.3 slice_multiply_fusion.1
  315.6 0.6 copy-done.13
  316.2 1.0 multiply_reduce_fusion.2
  317.2 0.2 copy-done.3
  317.4 0.1 copy-done.8
  317.5 1.0 fusion.9
  318.6 1.0 copy-done.9
  319.6 1.7 fusion.20
  321.3 30.2 %all-to-all-done.3 = f32[32,1,17472]{2,1,0:T(1,128)} async-done(((f32[32,1,17472]{2,1,0:T(1,128)}), f32[32,1,17472]{2,1,0:T(1,128)}, u32[]{:S(2)}, u32[]{:S(2)}) %all-to-all-start.3) | async-done | bytes 2236448 | tf_op jit(solution)/shard_map/all_to_all | solution.py:127
  351.5 15.5 %all-to-all-start.4 = ((bf16[128,8,512]{0,2,1:T(8,128)(2,1)}), bf16[128,8,512]{0,2,1:T(8,128)(2,1)}, u32[]{:S(2)}, u32[]{:S(2)}) async-start(bf16[128,8,512]{0,2,1:T(8,128)(2,1)} %bitcast.40), calls=%async_computation.4 | async-start | bytes 2097152 | tf_op jit(solution)/shard_map/all_to_all | solution.py:96
  367.0 0.2 all-gather.5.cloned.1.call-start
  367.2 8.4 %reduce.1 = f32[32,17472]{1,0:T(8,128)} reduce(f32[32,1,17472]{2,1,0:T(1,128)} %all-to-all-done.3, f32[]{:T(128)} %constant.24), dimensions={1}, to_apply=%all_to_all.67.reduce_sub_computation | reduce | bytes 4472836 | tf_op jit(solution)/shard_map/all_to_all | solution.py:127
  375.7 2.2 reshape.146
  377.9 3.1 fusion.27
  380.9 0.3 slice_multiply_fusion
  381.2 1.1 multiply_reduce_fusion
  382.3 0.1 copy-done.10
  382.4 1.0 fusion.19
  383.5 0.7 pad_maximum_fusion.6
  384.2 0.3 reduce-scatter.4.cloned.1.call-start
  384.5 2.3 copy.58
  386.8 30.1 %all-gather.5.cloned.1.call-done = bf16[1024,512]{0,1:T(8,128)(2,1)} async-done(((bf16[128,512]{0,1:T(8,128)(2,1)}), bf16[1024,512]{0,1:T(8,128)(2,1)}) %all-gather.5.cloned.1.call-update) | async-done | bytes 1048592 | tf_op jit(solution)/shard_map/all_gather | solution.py:153
  416.8 3.3 convolution_bitcast_fusion.2
  420.1 2.5 copy.68
  422.6 2.2 fusion.21
  424.8 2.0 copy.59
  426.9 7.0 %fusion.5 = f32[16,128,128]{1,2,0:T(8,128)S(1)} fusion(f32[16,273,128]{2,1,0:T(8,128)S(1)} %reshape.146, f32[16,256,128]{2,1,0:T(8,128)} %bitcast.122, f32[16,16,128]{2,1,0:T(8,128)S(1)} %copy-done.16, f32[273]{0:T(512)} %copy-done.21), kind=kOutput, calls=%fused_computation.18 | convolution fusion | flops 859901952 | bytes 5514308 | tf_op jit(solution)/shard_map/het,hed->htd/dot_general | solution.py:73
  433.8 1.4 fusion.10
  435.2 1.0 copy.60
  436.2 4.6 fusion
  440.9 74.0 %reduce-scatter.4.cloned.1.call-done = f32[16,512]{1,0:T(8,128)} async-done(((f32[512,512]{1,0:T(8,128)}), f32[16,512]{1,0:T(8,128)}) %reduce-scatter.4.cloned.1.call-update) | async-done | bytes 32784
  (48 shorter events, 0.5 us)
Async XLA Ops:
  7.2 61.6 %all-gather.3.cloned.1.call-start = ((), (), s32[]{:S(2)}) async-start(), calls=%async_computation.6 | async-start | bytes 4718592 | tf_op jit(solution)/shard_map/all_gather | solution.py:99
  9.1 63.4 %copy-start.6 = (bf16[16,8,16,128]{3,2,1,0:T(8,128)(2,1)}, bf16[16,8,16,128]{3,2,1,0:T(8,128)(2,1)S(1)}, u32[]{:S(2)}) copy-start(bf16[16,8,16,128]{3,2,1,0:T(8,128)(2,1)S(1)} %copy.72) | copy-start | bytes 1572868
  9.1 207.9 %copy-start.21 = (f32[273]{0:T(512)}, f32[273]{0:T(512)S(1)}, u32[]{:S(2)}) copy-start(f32[273]{0:T(512)S(1)} %pad.5.clone) | copy-start | bytes 3280
  72.2 3.8 copy-start.15
  72.5 1.4 copy-start.1
  143.7 10.2 %copy-start.20 = (bf16[1,128,2048]{2,1,0:T(8,128)(2,1)S(1)}, bf16[1,128,2048]{2,1,0:T(8,128)(2,1)}, u32[]{:S(2)}) copy-start(bf16[1,128,2048]{2,1,0:T(8,128)(2,1)} %param.7) | copy-start | bytes 1572868
  143.7 53.9 %all-to-all-start.1 = ((f32[32,1,17472]{2,1,0:T(1,128)}), f32[32,1,17472]{2,1,0:T(1,128)S(1)}, u32[]{:S(2)}, u32[]{:S(2)}) async-start(f32[32,1,17472]{2,1,0:T(1,128)} %copy.50), calls=%async_computation.1 | async-start | bytes 4489216 | tf_op jit(solution)/shard_map/all_to_all | solution.py:113
  155.2 0.7 copy-start.12
  158.7 55.7 %copy-start.2 = (f32[16,128,128]{2,1,0:T(8,128)}, f32[16,128,128]{2,1,0:T(8,128)S(1)}, u32[]{:S(2)}) copy-start(f32[16,128,128]{2,1,0:T(8,128)S(1)} %fusion.60) | copy-start | bytes 3145732
  207.4 7.0 %copy-start.7 = (bf16[16,8,16,128]{3,2,1,0:T(8,128)(2,1)S(1)}, bf16[16,8,16,128]{3,2,1,0:T(8,128)(2,1)}, u32[]{:S(2)}) copy-start(bf16[16,8,16,128]{3,2,1,0:T(8,128)(2,1)} %copy-done.6) | copy-start | bytes 1572868
  214.4 2.1 copy-start.11
  215.8 1.0 copy-start.5
  216.4 1.6 copy-start
  216.4 1.6 copy-start.17
  296.3 55.2 %all-to-all-start.3 = ((f32[32,1,17472]{2,1,0:T(1,128)}), f32[32,1,17472]{2,1,0:T(1,128)}, u32[]{:S(2)}, u32[]{:S(2)}) async-start(f32[32,1,17472]{2,1,0:T(1,128)} %copy.56), calls=%async_computation.3 | async-start | bytes 4489216 | tf_op jit(solution)/shard_map/all_to_all | solution.py:127
  315.3 0.9 copy-start.13
  316.2 1.2 copy-start.3
  316.2 1.4 copy-start.8
  318.6 1.0 copy-start.9
  351.5 32.9 %all-to-all-start.4 = ((bf16[128,8,512]{0,2,1:T(8,128)(2,1)}), bf16[128,8,512]{0,2,1:T(8,128)(2,1)}, u32[]{:S(2)}, u32[]{:S(2)}) async-start(bf16[128,8,512]{0,2,1:T(8,128)(2,1)} %bitcast.40), calls=%async_computation.4 | async-start | bytes 2097152 | tf_op jit(solution)/shard_map/all_to_all | solution.py:96
  367.0 49.8 %all-gather.5.cloned.1.call-start = ((), (), s32[]{:S(2)}) async-start(), calls=%async_computation.7 | async-start | bytes 1179648 | tf_op jit(solution)/shard_map/all_gather | solution.py:153
  381.2 1.2 copy-start.10
  381.2 1.2 copy-start.14
  383.4 36.6 %copy-start.18 = (bf16[128,16,16]{0,2,1:T(8,128)(2,1)}, bf16[128,16,16]{0,2,1:T(8,128)(2,1)S(1)}, u32[]{:S(2)}) copy-start(bf16[128,16,16]{0,2,1:T(8,128)(2,1)S(1)} %fusion.19) | copy-start | bytes 196612
  384.2 130.7 %reduce-scatter.4.cloned.1.call-start = ((), (), s32[]{:S(2)}) async-start(), calls=%async_computation.8 | async-start | bytes 1081344
  422.6 4.2 copy-start.16
  426.9 7.0 %copy-start.4 = (f32[16,128,128]{2,1,0:T(8,128)S(1)}, f32[16,128,128]{2,1,0:T(8,128)}, u32[]{:S(2)}) copy-start(f32[16,128,128]{2,1,0:T(8,128)} %copy-done.2) | copy-start | bytes 3145732
  433.8 2.4 copy-start.19
Sparse Core Ops, SparseCore 0:
  9.8 58.9 all-gather.2
  384.3 32.5 all-gather.4
  422.8 92.0 reduce-scatter.3

commit v2 on v0

v2 whole, which is shorter than its diff:
```python
import functools

import jax
import jax.numpy as jnp
from jax import lax
from jax.experimental import pallas as pl
from jax.experimental.pallas import tpu as pltpu
from jax.sharding import PartitionSpec as P

H = 16
F = 16
DH = 128
EP = 160
QUAD = 1.0 / 32.0
EPSILON = 1e-05
MESH = pl.DeviceIdType.MESH
F32 = jnp.float32
BF16 = jnp.bfloat16
VMEM = pl.BlockSpec(memory_space=pltpu.VMEM)
NY = 4
NZ = 4
NDP = 8
NC = 2
RC = 2 * EP // NC


def dot(lhs, rhs, left, right):
    return lax.dot_general(lhs, rhs, (((left,), (right,)), ((), ())), preferred_element_type=F32)


def remote(src, dst, send, recv, **where):
    return pltpu.make_async_remote_copy(
        src_ref=src, dst_ref=dst, send_sem=send, recv_sem=recv, device_id=where, device_id_type=MESH
    )


def greet(peers):
    barrier = pltpu.get_barrier_semaphore()
    for where in peers:
        pl.semaphore_signal(barrier, inc=1, device_id=where, device_id_type=MESH)
    pl.semaphore_wait(barrier, len(peers))


def across(dp, dz, dx):
    return (dp // 4 + dz) % 2 * 4 + (dp % 4 + dx + 4) % 4


def place():
    ctx = lax.axis_index("ctx")
    return ctx // 8, (ctx // 2) % 4, ctx % 2


def at(z, y, c):
    return z * 8 + y * 2 + c


def gather_weight_kernel(w_ref, out_ref, own_sem, send1, recv1, send2, recv2):
    dp = lax.axis_index("dp")
    z, y, c = place()
    partner = at(z, y, 1 - c)
    greet([{"dp": (dp + d) % NDP} for d in range(1, NDP)] + [{"ctx": partner}])
    half = w_ref.shape[0] // 2
    rows = w_ref.shape[0]

    def spot(owner):
        return pl.ds(pl.multiple_of(owner * rows + c * half, half), half)

    own = pltpu.make_async_copy(
        w_ref, out_ref.at[pl.ds(pl.multiple_of(dp * rows, rows), rows)], own_sem
    )
    mine = w_ref.at[pl.ds(pl.multiple_of(c * half, half), half)]
    first = []
    for d in range(1, NDP):
        first.append(
            remote(mine, out_ref.at[spot(dp)], send1.at[d], recv1.at[d], dp=(dp + d) % NDP)
        )
        first[-1].start()
    own.start()
    second = []
    for d in range(1, NDP):
        first[d - 1].wait_recv()
        landed = out_ref.at[spot((dp + NDP - d) % NDP)]
        second.append(remote(landed, landed, send2.at[d], recv2.at[d], ctx=partner))
        second[-1].start()
    for copy in first:
        copy.wait_send()
    for copy in second:
        copy.wait()
    own.wait()


def gather_weight(w):
    return pl.pallas_call(
        gather_weight_kernel,
        out_shape=jax.ShapeDtypeStruct((NDP * w.shape[0], w.shape[1]), w.dtype),
        in_specs=[VMEM],
        out_specs=VMEM,
        scratch_shapes=[pltpu.SemaphoreType.DMA] + [pltpu.SemaphoreType.DMA((NDP,))] * 4,
        compiler_params=pltpu.CompilerParams(collective_id=0, has_side_effects=True),
        name="gather_weight",
    )(w)


def scan_kernel(later, slots, *refs):
    s_ref, tok_ref, out_ref, cols_ref = refs[:4]
    rest = refs[4:]
    sib, chip, yin, tz, zin, yout, pin, hand, pre, sem_c, sem_y, sem_z, sem_b, sem_p = rest[:14]
    z, y, c = place()
    dp = lax.axis_index("dp")
    partner = at(z, y, 1 - c)
    peers = [{"ctx": partner}]
    peers += [{"ctx": at(z, (y + d) % NY, c)} for d in range(1, NY)]
    peers += [{"ctx": at((z + d) % NZ, y, c)} for d in range(1, NZ)]
    moves = [move for move in slots if move != (0, 0)]
    met = sorted({(dz, step % 4) for dz, dx in moves for step in (dx, -dx)})
    peers += [{"dp": across(dp, dz, dx)} for dz, dx in met]
    greet(peers)

    def before(other, me):
        return other > me if later else other < me

    copies_c = []
    for n in range(NC):
        copies_c.append(
            remote(s_ref.at[1 - c, n], sib.at[n], sem_c.at[0, n], sem_c.at[1, n], ctx=partner)
        )
        copies_c[-1].start()
    token_copies = []

    def send_tokens(slots):
        for index, (dz, dx) in slots:
            peer = across(dp, dz, dx)
            where = pl.ds(pl.multiple_of(peer * width, width), width)
            token_copies.append(
                remote(
                    tok_ref.at[:, where], cols_ref.at[index], sem_t.at[0, index],
                    sem_t.at[1, index], dp=peer,
                )
            )
            token_copies[-1].start()

    sem_t, own_t = rest[14:]
    width = cols_ref.shape[2]
    listed = list(enumerate(slots))
    send_tokens([(i, s) for i, s in listed if s[0] == 0 and s[1] > 0])
    own_copies = []
    for index, s in listed:
        if s == (0, 0):
            where = pl.ds(pl.multiple_of(dp * width, width), width)
            own_copies.append(
                pltpu.make_async_copy(tok_ref.at[:, where], cols_ref.at[index], own_t)
            )
            own_copies[-1].start()
    copies_y = []
    for n in range(NC):
        copies_c[n].wait_recv()
        for j in range(NY):
            chip[n, j] = (s_ref[c, n, j] + sib[n, j]).astype(BF16)
        for d in range(1, NY):
            to = (y + d) % NY
            copies_y.append(
                remote(
                    chip.at[n, to], yin.at[n, y], sem_y.at[0, n, d], sem_y.at[1, n, d],
                    ctx=at(z, to, c),
                )
            )
            copies_y[-1].start()
    copies_z = []
    for n in range(NC):
        for d in range(1, NY):
            copies_y[n * 3 + d - 1].wait_recv()
        blocks = [
            jnp.where(j == y, chip[n, j], yin[n, j]).astype(F32) for j in range(NY)
        ]
        order = list(range(NY))[::-1] if later else list(range(NY))
        total = jnp.zeros_like(blocks[0])
        for j in order:
            pre[n, j] = total
            total = total + blocks[j]
        tz[n] = total.astype(BF16)
        for d in range(1, NZ):
            copies_z.append(
                remote(
                    tz.at[n], zin.at[n, z], sem_z.at[0, n, d], sem_z.at[1, n, d],
                    ctx=at((z + d) % NZ, y, c),
                )
            )
            copies_z[-1].start()
    send_tokens([(i, s) for i, s in listed if s[0] == 1])
    copies_b = []
    for n in range(NC):
        for d in range(1, NZ):
            copies_z[n * 3 + d - 1].wait_recv()
        base = jnp.zeros(pre.shape[2:], F32)
        for j in range(NZ):
            base = base + jnp.where(before(j, z), zin[n, j].astype(F32), 0.0)
        for j in range(NY):
            yout[n, j] = (base + pre[n, j]).astype(BF16)
        for d in range(1, NY):
            to = (y + d) % NY
            copies_b.append(
                remote(
                    yout.at[n, to], pin.at[n, y], sem_b.at[0, n, d], sem_b.at[1, n, d],
                    ctx=at(z, to, c),
                )
            )
            copies_b[-1].start()
    copies_p = []
    for n in range(NC):
        for d in range(1, NY):
            copies_b[n * 3 + d - 1].wait_recv()
        for j in range(NY):
            prefix = jnp.where(j == y, yout[n, j], pin[n, j]).astype(F32)
            mine = prefix + jnp.where(before(1 - c, c), sib[n, j], 0.0)
            theirs = prefix + jnp.where(before(c, 1 - c), s_ref[c, n, j], 0.0)
            hand[n, j] = theirs
            out_ref[c, n, j] = mine
        copies_p.append(
            remote(hand.at[n], out_ref.at[c, n], sem_p.at[0, n], sem_p.at[1, n], ctx=partner)
        )
        copies_p[-1].start()
    for copy in copies_p:
        copy.wait()
    for copy in copies_c + copies_y + copies_z + copies_b:
        copy.wait_send()
    for copy in token_copies + own_copies:
        copy.wait()


def scan(state, later, collective, tokens, slots):
    shape = (2, NC, NY, RC, DH)
    slab = (NC, NY, RC, DH)
    thin = (NC, RC, DH)
    rows, width = tokens.shape
    dma = pltpu.SemaphoreType.DMA
    return pl.pallas_call(
        functools.partial(scan_kernel, later, slots),
        out_shape=(
            jax.ShapeDtypeStruct(shape, F32),
            jax.ShapeDtypeStruct((len(slots), rows, width // NDP), BF16),
        ),
        in_specs=[VMEM, VMEM],
        out_specs=(VMEM, VMEM),
        scratch_shapes=[
            pltpu.VMEM(slab, F32),
            pltpu.VMEM(slab, BF16),
            pltpu.VMEM(slab, BF16),
            pltpu.VMEM(thin, BF16),
            pltpu.VMEM((NC, NZ, RC, DH), BF16),
            pltpu.VMEM(slab, BF16),
            pltpu.VMEM(slab, BF16),
            pltpu.VMEM(slab, F32),
            pltpu.VMEM(slab, F32),
            dma((2, NC)),
            dma((2, NC, NY)),
            dma((2, NC, NZ)),
            dma((2, NC, NY)),
            dma((2, NC)),
            dma((2, len(slots))),
            dma,
        ],
        compiler_params=pltpu.CompilerParams(collective_id=collective, has_side_effects=True),
        name="scan_later" if later else "scan_earlier",
    )(state, tokens)


def gather_rows_kernel(r_ref, out_ref, own_sem, send, recv):
    dp = lax.axis_index("dp")
    right, left, other = across(dp, 0, 1), across(dp, 0, 3), across(dp, 1, 0)
    greet([{"dp": right}, {"dp": left}, {"dp": other}])
    half = r_ref.shape[0] // 2
    low, high = pl.ds(0, half), pl.ds(half, half)
    started = []

    def push(index, src, dst, to):
        copy = remote(src, dst, send.at[index], recv.at[index], dp=to)
        copy.start()
        started.append(copy)
        return copy

    over = push(0, r_ref, out_ref.at[4], other)
    rights = [push(1, r_ref, out_ref.at[1], right), None]
    lefts = [push(2, r_ref, out_ref.at[3], left), None]
    own = pltpu.make_async_copy(r_ref, out_ref.at[0], own_sem)
    own.start()
    over.wait_recv()
    rights[1] = push(3, out_ref.at[4], out_ref.at[5], right)
    lefts[1] = push(4, out_ref.at[4], out_ref.at[7], left)
    ends = []
    for n in range(2):
        base = 4 * n
        rights[n].wait_recv()
        ends.append(
            push(5 + n, out_ref.at[base + 1, low], out_ref.at[base + 2, low], right)
        )
        lefts[n].wait_recv()
        ends.append(
            push(7 + n, out_ref.at[base + 3, high], out_ref.at[base + 2, high], left)
        )
    for copy in ends:
        copy.wait_recv()
    for copy in started:
        copy.wait_send()
    own.wait()


def gather_rows(r):
    return pl.pallas_call(
        gather_rows_kernel,
        out_shape=jax.ShapeDtypeStruct((NDP,) + r.shape, r.dtype),
        in_specs=[VMEM],
        out_specs=VMEM,
        scratch_shapes=[pltpu.SemaphoreType.DMA] + [pltpu.SemaphoreType.DMA((9,))] * 2,
        compiler_params=pltpu.CompilerParams(collective_id=3, has_side_effects=True),
        name="gather_rows",
    )(r)


def reduce_kernel(g_ref, out_ref, sib, pair, yin, ysum, zin, sem_c, sem_y, sem_z):
    z, y, c = place()
    partner = at(z, y, 1 - c)
    peers = [{"ctx": partner}]
    peers += [{"ctx": at(z, (y + d) % NY, c)} for d in range(1, NY)]
    peers += [{"ctx": at((z + d) % NZ, y, c)} for d in range(1, NZ)]
    greet(peers)
    copies_c, copies_y, copies_z = [], [], []
    for d in range(NY):
        to = (y + d) % NY
        copies_c.append(
            remote(
                g_ref.at[:, to, 1 - c], sib.at[to], sem_c.at[0, d], sem_c.at[1, d], ctx=partner
            )
        )
    for d in (1, 2, 3, 0):
        copies_c[d].start()
    for d in (1, 2, 3, 0):
        to = (y + d) % NY
        copies_c[d].wait_recv()
        both = g_ref[:, to, c] + sib[to]
        if d == 0:
            ysum[...] = both
        else:
            pair[to] = both.astype(BF16)
            copies_y.append(
                remote(pair.at[to], yin.at[y], sem_y.at[0, d], sem_y.at[1, d], ctx=at(z, to, c))
            )
            copies_y[-1].start()
    for copy in copies_y:
        copy.wait_recv()
    for j in range(NY):
        ysum[...] += jnp.where(j == y, 0.0, yin[j].astype(F32))
    for d in range(1, NZ):
        to = (z + d) % NZ
        copies_z.append(
            remote(ysum.at[to], zin.at[z], sem_z.at[0, d], sem_z.at[1, d], ctx=at(to, y, c))
        )
        copies_z[-1].start()
    for copy in copies_z:
        copy.wait_recv()
    total = ysum[z]
    for j in range(NZ):
        total = total + jnp.where(j == z, 0.0, zin[j])
    out_ref[...] = total
    for copy in copies_c + copies_y + copies_z:
        copy.wait_send()


def reduce_ctx(grad):
    rows, width = grad.shape
    own = rows // (2 * NY * NZ)
    view = grad.reshape(NZ, NY, 2, own, width)
    slab = (NY, NZ, own, width)
    dma = pltpu.SemaphoreType.DMA
    return pl.pallas_call(
        reduce_kernel,
        out_shape=jax.ShapeDtypeStruct((own, width), F32),
        in_specs=[VMEM],
        out_specs=VMEM,
        scratch_shapes=[
            pltpu.VMEM(slab, F32),
            pltpu.VMEM(slab, BF16),
            pltpu.VMEM(slab, BF16),
            pltpu.VMEM((NZ, own, width), F32),
            pltpu.VMEM((NZ, own, width), F32),
            dma((2, NY)),
            dma((2, NY)),
            dma((2, NZ)),
        ],
        compiler_params=pltpu.CompilerParams(collective_id=4, has_side_effects=True),
        name="reduce_ctx",
    )(view)


def ahead(x, d):
    return pltpu.roll(x, F - d, 0)


def behind(x, d):
    return pltpu.roll(x, d, 0)


def features(x, weighted):
    quad, linear = (QUAD, 0.25) if weighted else (1.0, 1.0)
    twice = 2.0 * quad if weighted else 1.0
    parts = [x * x * quad] + [x * ahead(x, d) * twice for d in range(1, 8)]
    parts += [x[:8] * x[8:] * twice, x * linear]
    row = lax.broadcasted_iota(jnp.int32, (8, x.shape[1]), 0)
    parts.append(jnp.where(row == 0, 1.0, 0.0))
    return jnp.concatenate(parts, axis=0)


def pull_features(x, cot):
    out = 2.0 * QUAD * cot[:F] * x
    for d in range(1, 8):
        part = 2.0 * QUAD * cot[F * d : F * (d + 1)]
        out = out + part * ahead(x, d) + behind(part * x, d)
    half = 2.0 * QUAD * cot[128:136]
    out = out + jnp.concatenate([half * x[8:], half * x[:8]], axis=0)
    return out + 0.25 * cot[136:152]


def split(x):
    high = x.astype(BF16)
    return high, (x - high.astype(F32)).astype(BF16)


def scores(q, k):
    qh, ql = split(q)
    kh, kl = split(k)
    left = jnp.concatenate([qh, qh, ql, ql], axis=0)
    right = jnp.concatenate([kh, kl, kh, kl], axis=0)
    return dot(left, right, 0, 0) * 0.25


def product(feat, state):
    fh, fl = split(feat)
    sh, sl = split(state)
    left = jnp.concatenate([fh, fl, fh], axis=0)
    right = jnp.concatenate([sh, sh, sl], axis=0)
    return dot(left, right, 0, 0)


def pulled(state, rows, fine=None):
    high, low = split(state)
    both = dot(jnp.concatenate([high, low], axis=0), rows, 1, 1)
    both = both[:EP] + both[EP:]
    return both if fine is None else both + dot(high, fine, 1, 1)


def causal():
    shape = (128, 128)
    return lax.broadcasted_iota(jnp.int32, shape, 0) >= lax.broadcasted_iota(jnp.int32, shape, 1)


def head_cols(h):
    return slice(h * DH, (h + 1) * DH)


def head_rows(h):
    return slice(h * F, (h + 1) * F)


def slot(h):
    return h // 8, h % 2, (h // 2) % 4


def project_kernel(tok_ref, w_ref, v_ref, proj_ref, state_ref):
    proj = dot(tok_ref[...], w_ref[...], 1, 0)
    proj_ref[...] = proj.T
    for h in range(H):
        keys = proj_ref[256 + h * F : 256 + (h + 1) * F, :]
        high, low = split(features(keys, False))
        v = v_ref[:, head_cols(h)]
        state = dot(
            jnp.concatenate([high, low], axis=1), jnp.concatenate([v, v], axis=0), 1, 0
        )
        state_ref[slot(h)] = state


def forward_kernel(proj_ref, v_ref, g_ref, prefix_ref, att_ref, gn_ref, state_ref):
    mask = causal()
    for h in range(H):
        q = proj_ref[head_rows(h), :]
        k = proj_ref[256 + h * F : 256 + (h + 1) * F, :]
        a = scores(q, k)
        kernel = jnp.where(mask, 1.0 + a + 0.5 * a * a, 0.0)
        feat = features(q, False)
        v = v_ref[:, head_cols(h)]
        numerator = dot(
            jnp.concatenate(split(kernel), axis=1), jnp.concatenate([v, v], axis=0), 1, 0
        )
        numerator += product(features(q, True), prefix_ref[slot(h)])
        inv = lax.rsqrt(jnp.mean(numerator * numerator, axis=1, keepdims=True) + EPSILON)
        normed = numerator * inv
        att_ref[:, head_cols(h)] = normed.astype(BF16)
        g = g_ref[:, head_cols(h)].astype(F32)
        gn = inv * (g - normed * jnp.mean(normed * g, axis=1, keepdims=True))
        gn_ref[:, head_cols(h)] = gn
        high, low = split(feat)
        gh, gl = split(gn)
        state_ref[slot(h)] = dot(
            jnp.concatenate([high, low, high], axis=1),
            jnp.concatenate([gh, gh, gl], axis=0),
            1,
            0,
        )


def backward_kernel(proj_ref, v_ref, gn_ref, prefix_ref, suffix_ref, gv_ref, rows_ref, acc):
    mask = causal()
    for h in range(H):
        q = proj_ref[head_rows(h), :]
        k = proj_ref[256 + h * F : 256 + (h + 1) * F, :]
        v = v_ref[:, head_cols(h)]
        gh, gl = split(gn_ref[:, head_cols(h)])
        a = scores(q, k)
        mh, ml = split(jnp.where(mask, 1.0 + a + 0.5 * a * a, 0.0))
        mixing = dot(
            jnp.concatenate([gh, gl], axis=1), jnp.concatenate([v, v], axis=1), 1, 1
        )
        sh, sl = split(jnp.where(mask, mixing * (1.0 + a) * 0.25, 0.0))
        qh, ql = split(q)
        kh, kl = split(k)
        dq = dot(jnp.concatenate([kh, kl], axis=0), sh, 1, 1)
        dq = dq[:F] + dq[F:] + dot(kh, sl, 1, 1)
        dk = dot(jnp.concatenate([qh, ql], axis=0), sh, 1, 0)
        dk = dk[:F] + dk[F:] + dot(qh, sl, 1, 0)
        pre = prefix_ref[slot(h)]
        suf = suffix_ref[slot(h)]
        acc[head_rows(h), :] = dq + pull_features(q, pulled(pre, gh, gl))
        acc[256 + h * F : 256 + (h + 1) * F, :] = dk + pull_features(k, pulled(suf, v))
        gv = dot(
            jnp.concatenate([mh, ml, mh], axis=0), jnp.concatenate([gh, gh, gl], axis=0), 0, 0
        )
        gv += product(features(k, True), suf)
        gv_ref[:, head_cols(h)] = gv.astype(BF16)
    rows_ref[...] = acc[...].T.astype(BF16)


def weight_grad_kernel(early_ref, late_ref, rows_ref, out_ref):
    early = early_ref.shape[0]
    flat = rows_ref[...].reshape(-1, rows_ref.shape[2])
    cols = jnp.concatenate(
        [early_ref[n] for n in range(early)] + [late_ref[n] for n in range(late_ref.shape[0])],
        axis=0,
    )
    out_ref[...] = dot(cols, flat, 0, 0)


def plain(kernel, outs, args, scratch=(), name=None):
    return pl.pallas_call(
        kernel,
        out_shape=outs,
        in_specs=[VMEM] * len(args),
        out_specs=jax.tree.map(lambda _: VMEM, outs),
        scratch_shapes=list(scratch),
        name=name,
    )(*args)


def shaped(shape, dtype):
    return jax.ShapeDtypeStruct(shape, dtype)


def local(tokens, proj_weight, values, grad_out):
    tok, val, up = tokens[0], values[0], grad_out[0]
    rows = tok.shape[0]
    packed = shaped((2, NC, NY, RC, DH), F32)
    weight = gather_weight(proj_weight)
    proj, state = plain(
        project_kernel, (shaped((2 * H * F, rows), F32), packed), (tok, weight, val), name="project"
    )
    early = ((0, 0), (0, 1), (0, 2), (0, 3), (1, 0), (1, 1))
    late = ((1, 2), (1, 3))
    prefix, cols_early = scan(state, False, 1, tok, early)
    attended, grad_num, carried = plain(
        forward_kernel,
        (shaped(val.shape, BF16), shaped(val.shape, F32), packed),
        (proj, val, up, prefix),
        name="forward",
    )
    suffix, cols_late = scan(carried, True, 2, tok, late)
    grad_values, grad_rows = plain(
        backward_kernel,
        (shaped(val.shape, BF16), shaped((rows, 2 * H * F), BF16)),
        (proj, val, grad_num, prefix, suffix),
        scratch=[pltpu.VMEM((2 * H * F, rows), F32)],
        name="backward",
    )
    rows_all = gather_rows(grad_rows)
    grad_tokens = dot(grad_rows, weight, 1, 1).astype(BF16)
    (part,) = plain(
        weight_grad_kernel,
        (shaped((tok.shape[1] // NDP, 2 * H * F), F32),),
        (cols_early, cols_late, rows_all),
        name="weight_grad",
    )
    grad_proj = reduce_ctx(part)
    return (attended[None], grad_tokens[None], grad_values[None], grad_proj)


def solution(mesh):
    return jax.shard_map(
        local,
        mesh=mesh,
        in_specs=(P("dp", "ctx", None), P("dp", None), P("dp", "ctx", None), P("dp", "ctx", None)),
        out_specs=(
            P("dp", "ctx", None),
            P("dp", "ctx", None),
            P("dp", "ctx", None),
            P(("dp", "ctx"), None),
        ),
        check_vma=False,
    )
```

time: 2050 us -> 171 us (0.08)
  the two profiles are of different devices: /device:TPU:32 before, /device:TPU:1 now
where the time goes in v2:
time: 171 us
  Pallas kernels  164 us (96%)
  matrix products  4.71 us (3%)
    pallas_call x2, Pallas kernels, scan(): pl.pallas_call(functools.partial(scan_kernel, later, slots), out_shape=(j...  68.3 us
    pallas_call x1, Pallas kernels, gather_weight(): pl.pallas_call(gather_weight_kernel, out_shape=jax.ShapeDtypeStruct((NDP...  35.1 us
    pallas_call x4, Pallas kernels, plain(): pl.pallas_call(kernel, out_shape=outs, in_specs=[VMEM] * len(args), out_s...  28.2 us
    pallas_call x1, Pallas kernels, reduce_ctx(): pl.pallas_call(reduce_kernel, out_shape=jax.ShapeDtypeStruct((own, width)...  18 us
    pallas_call x1, Pallas kernels, gather_rows(): pl.pallas_call(gather_rows_kernel, out_shape=jax.ShapeDtypeStruct((NDP,)...  14.3 us
    dot_general x1, matrix products, dot(): lax.dot_general(lhs, rhs, (((left,), (right,)), ((), ())), preferred_elem...  4.71 us

profile of v2, /device:TPU:1, one launch (start us, length us, event | category | flops | bytes accessed | tf_op | source)
XLA Modules:
  0.0 170.7 jit_solution(8237435404648766028)
XLA Ops:
  0.6 35.1 %gather_weight.1.w_ref = bf16[4096,512]{1,0:T(8,128)(2,1)} custom-call(bf16[512,512]{1,0:T(8,128)(2,1)} %w_ref.1), custom_call_target="tpu_custom_call" | custom-call | tf_op jit(solution)/shard_map/gather_weight/pallas_call | solution.py:93
  35.7 5.0 %project.1 = (f32[512,128]{1,0:T(8,128)}, f32[2,2,4,160,128]{4,3,2,1,0:T(8,128)}) custom-call(bf16[128,4096]{1,0:T(8,128)(2,1)} %bitcast.10, bf16[4096,512]{1,0:T(8,128)(2,1)} %gather_weight.1.w_ref, bf16[128,2048]{1,0:T(8,128)(2,1)} %bitcast.13), custom_call_target="tpu_custom_call" | custom-call | tf_op jit(solution)/shard_map/project/pallas_call | solution.py:551
  40.7 39.5 %scan_earlier.1 = (f32[2,2,4,160,128]{4,3,2,1,0:T(8,128)}, bf16[6,128,512]{2,1,0:T(8,128)(2,1)}) custom-call(f32[2,2,4,160,128]{4,3,2,1,0:T(8,128)} %get-tuple-element.16.refs_0_, bf16[128,4096]{1,0:T(8,128)(2,1)} %bitcast.11), custom_call_target="tpu_custom_call" | custom-call | tf_op jit(solution)/shard_map/scan_earlier/pallas_call | solution.py:236
  80.3 11.0 %forward.1 = (bf16[128,2048]{1,0:T(8,128)(2,1)}, f32[128,2048]{1,0:T(8,128)}, f32[2,2,4,160,128]{4,3,2,1,0:T(8,128)}) custom-call(f32[512,128]{1,0:T(8,128)} %get-tuple-element.15.proj_ref, bf16[128,2048]{1,0:T(8,128)(2,1)} %bitcast.14, bf16[128,2048]{1,0:T(8,128)(2,1)} %bitcast.17, f32[2,2,4,160,128]{4,3,2,1,0:T(8,128)} %get-tuple-element.17.prefix_ref), custom_call_target="tpu_custom_call" | custom-call | tf_op jit(solution)/shard_map/forward/pallas_call | solution.py:551
  91.3 28.8 %scan_later.1 = (f32[2,2,4,160,128]{4,3,2,1,0:T(8,128)}, bf16[2,128,512]{2,1,0:T(8,128)(2,1)}) custom-call(f32[2,2,4,160,128]{4,3,2,1,0:T(8,128)} %get-tuple-element.20.refs_0_, bf16[128,4096]{1,0:T(8,128)(2,1)} %bitcast.12), custom_call_target="tpu_custom_call" | custom-call | tf_op jit(solution)/shard_map/scan_later/pallas_call | solution.py:236
  120.1 8.8 %backward.1 = (bf16[128,2048]{1,0:T(8,128)(2,1)}, bf16[128,512]{1,0:T(8,128)(2,1)}) custom-call(f32[512,128]{1,0:T(8,128)} %get-tuple-element.15.proj_ref, bf16[128,2048]{1,0:T(8,128)(2,1)} %bitcast.15, f32[128,2048]{1,0:T(8,128)} %get-tuple-element.19.gn_ref, f32[2,2,4,160,128]{4,3,2,1,0:T(8,128)} %get-tuple-element.17.prefix_ref, ...), custom_call_target="tpu_custom_call" | custom-call | tf_op jit(solution)/shard_map/backward/pallas_call | solution.py:551
  129.0 4.7 %fusion = bf16[1,128,4096]{2,1,0:T(8,128)(2,1)} fusion(bf16[128,512]{1,0:T(8,128)(2,1)} %get-tuple-element.22.r_ref, bf16[4096,512]{1,0:T(8,128)(2,1)} %gather_weight.1.w_ref), kind=kOutput, calls=%fused_computation.1 | convolution fusion | flops 537395200 | bytes 5373952 | tf_op jit(solution)/shard_map/dot_general | solution.py:28
  133.7 14.3 %gather_rows.1.rows_ref = bf16[8,128,512]{2,1,0:T(8,128)(2,1)} custom-call(bf16[128,512]{1,0:T(8,128)(2,1)} %get-tuple-element.22.r_ref), custom_call_target="tpu_custom_call" | custom-call | tf_op jit(solution)/shard_map/gather_rows/pallas_call | solution.py:308
  148.0 3.3 %weight_grad.1 = f32[512,512]{1,0:T(8,128)} custom-call(bf16[6,128,512]{2,1,0:T(8,128)(2,1)} %get-tuple-element.24.early_ref, bf16[2,128,512]{2,1,0:T(8,128)(2,1)} %get-tuple-element.25.late_ref, bf16[8,128,512]{2,1,0:T(8,128)(2,1)} %gather_rows.1.rows_ref), custom_call_target="tpu_custom_call" | custom-call | tf_op jit(solution)/shard_map/weight_grad/pallas_call | solution.py:551
  151.3 18.0 %reduce_ctx.1 = f32[16,512]{1,0:T(8,128)} custom-call(f32[4,4,2,16,512]{4,3,2,1,0:T(8,128)} %bitcast.16), custom_call_target="tpu_custom_call" | custom-call | tf_op jit(solution)/shard_map/reduce_ctx/pallas_call | solution.py:374
  169.3 1.4 copy.9

commit v3 on v2

v3 whole, which is shorter than its diff:
```python
import functools

import jax
import jax.numpy as jnp
from jax import lax
from jax.experimental import pallas as pl
from jax.experimental.pallas import tpu as pltpu
from jax.sharding import PartitionSpec as P

H = 16
F = 16
DH = 128
EP = 160
QUAD = 1.0 / 32.0
EPSILON = 1e-05
MESH = pl.DeviceIdType.MESH
F32 = jnp.float32
BF16 = jnp.bfloat16
VMEM = pl.BlockSpec(memory_space=pltpu.VMEM)
NY = 4
NZ = 4
NDP = 8
NC = 2
RC = 2 * EP // NC


def dot(lhs, rhs, left, right):
    return lax.dot_general(lhs, rhs, (((left,), (right,)), ((), ())), preferred_element_type=F32)


def remote(src, dst, send, recv, **where):
    return pltpu.make_async_remote_copy(
        src_ref=src, dst_ref=dst, send_sem=send, recv_sem=recv, device_id=where, device_id_type=MESH
    )


def greet(peers):
    barrier = pltpu.get_barrier_semaphore()
    for where in peers:
        pl.semaphore_signal(barrier, inc=1, device_id=where, device_id_type=MESH)
    pl.semaphore_wait(barrier, len(peers))


def across(dp, dz, dx):
    return (dp // 4 + dz) % 2 * 4 + (dp % 4 + dx + 4) % 4


def place():
    ctx = lax.axis_index("ctx")
    return ctx // 8, (ctx // 2) % 4, ctx % 2


def at(z, y, c):
    return z * 8 + y * 2 + c


class Wires:
    def __init__(self, send, recv):
        self.send, self.recv, self.copies = send, recv, []

    def push(self, src, dst, **where):
        n = len(self.copies)
        copy = remote(src, dst, self.send.at[n], self.recv.at[n], **where)
        copy.start()
        self.copies.append(copy)
        return copy

    def drain(self):
        for copy in self.copies:
            copy.wait_send()


def gather_weight_kernel(w_ref, out_ref, own_sem, send, recv):
    dp = lax.axis_index("dp")
    z, y, c = place()
    partner = at(z, y, 1 - c)
    up, down = at(z, (y + 1) % NY, c), at(z, (y + 3) % NY, c)
    right, left, other = across(dp, 0, 1), across(dp, 0, 3), across(dp, 1, 0)
    greet(
        [{"dp": right}, {"dp": left}, {"dp": other}, {"ctx": partner}, {"ctx": up}, {"ctx": down}]
    )
    rows = w_ref.shape[0]
    half = rows // 2
    wide = half // 2
    thin = wide // NY
    wires = Wires(send, recv)

    def part(owner, start, size):
        return out_ref.at[pl.ds(pl.multiple_of(owner * rows + start, thin // 2), size)]

    def here(start, size):
        return w_ref.at[pl.ds(pl.multiple_of(start, thin // 2), size)]

    base_a = c * half
    base_b = c * half + wide

    def own_sends(start, size):
        src, dst = here(start, size), part(dp, start, size)
        return (
            wires.push(src, dst, dp=other),
            wires.push(src, dst, dp=right),
            wires.push(src, dst, dp=left),
        )

    def pass_on(owner, start, size):
        piece = part(owner, start, size)
        return wires.push(piece, piece, dp=right), wires.push(piece, piece, dp=left)

    def relay(near, far, start, size):
        one = part(near, start, size // 2)
        two = part(far, start + size // 2, size // 2)
        return wires.push(one, one, dp=right), wires.push(two, two, dp=left)

    def over_y(owner):
        piece = part(owner, base_b + y * thin, thin)
        return wires.push(piece, piece, ctx=up), wires.push(piece, piece, ctx=down)

    def on_chip(owner, start, size):
        piece = part(owner, start, size)
        return wires.push(piece, piece, ctx=partner)

    mine_b = base_b + y * thin
    b_over, b_right, b_left = own_sends(mine_b, thin)
    a_over, a_right, a_left = own_sends(base_a, wide)
    own = pltpu.make_async_copy(
        w_ref, out_ref.at[pl.ds(pl.multiple_of(dp * rows, rows), rows)], own_sem
    )
    own.start()
    owners = [other, left, right, across(dp, 1, 3), across(dp, 1, 1), across(dp, 0, 2), across(dp, 1, 2)]
    chain_y = []
    b_over.wait_recv()
    b_right2, b_left2 = pass_on(other, mine_b, thin)
    chain_y.append(over_y(owners[0]))
    b_right.wait_recv()
    b_left.wait_recv()
    b_ends = relay(left, right, mine_b, thin)
    chain_y.append(over_y(owners[1]))
    chain_y.append(over_y(owners[2]))
    a_over.wait_recv()
    a_right2, a_left2 = pass_on(other, base_a, wide)
    b_right2.wait_recv()
    b_left2.wait_recv()
    b_ends2 = relay(owners[3], owners[4], mine_b, thin)
    chain_y.append(over_y(owners[3]))
    chain_y.append(over_y(owners[4]))
    last = [on_chip(owners[0], base_a, wide)]
    a_right.wait_recv()
    a_left.wait_recv()
    a_ends = relay(left, right, base_a, wide)
    for copy in b_ends:
        copy.wait_recv()
    chain_y.append(over_y(owners[5]))
    for copy in b_ends2:
        copy.wait_recv()
    chain_y.append(over_y(owners[6]))
    last += [on_chip(owners[1], base_a, wide), on_chip(owners[2], base_a, wide)]
    ends_y = []
    below = base_b + (y + 3) % NY * thin
    above = base_b + (y + 1) % NY * thin + thin // 2

    def relay_y(n):
        chain_y[n][0].wait_recv()
        one = part(owners[n], below, thin // 2)
        ends_y.append([wires.push(one, one, ctx=up)])
        chain_y[n][1].wait_recv()
        two = part(owners[n], above, thin // 2)
        ends_y[-1].append(wires.push(two, two, ctx=down))

    for n in range(3):
        relay_y(n)
    a_right2.wait_recv()
    a_left2.wait_recv()
    a_ends2 = relay(owners[3], owners[4], base_a, wide)
    last += [on_chip(owners[3], base_a, wide), on_chip(owners[4], base_a, wide)]
    for n in range(3, 7):
        relay_y(n)
    for n in range(5):
        for copy in ends_y[n]:
            copy.wait_recv()
        last.append(on_chip(owners[n], base_b, wide))
    for copy in a_ends:
        copy.wait_recv()
    last.append(on_chip(owners[5], base_a, wide))
    for n in (5, 6):
        for copy in ends_y[n]:
            copy.wait_recv()
        last.append(on_chip(owners[n], base_b, wide))
    for copy in a_ends2:
        copy.wait_recv()
    last.append(on_chip(owners[6], base_a, wide))
    for copy in last:
        copy.wait_recv()
    wires.drain()
    own.wait()


def gather_weight(w):
    return pl.pallas_call(
        gather_weight_kernel,
        out_shape=jax.ShapeDtypeStruct((NDP * w.shape[0], w.shape[1]), w.dtype),
        in_specs=[VMEM],
        out_specs=VMEM,
        scratch_shapes=[pltpu.SemaphoreType.DMA] + [pltpu.SemaphoreType.DMA((64,))] * 2,
        compiler_params=pltpu.CompilerParams(collective_id=0, has_side_effects=True),
        name="gather_weight",
    )(w)


def scan_kernel(later, slots, *refs):
    s_ref, tok_ref, out_ref, cols_ref = refs[:4]
    sib, chip, yin, tz, zin, yout, pin, hand, pre, hop_y, hop_b, send, recv, send_t, recv_t, own_t = refs[4:]
    z, y, c = place()
    dp = lax.axis_index("dp")
    partner = at(z, y, 1 - c)
    up, down = at(z, (y + 1) % NY, c), at(z, (y + 3) % NY, c)
    fore, back = at((z + 1) % NZ, y, c), at((z + 3) % NZ, y, c)
    moves = [move for move in slots if move != (0, 0)]
    met = sorted({(dz, step % 4) for dz, dx in moves for step in (dx, -dx)})
    greet(
        [{"ctx": peer} for peer in (partner, up, down, fore, back)]
        + [{"dp": across(dp, dz, dx)} for dz, dx in met]
    )
    low, high = pl.ds(0, RC // 2), pl.ds(RC // 2, RC // 2)
    wires, token_wires = Wires(send, recv), Wires(send_t, recv_t)

    def before(other, me):
        return other > me if later else other < me

    copies_c = [wires.push(s_ref.at[1 - c, n], sib.at[n], ctx=partner) for n in range(NC)]
    width = cols_ref.shape[2]
    own_copies = []

    def send_tokens(dz_now):
        for index, (dz, dx) in enumerate(slots):
            if dz != dz_now:
                continue
            peer = across(dp, dz, dx)
            src = tok_ref.at[:, pl.ds(pl.multiple_of(peer * width, width), width)]
            if (dz, dx) == (0, 0):
                own_copies.append(pltpu.make_async_copy(src, cols_ref.at[index], own_t))
                own_copies[-1].start()
            else:
                token_wires.push(src, cols_ref.at[index], dp=peer)

    def exchange_y(src, dst, hop, n):
        far = src.at[n, (y + 2) % NY]
        return [
            wires.push(far.at[low], hop.at[n, 0], ctx=up),
            wires.push(far.at[high], hop.at[n, 1], ctx=down),
            wires.push(src.at[n, (y + 1) % NY], dst.at[n, y], ctx=up),
            wires.push(src.at[n, (y + 3) % NY], dst.at[n, y], ctx=down),
        ]

    def relay_y(copies, dst, hop, n):
        copies[0].wait_recv()
        one = wires.push(hop.at[n, 0], dst.at[n, (y + 3) % NY, low], ctx=up)
        copies[1].wait_recv()
        two = wires.push(hop.at[n, 1], dst.at[n, (y + 1) % NY, high], ctx=down)
        return copies[2:] + [one, two]

    copies_y = []
    for n in range(NC):
        copies_c[n].wait_recv()
        for j in range(NY):
            chip[n, j] = (s_ref[c, n, j] + sib[n, j]).astype(BF16)
        copies_y.append(exchange_y(chip, yin, hop_y, n))
    send_tokens(0)
    for n in range(NC):
        copies_y[n] = relay_y(copies_y[n], yin, hop_y, n)
    copies_z = []
    for n in range(NC):
        for copy in copies_y[n]:
            copy.wait_recv()
        blocks = [jnp.where(j == y, chip[n, j], yin[n, j]).astype(F32) for j in range(NY)]
        order = list(range(NY))[::-1] if later else list(range(NY))
        total = jnp.zeros_like(blocks[0])
        for j in order:
            pre[n, j] = total
            total = total + blocks[j]
        tz[n] = total.astype(BF16)
        copies_z.append(
            [
                wires.push(tz.at[n], zin.at[n, z], ctx=fore),
                wires.push(tz.at[n], zin.at[n, z], ctx=back),
            ]
        )
    for n in range(NC):
        copies_z[n][0].wait_recv()
        behind_me, ahead_me = (z + 3) % NZ, (z + 1) % NZ
        one = wires.push(zin.at[n, behind_me, low], zin.at[n, behind_me, low], ctx=fore)
        copies_z[n][1].wait_recv()
        two = wires.push(zin.at[n, ahead_me, high], zin.at[n, ahead_me, high], ctx=back)
        copies_z[n] = [one, two]
    send_tokens(1)
    copies_b = []
    for n in range(NC):
        for copy in copies_z[n]:
            copy.wait_recv()
        base = jnp.zeros(pre.shape[2:], F32)
        for j in range(NZ):
            base = base + jnp.where(before(j, z), zin[n, j].astype(F32), 0.0)
        for j in range(NY):
            yout[n, j] = (base + pre[n, j]).astype(BF16)
        copies_b.append(exchange_y(yout, pin, hop_b, n))
    for n in range(NC):
        copies_b[n] = relay_y(copies_b[n], pin, hop_b, n)
    copies_p = []
    for n in range(NC):
        for copy in copies_b[n]:
            copy.wait_recv()
        for j in range(NY):
            prefix = jnp.where(j == y, yout[n, j], pin[n, j]).astype(F32)
            hand[n, j] = prefix + jnp.where(before(c, 1 - c), s_ref[c, n, j], 0.0)
            out_ref[c, n, j] = prefix + jnp.where(before(1 - c, c), sib[n, j], 0.0)
        copies_p.append(wires.push(hand.at[n], out_ref.at[c, n], ctx=partner))
    for copy in copies_p:
        copy.wait_recv()
    wires.drain()
    for copy in token_wires.copies + own_copies:
        copy.wait()


def scan(state, later, collective, tokens, slots):
    shape = (2, NC, NY, RC, DH)
    slab = (NC, NY, RC, DH)
    thin = (NC, RC, DH)
    rows, width = tokens.shape
    dma = pltpu.SemaphoreType.DMA
    return pl.pallas_call(
        functools.partial(scan_kernel, later, slots),
        out_shape=(
            jax.ShapeDtypeStruct(shape, F32),
            jax.ShapeDtypeStruct((len(slots), rows, width // NDP), BF16),
        ),
        in_specs=[VMEM, VMEM],
        out_specs=(VMEM, VMEM),
        scratch_shapes=[
            pltpu.VMEM(slab, F32),
            pltpu.VMEM(slab, BF16),
            pltpu.VMEM(slab, BF16),
            pltpu.VMEM(thin, BF16),
            pltpu.VMEM((NC, NZ, RC, DH), BF16),
            pltpu.VMEM(slab, BF16),
            pltpu.VMEM(slab, BF16),
            pltpu.VMEM(slab, F32),
            pltpu.VMEM(slab, F32),
            pltpu.VMEM((NC, 2, RC // 2, DH), BF16),
            pltpu.VMEM((NC, 2, RC // 2, DH), BF16),
            dma((18 * NC,)),
            dma((18 * NC,)),
            dma((len(slots),)),
            dma((len(slots),)),
            dma,
        ],
        compiler_params=pltpu.CompilerParams(collective_id=collective, has_side_effects=True),
        name="scan_later" if later else "scan_earlier",
    )(state, tokens)


def tail_kernel(
    order, r_ref, early_ref, late_ref, w_hbm, gt_ref, out_ref,
    w_ref, all_ref, g_ref, sib, pair, yin, ysum, hop, zin, send, recv, w_sem,
):
    dp = lax.axis_index("dp")
    z, y, c = place()
    partner = at(z, y, 1 - c)
    up, down = at(z, (y + 1) % NY, c), at(z, (y + 3) % NY, c)
    right, left, other = across(dp, 0, 1), across(dp, 0, 3), across(dp, 1, 0)
    greet(
        [{"dp": right}, {"dp": left}, {"dp": other}]
        + [{"ctx": peer} for peer in (partner, up, down)]
        + [{"ctx": at((z + d) % NZ, y, c)} for d in range(1, NZ)]
    )
    wires = Wires(send, recv)
    half = r_ref.shape[0] // 2
    low, high = pl.ds(0, half), pl.ds(half, half)
    over = wires.push(r_ref, all_ref.at[4], dp=other)
    rights = [wires.push(r_ref, all_ref.at[1], dp=right)]
    lefts = [wires.push(r_ref, all_ref.at[3], dp=left)]
    load = pltpu.make_async_copy(w_hbm, w_ref, w_sem)
    load.start()
    early = early_ref.shape[0]

    def cols(slot_at):
        n = order.index((slot_at // 4, slot_at % 4))
        return early_ref[n] if n < early else late_ref[n - early]

    def product_of(slots):
        left_rows = jnp.concatenate([cols(n) for n in slots], axis=0)
        right_rows = jnp.concatenate([r_ref[...] if n == 0 else all_ref[n] for n in slots], axis=0)
        return dot(left_rows, right_rows, 0, 0).reshape(g_ref.shape)

    block = w_ref.shape[0] // 4

    def input_grad(n):
        piece = dot(r_ref[...], w_ref[n * block : (n + 1) * block, :], 1, 1)
        gt_ref[:, n * block : (n + 1) * block] = piece.astype(BF16)

    over.wait_recv()
    rights.append(wires.push(all_ref.at[4], all_ref.at[5], dp=right))
    lefts.append(wires.push(all_ref.at[4], all_ref.at[7], dp=left))
    load.wait()
    input_grad(0)
    ends = []
    for n in range(2):
        rights[n].wait_recv()
        one = wires.push(all_ref.at[4 * n + 1, low], all_ref.at[4 * n + 2, low], dp=right)
        lefts[n].wait_recv()
        two = wires.push(all_ref.at[4 * n + 3, high], all_ref.at[4 * n + 2, high], dp=left)
        ends.append((one, two))
        input_grad(2 * n + 1)
        if n == 0:
            g_ref[...] = product_of((0, 1, 3, 4))
            input_grad(2)
    for pair_of in ends:
        for copy in pair_of:
            copy.wait_recv()
    g_ref[...] += product_of((2, 5, 6, 7))

    copies_c = {}
    for d in (2, 1, 3, 0):
        to = (y + d) % NY
        copies_c[d] = wires.push(g_ref.at[:, to, 1 - c], sib.at[to], ctx=partner)
    near = []
    for d in (2, 1, 3, 0):
        to = (y + d) % NY
        copies_c[d].wait_recv()
        both = g_ref[:, to, c] + sib[to]
        if d == 0:
            ysum[...] = both
        else:
            pair[to] = both.astype(BF16)
            if d == 2:
                far = pair.at[to]
                relays = [
                    wires.push(far.at[pl.ds(0, NZ // 2)], hop.at[0], ctx=up),
                    wires.push(far.at[pl.ds(NZ // 2, NZ // 2)], hop.at[1], ctx=down),
                ]
            else:
                near.append(wires.push(pair.at[to], yin.at[y], ctx=up if d == 1 else down))
    relays[0].wait_recv()
    near.append(wires.push(hop.at[0], yin.at[(y + 3) % NY, pl.ds(0, NZ // 2)], ctx=up))
    relays[1].wait_recv()
    near.append(wires.push(hop.at[1], yin.at[(y + 1) % NY, pl.ds(NZ // 2, NZ // 2)], ctx=down))
    for copy in near:
        copy.wait_recv()
    for j in range(NY):
        ysum[...] += jnp.where(j == y, 0.0, yin[j].astype(F32))
    copies_z = []
    for d in (2, 1, 3):
        to = (z + d) % NZ
        copies_z.append(wires.push(ysum.at[to], zin.at[z], ctx=at(to, y, c)))
    for copy in copies_z:
        copy.wait_recv()
    total = ysum[z]
    for j in range(NZ):
        total = total + jnp.where(j == z, 0.0, zin[j])
    out_ref[...] = total
    wires.drain()


def tail(rows, early, late, order, weight):
    width = rows.shape[1]
    own = early.shape[2] // (2 * NY * NZ)
    slab = (NY, NZ, own, width)
    dma = pltpu.SemaphoreType.DMA
    return pl.pallas_call(
        functools.partial(tail_kernel, order),
        out_shape=(
            jax.ShapeDtypeStruct((rows.shape[0], weight.shape[0]), BF16),
            jax.ShapeDtypeStruct((own, width), F32),
        ),
        in_specs=[VMEM, VMEM, VMEM, pl.BlockSpec(memory_space=pl.ANY)],
        out_specs=(VMEM, VMEM),
        scratch_shapes=[
            pltpu.VMEM(weight.shape, BF16),
            pltpu.VMEM((NDP,) + rows.shape, BF16),
            pltpu.VMEM((NZ, NY, 2, own, width), F32),
            pltpu.VMEM(slab, F32),
            pltpu.VMEM(slab, BF16),
            pltpu.VMEM(slab, BF16),
            pltpu.VMEM((NZ, own, width), F32),
            pltpu.VMEM((2, NZ // 2, own, width), BF16),
            pltpu.VMEM((NZ, own, width), F32),
            dma((24,)),
            dma((24,)),
            dma,
        ],
        compiler_params=pltpu.CompilerParams(collective_id=3, has_side_effects=True),
        name="tail",
    )(rows, early, late, weight)


def ahead(x, d):
    return pltpu.roll(x, F - d, 0)


def behind(x, d):
    return pltpu.roll(x, d, 0)


def features(x, weighted):
    quad, linear = (QUAD, 0.25) if weighted else (1.0, 1.0)
    twice = 2.0 * quad if weighted else 1.0
    parts = [x * x * quad] + [x * ahead(x, d) * twice for d in range(1, 8)]
    parts += [x[:8] * x[8:] * twice, x * linear]
    row = lax.broadcasted_iota(jnp.int32, (8, x.shape[1]), 0)
    parts.append(jnp.where(row == 0, 1.0, 0.0))
    return jnp.concatenate(parts, axis=0)


def pull_features(x, cot):
    out = 2.0 * QUAD * cot[:F] * x
    for d in range(1, 8):
        part = 2.0 * QUAD * cot[F * d : F * (d + 1)]
        out = out + part * ahead(x, d) + behind(part * x, d)
    half = 2.0 * QUAD * cot[128:136]
    out = out + jnp.concatenate([half * x[8:], half * x[:8]], axis=0)
    return out + 0.25 * cot[136:152]


def split(x):
    high = x.astype(BF16)
    return high, (x - high.astype(F32)).astype(BF16)


def scores(q, k):
    qh, ql = split(q)
    kh, kl = split(k)
    left = jnp.concatenate([qh, qh, ql, ql], axis=0)
    right = jnp.concatenate([kh, kl, kh, kl], axis=0)
    return dot(left, right, 0, 0) * 0.25


def product(feat, state):
    fh, fl = split(feat)
    sh, sl = split(state)
    left = jnp.concatenate([fh, fl, fh], axis=0)
    right = jnp.concatenate([sh, sh, sl], axis=0)
    return dot(left, right, 0, 0)


def pulled(state, rows, fine=None):
    high, low = split(state)
    both = dot(jnp.concatenate([high, low], axis=0), rows, 1, 1)
    both = both[:EP] + both[EP:]
    return both if fine is None else both + dot(high, fine, 1, 1)


def causal():
    shape = (128, 128)
    return lax.broadcasted_iota(jnp.int32, shape, 0) >= lax.broadcasted_iota(jnp.int32, shape, 1)


def head_cols(h):
    return slice(h * DH, (h + 1) * DH)


def head_rows(h):
    return slice(h * F, (h + 1) * F)


def slot(h):
    return h // 8, h % 2, (h // 2) % 4


def project_kernel(tok_ref, w_ref, v_ref, proj_ref, state_ref):
    proj = dot(tok_ref[...], w_ref[...], 1, 0)
    proj_ref[...] = proj.T
    for h in range(H):
        keys = proj_ref[256 + h * F : 256 + (h + 1) * F, :]
        high, low = split(features(keys, False))
        v = v_ref[:, head_cols(h)]
        state = dot(
            jnp.concatenate([high, low], axis=1), jnp.concatenate([v, v], axis=0), 1, 0
        )
        state_ref[slot(h)] = state


def forward_kernel(proj_ref, v_ref, g_ref, prefix_ref, att_ref, gn_ref, state_ref):
    mask = causal()
    for h in range(H):
        q = proj_ref[head_rows(h), :]
        k = proj_ref[256 + h * F : 256 + (h + 1) * F, :]
        a = scores(q, k)
        kernel = jnp.where(mask, 1.0 + a + 0.5 * a * a, 0.0)
        feat = features(q, False)
        v = v_ref[:, head_cols(h)]
        numerator = dot(
            jnp.concatenate(split(kernel), axis=1), jnp.concatenate([v, v], axis=0), 1, 0
        )
        numerator += product(features(q, True), prefix_ref[slot(h)])
        inv = lax.rsqrt(jnp.mean(numerator * numerator, axis=1, keepdims=True) + EPSILON)
        normed = numerator * inv
        att_ref[:, head_cols(h)] = normed.astype(BF16)
        g = g_ref[:, head_cols(h)].astype(F32)
        gn = inv * (g - normed * jnp.mean(normed * g, axis=1, keepdims=True))
        gn_ref[:, head_cols(h)] = gn
        high, low = split(feat)
        gh, gl = split(gn)
        state_ref[slot(h)] = dot(
            jnp.concatenate([high, low, high], axis=1),
            jnp.concatenate([gh, gh, gl], axis=0),
            1,
            0,
        )


def backward_kernel(proj_ref, v_ref, gn_ref, prefix_ref, suffix_ref, gv_ref, rows_ref, acc):
    mask = causal()
    for h in range(H):
        q = proj_ref[head_rows(h), :]
        k = proj_ref[256 + h * F : 256 + (h + 1) * F, :]
        v = v_ref[:, head_cols(h)]
        gh, gl = split(gn_ref[:, head_cols(h)])
        a = scores(q, k)
        mh, ml = split(jnp.where(mask, 1.0 + a + 0.5 * a * a, 0.0))
        mixing = dot(
            jnp.concatenate([gh, gl], axis=1), jnp.concatenate([v, v], axis=1), 1, 1
        )
        sh, sl = split(jnp.where(mask, mixing * (1.0 + a) * 0.25, 0.0))
        qh, ql = split(q)
        kh, kl = split(k)
        dq = dot(jnp.concatenate([kh, kl], axis=0), sh, 1, 1)
        dq = dq[:F] + dq[F:] + dot(kh, sl, 1, 1)
        dk = dot(jnp.concatenate([qh, ql], axis=0), sh, 1, 0)
        dk = dk[:F] + dk[F:] + dot(qh, sl, 1, 0)
        pre = prefix_ref[slot(h)]
        suf = suffix_ref[slot(h)]
        acc[head_rows(h), :] = dq + pull_features(q, pulled(pre, gh, gl))
        acc[256 + h * F : 256 + (h + 1) * F, :] = dk + pull_features(k, pulled(suf, v))
        gv = dot(
            jnp.concatenate([mh, ml, mh], axis=0), jnp.concatenate([gh, gh, gl], axis=0), 0, 0
        )
        gv += product(features(k, True), suf)
        gv_ref[:, head_cols(h)] = gv.astype(BF16)
    rows_ref[...] = acc[...].T.astype(BF16)


def plain(kernel, outs, args, scratch=(), name=None):
    return pl.pallas_call(
        kernel,
        out_shape=outs,
        in_specs=[VMEM] * len(args),
        out_specs=jax.tree.map(lambda _: VMEM, outs),
        scratch_shapes=list(scratch),
        name=name,
    )(*args)


def shaped(shape, dtype):
    return jax.ShapeDtypeStruct(shape, dtype)


def local(tokens, proj_weight, values, grad_out):
    tok, val, up = tokens[0], values[0], grad_out[0]
    rows = tok.shape[0]
    packed = shaped((2, NC, NY, RC, DH), F32)
    weight = gather_weight(proj_weight)
    proj, state = plain(
        project_kernel, (shaped((2 * H * F, rows), F32), packed), (tok, weight, val), name="project"
    )
    early = ((0, 0), (0, 1), (0, 3), (1, 0), (1, 2))
    late = ((0, 2), (1, 1), (1, 3))
    prefix, cols_early = scan(state, False, 1, tok, early)
    attended, grad_num, carried = plain(
        forward_kernel,
        (shaped(val.shape, BF16), shaped(val.shape, F32), packed),
        (proj, val, up, prefix),
        name="forward",
    )
    suffix, cols_late = scan(carried, True, 2, tok, late)
    grad_values, grad_rows = plain(
        backward_kernel,
        (shaped(val.shape, BF16), shaped((rows, 2 * H * F), BF16)),
        (proj, val, grad_num, prefix, suffix),
        scratch=[pltpu.VMEM((2 * H * F, rows), F32)],
        name="backward",
    )
    grad_tokens, grad_proj = tail(grad_rows, cols_early, cols_late, early + late, weight)
    return (attended[None], grad_tokens[None], grad_values[None], grad_proj)


def solution(mesh):
    return jax.shard_map(
        local,
        mesh=mesh,
        in_specs=(P("dp", "ctx", None), P("dp", None), P("dp", "ctx", None), P("dp", "ctx", None)),
        out_specs=(
            P("dp", "ctx", None),
            P("dp", "ctx", None),
            P("dp", "ctx", None),
            P(("dp", "ctx"), None),
        ),
        check_vma=False,
    )
```

time: 171 us -> 157 us (0.918)
  Pallas kernels: 164 us -> 153 us
  matrix products: 4.71 us -> 0 us
    pallas_call x1, Pallas kernels: 35.1 us -> 28.4 us  [gather_weight(): pl.pallas_call(gather_weight_kernel, out_shape=jax.ShapeDtypeStruct((NDP...]
    dot_general x1 -> x0, matrix products: 4.71 us -> none  [dot(): lax.dot_general(lhs, rhs, (((left,), (right,)), ((), ())), preferred_elem...]
    pallas_call x4 -> x3, Pallas kernels: 28.2 us -> 24.8 us  [plain(): pl.pallas_call(kernel, out_shape=outs, in_specs=[VMEM] * len(args), out_s...]
    pallas_call x2 -> x1, Pallas kernels: 32.3 us -> 33 us  [tail(): pl.pallas_call(functools.partial(tail_kernel, order), out_shape=(jax.Shap...]
where the time goes in v3:
time: 157 us
  Pallas kernels  153 us (97%)
  local copies, waits for them, and re-layouts  2.91 us (2%)
    pallas_call x2, Pallas kernels, scan(): pl.pallas_call(functools.partial(scan_kernel, later, slots), out_shape=(j...  67 us
    pallas_call x1, Pallas kernels, tail(): pl.pallas_call(functools.partial(tail_kernel, order), out_shape=(jax.Shap...  33 us
    pallas_call x1, Pallas kernels, gather_weight(): pl.pallas_call(gather_weight_kernel, out_shape=jax.ShapeDtypeStruct((NDP...  28.4 us
    pallas_call x3, Pallas kernels, plain(): pl.pallas_call(kernel, out_shape=outs, in_specs=[VMEM] * len(args), out_s...  24.8 us

profile of v3, /device:TPU:1, one launch (start us, length us, event | category | flops | bytes accessed | tf_op | source)
XLA Modules:
  0.0 156.9 jit_solution(5894482127324245949)
XLA Ops:
  0.6 28.4 %gather_weight.1.w_ref.w_hbm = bf16[4096,512]{1,0:T(8,128)(2,1)} custom-call(bf16[512,512]{1,0:T(8,128)(2,1)} %w_ref.1), custom_call_target="tpu_custom_call" | custom-call | tf_op jit(solution)/shard_map/gather_weight/pallas_call | solution.py:198
  29.0 5.0 %project.1 = (f32[512,128]{1,0:T(8,128)}, f32[2,2,4,160,128]{4,3,2,1,0:T(8,128)}) custom-call(bf16[128,4096]{1,0:T(8,128)(2,1)} %bitcast.6, bf16[4096,512]{1,0:T(8,128)(2,1)} %gather_weight.1.w_ref.w_hbm, bf16[128,2048]{1,0:T(8,128)(2,1)} %bitcast.9), custom_call_target="tpu_custom_call" | custom-call | tf_op jit(solution)/shard_map/project/pallas_call | solution.py:641
  34.1 34.4 %scan_earlier.1 = (f32[2,2,4,160,128]{4,3,2,1,0:T(8,128)}, bf16[5,128,512]{2,1,0:T(8,128)(2,1)}) custom-call(f32[2,2,4,160,128]{4,3,2,1,0:T(8,128)} %get-tuple-element.18.refs_0_, bf16[128,4096]{1,0:T(8,128)(2,1)} %bitcast.7), custom_call_target="tpu_custom_call" | custom-call | tf_op jit(solution)/shard_map/scan_earlier/pallas_call | solution.py:329
  68.5 11.0 %forward.1 = (bf16[128,2048]{1,0:T(8,128)(2,1)}, f32[128,2048]{1,0:T(8,128)}, f32[2,2,4,160,128]{4,3,2,1,0:T(8,128)}) custom-call(f32[512,128]{1,0:T(8,128)} %get-tuple-element.17.proj_ref, bf16[128,2048]{1,0:T(8,128)(2,1)} %bitcast.10, bf16[128,2048]{1,0:T(8,128)(2,1)} %bitcast.13, f32[2,2,4,160,128]{4,3,2,1,0:T(8,128)} %get-tuple-element.19.prefix_ref), custom_call_target="tpu_custom_call" | custom-call | tf_op jit(solution)/shard_map/forward/pallas_call | solution.py:641
  79.5 32.6 %scan_later.1 = (f32[2,2,4,160,128]{4,3,2,1,0:T(8,128)}, bf16[3,128,512]{2,1,0:T(8,128)(2,1)}) custom-call(f32[2,2,4,160,128]{4,3,2,1,0:T(8,128)} %get-tuple-element.22.refs_0_, bf16[128,4096]{1,0:T(8,128)(2,1)} %bitcast.8), custom_call_target="tpu_custom_call" | custom-call | tf_op jit(solution)/shard_map/scan_later/pallas_call | solution.py:329
  112.1 8.8 %backward.1 = (bf16[128,2048]{1,0:T(8,128)(2,1)}, bf16[128,512]{1,0:T(8,128)(2,1)}) custom-call(f32[512,128]{1,0:T(8,128)} %get-tuple-element.17.proj_ref, bf16[128,2048]{1,0:T(8,128)(2,1)} %bitcast.11, f32[128,2048]{1,0:T(8,128)} %get-tuple-element.21.gn_ref, f32[2,2,4,160,128]{4,3,2,1,0:T(8,128)} %get-tuple-element.19.prefix_ref, ...), custom_call_target="tpu_custom_call" | custom-call | tf_op jit(solution)/shard_map/backward/pallas_call | solution.py:641
  120.9 33.0 %tail.1 = (bf16[128,4096]{1,0:T(8,128)(2,1)}, f32[16,512]{1,0:T(8,128)}) custom-call(bf16[128,512]{1,0:T(8,128)(2,1)} %get-tuple-element.24.r_ref, bf16[5,128,512]{2,1,0:T(8,128)(2,1)} %get-tuple-element.25.early_ref, bf16[3,128,512]{2,1,0:T(8,128)(2,1)} %get-tuple-element.26.late_ref, bf16[4096,512]{1,0:T(8,128)(2,1)} %gather_weight.1.w_ref.w_hbm), custom_call_target="tpu_custom_call" | custom-call | tf_op jit(solution)/shard_map/tail/pallas_call | solution.py:467
  153.9 0.0 copy-start
  153.9 2.3 %copy.10 = bf16[1,128,4096]{2,1,0:T(8,128)(2,1)} copy(bf16[1,128,4096]{2,1,0:T(8,128)(2,1)} %bitcast.12) | data formatting | bytes 2097152
  156.2 0.0 copy-done
  156.2 0.6 copy.11
Async XLA Ops:
  153.9 2.3 %copy-start = (f32[16,512]{1,0:T(8,128)S(1)}, f32[16,512]{1,0:T(8,128)}, u32[]{:S(2)}) copy-start(f32[16,512]{1,0:T(8,128)} %get-tuple-element.37) | copy-start | bytes 98308

commit v4 on v3

--- a/solution.py
+++ b/solution.py
@@ -7,7 +7,7 @@
 from jax.experimental.pallas import tpu as pltpu
 from jax.sharding import PartitionSpec as P
 
-H = 16
+H = 8
 F = 16
 DH = 128
 EP = 160
@@ -22,6 +22,8 @@
 NDP = 8
 NC = 2
 RC = 2 * EP // NC
+HF = H * F
+HD = H * DH
 
 
 def dot(lhs, rhs, left, right):
@@ -70,32 +72,31 @@
             copy.wait_send()
 
 
-def gather_weight_kernel(w_ref, out_ref, own_sem, send, recv):
+def gather_kernel(w_ref, tok_ref, v_ref, g_ref, out_ref, tok2_ref, v2_ref, g2_ref, own_sem, send, recv):
     dp = lax.axis_index("dp")
     z, y, c = place()
     partner = at(z, y, 1 - c)
     up, down = at(z, (y + 1) % NY, c), at(z, (y + 3) % NY, c)
     right, left, other = across(dp, 0, 1), across(dp, 0, 3), across(dp, 1, 0)
+    rows = w_ref.shape[0]
+    wide = rows // 2
+    thin = wide // NY
+    wires = Wires(send, recv)
+    mine = pl.ds(pl.multiple_of(dp * rows, rows), rows)
+    for n in range(2):
+        columns = pl.ds(pl.multiple_of(n * 2 * HF + c * HF, HF), HF)
+        out_ref[mine, n * HF : (n + 1) * HF] = w_ref[:, columns]
     greet(
         [{"dp": right}, {"dp": left}, {"dp": other}, {"ctx": partner}, {"ctx": up}, {"ctx": down}]
     )
-    rows = w_ref.shape[0]
-    half = rows // 2
-    wide = half // 2
-    thin = wide // NY
-    wires = Wires(send, recv)
 
     def part(owner, start, size):
         return out_ref.at[pl.ds(pl.multiple_of(owner * rows + start, thin // 2), size)]
 
-    def here(start, size):
-        return w_ref.at[pl.ds(pl.multiple_of(start, thin // 2), size)]
-
-    base_a = c * half
-    base_b = c * half + wide
+    base_a, base_b = 0, wide
 
     def own_sends(start, size):
-        src, dst = here(start, size), part(dp, start, size)
+        src = dst = part(dp, start, size)
         return (
             wires.push(src, dst, dp=other),
             wires.push(src, dst, dp=right),
@@ -115,17 +116,25 @@
         piece = part(owner, base_b + y * thin, thin)
         return wires.push(piece, piece, ctx=up), wires.push(piece, piece, ctx=down)
 
-    def on_chip(owner, start, size):
-        piece = part(owner, start, size)
-        return wires.push(piece, piece, ctx=partner)
-
     mine_b = base_b + y * thin
     b_over, b_right, b_left = own_sends(mine_b, thin)
     a_over, a_right, a_left = own_sends(base_a, wide)
-    own = pltpu.make_async_copy(
-        w_ref, out_ref.at[pl.ds(pl.multiple_of(dp * rows, rows), rows)], own_sem
-    )
-    own.start()
+    count = tok_ref.shape[0]
+    ours = pl.ds(pl.multiple_of(c * count, count), count)
+    own_half = pl.ds(pl.multiple_of(c * HD, HD), HD)
+    their_half = pl.ds(pl.multiple_of((1 - c) * HD, HD), HD)
+    last = [
+        wires.push(v_ref.at[:, their_half], v2_ref.at[ours], ctx=partner),
+        wires.push(g_ref.at[:, their_half], g2_ref.at[ours], ctx=partner),
+        wires.push(tok_ref, tok2_ref.at[ours], ctx=partner),
+    ]
+    own = [
+        pltpu.make_async_copy(v_ref.at[:, own_half], v2_ref.at[ours], own_sem.at[0]),
+        pltpu.make_async_copy(g_ref.at[:, own_half], g2_ref.at[ours], own_sem.at[1]),
+        pltpu.make_async_copy(tok_ref, tok2_ref.at[ours], own_sem.at[2]),
+    ]
+    for copy in own:
+        copy.start()
     owners = [other, left, right, across(dp, 1, 3), across(dp, 1, 1), across(dp, 0, 2), across(dp, 1, 2)]
     chain_y = []
     b_over.wait_recv()
@@ -143,7 +152,6 @@
     b_ends2 = relay(owners[3], owners[4], mine_b, thin)
     chain_y.append(over_y(owners[3]))
     chain_y.append(over_y(owners[4]))
-    last = [on_chip(owners[0], base_a, wide)]
     a_right.wait_recv()
     a_left.wait_recv()
     a_ends = relay(left, right, base_a, wide)
@@ -153,7 +161,6 @@
     for copy in b_ends2:
         copy.wait_recv()
     chain_y.append(over_y(owners[6]))
-    last += [on_chip(owners[1], base_a, wide), on_chip(owners[2], base_a, wide)]
     ends_y = []
     below = base_b + (y + 3) % NY * thin
     above = base_b + (y + 1) % NY * thin + thin // 2
@@ -171,44 +178,38 @@
     a_right2.wait_recv()
     a_left2.wait_recv()
     a_ends2 = relay(owners[3], owners[4], base_a, wide)
-    last += [on_chip(owners[3], base_a, wide), on_chip(owners[4], base_a, wide)]
     for n in range(3, 7):
         relay_y(n)
-    for n in range(5):
-        for copy in ends_y[n]:
+    for copies in ends_y + [a_ends, a_ends2, last]:
+        for copy in copies:
             copy.wait_recv()
-        last.append(on_chip(owners[n], base_b, wide))
-    for copy in a_ends:
-        copy.wait_recv()
-    last.append(on_chip(owners[5], base_a, wide))
-    for n in (5, 6):
-        for copy in ends_y[n]:
-            copy.wait_recv()
-        last.append(on_chip(owners[n], base_b, wide))
-    for copy in a_ends2:
-        copy.wait_recv()
-    last.append(on_chip(owners[6], base_a, wide))
-    for copy in last:
-        copy.wait_recv()
     wires.drain()
-    own.wait()
-
-
-def gather_weight(w):
+    for copy in own:
+        copy.wait()
+
+
+def gather(w, tokens, values, grad_out):
+    count = 2 * tokens.shape[0]
     return pl.pallas_call(
-        gather_weight_kernel,
-        out_shape=jax.ShapeDtypeStruct((NDP * w.shape[0], w.shape[1]), w.dtype),
-        in_specs=[VMEM],
-        out_specs=VMEM,
-        scratch_shapes=[pltpu.SemaphoreType.DMA] + [pltpu.SemaphoreType.DMA((64,))] * 2,
+        gather_kernel,
+        out_shape=(
+            jax.ShapeDtypeStruct((NDP * w.shape[0], 2 * HF), w.dtype),
+            jax.ShapeDtypeStruct((count, tokens.shape[1]), BF16),
+            jax.ShapeDtypeStruct((count, HD), BF16),
+            jax.ShapeDtypeStruct((count, HD), BF16),
+        ),
+        in_specs=[VMEM] * 4,
+        out_specs=(VMEM,) * 4,
+        scratch_shapes=[pltpu.SemaphoreType.DMA((3,))] + [pltpu.SemaphoreType.DMA((52,))] * 2,
         compiler_params=pltpu.CompilerParams(collective_id=0, has_side_effects=True),
-        name="gather_weight",
-    )(w)
-
-
-def scan_kernel(later, slots, *refs):
-    s_ref, tok_ref, out_ref, cols_ref = refs[:4]
-    sib, chip, yin, tz, zin, yout, pin, hand, pre, hop_y, hop_b, send, recv, send_t, recv_t, own_t = refs[4:]
+        name="gather",
+    )(w, tokens, values, grad_out)
+
+
+def scan_kernel(
+    later, slots, across_chip, s_ref, tok_ref, side_ref, out_ref, cols_ref, far_ref,
+    yin, tz, zin, yout, pre, hop_y, hop_b, send, recv, send_t, recv_t, own_t,
+):
     z, y, c = place()
     dp = lax.axis_index("dp")
     partner = at(z, y, 1 - c)
@@ -226,7 +227,6 @@
     def before(other, me):
         return other > me if later else other < me
 
-    copies_c = [wires.push(s_ref.at[1 - c, n], sib.at[n], ctx=partner) for n in range(NC)]
     width = cols_ref.shape[2]
     own_copies = []
 
@@ -260,10 +260,8 @@
 
     copies_y = []
     for n in range(NC):
-        copies_c[n].wait_recv()
-        for j in range(NY):
-            chip[n, j] = (s_ref[c, n, j] + sib[n, j]).astype(BF16)
-        copies_y.append(exchange_y(chip, yin, hop_y, n))
+        copies_y.append(exchange_y(s_ref, yin, hop_y, n))
+    token_wires.push(*across_chip(side_ref, far_ref, c), ctx=partner)
     send_tokens(0)
     for n in range(NC):
         copies_y[n] = relay_y(copies_y[n], yin, hop_y, n)
@@ -271,7 +269,7 @@
     for n in range(NC):
         for copy in copies_y[n]:
             copy.wait_recv()
-        blocks = [jnp.where(j == y, chip[n, j], yin[n, j]).astype(F32) for j in range(NY)]
+        blocks = [jnp.where(j == y, s_ref[n, j], yin[n, j]).astype(F32) for j in range(NY)]
         order = list(range(NY))[::-1] if later else list(range(NY))
         total = jnp.zeros_like(blocks[0])
         for j in order:
@@ -301,65 +299,63 @@
             base = base + jnp.where(before(j, z), zin[n, j].astype(F32), 0.0)
         for j in range(NY):
             yout[n, j] = (base + pre[n, j]).astype(BF16)
-        copies_b.append(exchange_y(yout, pin, hop_b, n))
+        out_ref[n, y] = yout[n, y]
+        copies_b.append(exchange_y(yout, out_ref, hop_b, n))
     for n in range(NC):
-        copies_b[n] = relay_y(copies_b[n], pin, hop_b, n)
-    copies_p = []
-    for n in range(NC):
-        for copy in copies_b[n]:
+        copies_b[n] = relay_y(copies_b[n], out_ref, hop_b, n)
+    for copies in copies_b:
+        for copy in copies:
             copy.wait_recv()
-        for j in range(NY):
-            prefix = jnp.where(j == y, yout[n, j], pin[n, j]).astype(F32)
-            hand[n, j] = prefix + jnp.where(before(c, 1 - c), s_ref[c, n, j], 0.0)
-            out_ref[c, n, j] = prefix + jnp.where(before(1 - c, c), sib[n, j], 0.0)
-        copies_p.append(wires.push(hand.at[n], out_ref.at[c, n], ctx=partner))
-    for copy in copies_p:
-        copy.wait_recv()
     wires.drain()
     for copy in token_wires.copies + own_copies:
         copy.wait()
 
 
-def scan(state, later, collective, tokens, slots):
-    shape = (2, NC, NY, RC, DH)
+def scan(state, later, collective, tokens, slots, side, far, across_chip):
     slab = (NC, NY, RC, DH)
-    thin = (NC, RC, DH)
     rows, width = tokens.shape
     dma = pltpu.SemaphoreType.DMA
+    hbm = pl.BlockSpec(memory_space=pl.ANY)
     return pl.pallas_call(
-        functools.partial(scan_kernel, later, slots),
+        functools.partial(scan_kernel, later, slots, across_chip),
         out_shape=(
-            jax.ShapeDtypeStruct(shape, F32),
+            jax.ShapeDtypeStruct(slab, BF16),
             jax.ShapeDtypeStruct((len(slots), rows, width // NDP), BF16),
+            far,
         ),
-        in_specs=[VMEM, VMEM],
-        out_specs=(VMEM, VMEM),
+        in_specs=[VMEM, VMEM, hbm],
+        out_specs=(VMEM, VMEM, hbm),
         scratch_shapes=[
-            pltpu.VMEM(slab, F32),
             pltpu.VMEM(slab, BF16),
-            pltpu.VMEM(slab, BF16),
-            pltpu.VMEM(thin, BF16),
+            pltpu.VMEM((NC, RC, DH), BF16),
             pltpu.VMEM((NC, NZ, RC, DH), BF16),
             pltpu.VMEM(slab, BF16),
-            pltpu.VMEM(slab, BF16),
-            pltpu.VMEM(slab, F32),
             pltpu.VMEM(slab, F32),
             pltpu.VMEM((NC, 2, RC // 2, DH), BF16),
             pltpu.VMEM((NC, 2, RC // 2, DH), BF16),
-            dma((18 * NC,)),
-            dma((18 * NC,)),
-            dma((len(slots),)),
-            dma((len(slots),)),
+            dma((16 * NC,)),
+            dma((16 * NC,)),
+            dma((len(slots) + 1,)),
+            dma((len(slots) + 1,)),
             dma,
         ],
         compiler_params=pltpu.CompilerParams(collective_id=collective, has_side_effects=True),
         name="scan_later" if later else "scan_earlier",
-    )(state, tokens)
+    )(state, tokens, side)
+
+
+def whole(side_ref, far_ref, c):
+    return side_ref, far_ref
+
+
+def their_rows(side_ref, far_ref, c):
+    count = far_ref.shape[0]
+    return side_ref.at[pl.ds(pl.multiple_of((1 - c) * count, count), count)], far_ref
 
 
 def tail_kernel(
-    order, r_ref, early_ref, late_ref, w_hbm, gt_ref, out_ref,
-    w_ref, all_ref, g_ref, sib, pair, yin, ysum, hop, zin, send, recv, w_sem,
+    order, rows_ref, early_ref, late_ref, w_hbm, far_hbm, gv_ref, gt_ref, out_ref, gv_far_ref,
+    w_ref, far_ref, r_ref, r_far, all_ref, g_ref, sib, pair, yin, ysum, hop, zin, send, recv, w_sem,
 ):
     dp = lax.axis_index("dp")
     z, y, c = place()
@@ -372,13 +368,29 @@
         + [{"ctx": at((z + d) % NZ, y, c)} for d in range(1, NZ)]
     )
     wires = Wires(send, recv)
-    half = r_ref.shape[0] // 2
+    count = r_ref.shape[0]
+    half = count // 2
+    ours = pl.ds(pl.multiple_of(c * count, count), count)
+    theirs = pl.ds(pl.multiple_of((1 - c) * count, count), count)
+    swap = wires.push(rows_ref.at[theirs], r_far, ctx=partner)
+    loads = [
+        pltpu.make_async_copy(w_hbm, w_ref, w_sem.at[0]),
+        pltpu.make_async_copy(far_hbm, far_ref, w_sem.at[1]),
+    ]
+    for load in loads:
+        load.start()
+    for n in range(2):
+        columns = pl.ds(pl.multiple_of(n * 2 * HF + c * HF, HF), HF)
+        r_ref[:, columns] = rows_ref[ours, n * HF : (n + 1) * HF]
+    swap.wait_recv()
+    for n in range(2):
+        columns = pl.ds(pl.multiple_of(n * 2 * HF + (1 - c) * HF, HF), HF)
+        r_ref[:, columns] = r_far[:, n * HF : (n + 1) * HF]
     low, high = pl.ds(0, half), pl.ds(half, half)
     over = wires.push(r_ref, all_ref.at[4], dp=other)
     rights = [wires.push(r_ref, all_ref.at[1], dp=right)]
     lefts = [wires.push(r_ref, all_ref.at[3], dp=left)]
-    load = pltpu.make_async_copy(w_hbm, w_ref, w_sem)
-    load.start()
+    swap_values = wires.push(gv_ref.at[theirs], gv_far_ref, ctx=partner)
     early = early_ref.shape[0]
 
     def cols(slot_at):
@@ -393,13 +405,16 @@
     block = w_ref.shape[0] // 4
 
     def input_grad(n):
-        piece = dot(r_ref[...], w_ref[n * block : (n + 1) * block, :], 1, 1)
+        span = slice(n * block, (n + 1) * block)
+        piece = dot(rows_ref[ours, :], w_ref[span, :], 1, 1)
+        piece += dot(r_far[...], far_ref[span, :], 1, 1)
         gt_ref[:, n * block : (n + 1) * block] = piece.astype(BF16)
 
     over.wait_recv()
     rights.append(wires.push(all_ref.at[4], all_ref.at[5], dp=right))
     lefts.append(wires.push(all_ref.at[4], all_ref.at[7], dp=left))
-    load.wait()
+    for load in loads:
+        load.wait()
     input_grad(0)
     ends = []
     for n in range(2):
@@ -456,25 +471,31 @@
     for j in range(NZ):
         total = total + jnp.where(j == z, 0.0, zin[j])
     out_ref[...] = total
+    swap_values.wait_recv()
     wires.drain()
 
 
-def tail(rows, early, late, order, weight):
-    width = rows.shape[1]
+def tail(rows, early, late, order, weight, weight_far, grad_values):
+    count, width = rows.shape[0] // 2, 2 * rows.shape[1]
+    hbm = pl.BlockSpec(memory_space=pl.ANY)
     own = early.shape[2] // (2 * NY * NZ)
     slab = (NY, NZ, own, width)
     dma = pltpu.SemaphoreType.DMA
     return pl.pallas_call(
         functools.partial(tail_kernel, order),
         out_shape=(
-            jax.ShapeDtypeStruct((rows.shape[0], weight.shape[0]), BF16),
+            jax.ShapeDtypeStruct((count, weight.shape[0]), BF16),
             jax.ShapeDtypeStruct((own, width), F32),
+            jax.ShapeDtypeStruct((count, HD), BF16),
         ),
-        in_specs=[VMEM, VMEM, VMEM, pl.BlockSpec(memory_space=pl.ANY)],
-        out_specs=(VMEM, VMEM),
+        in_specs=[VMEM, VMEM, VMEM, hbm, hbm, hbm],
+        out_specs=(VMEM, VMEM, hbm),
         scratch_shapes=[
             pltpu.VMEM(weight.shape, BF16),
-            pltpu.VMEM((NDP,) + rows.shape, BF16),
+            pltpu.VMEM(weight.shape, BF16),
+            pltpu.VMEM((count, width), BF16),
+            pltpu.VMEM((count, width // 2), BF16),
+            pltpu.VMEM((NDP, count, width), BF16),
             pltpu.VMEM((NZ, NY, 2, own, width), F32),
             pltpu.VMEM(slab, F32),
             pltpu.VMEM(slab, BF16),
@@ -484,11 +505,11 @@
             pltpu.VMEM((NZ, own, width), F32),
             dma((24,)),
             dma((24,)),
-            dma,
+            dma((2,)),
         ],
         compiler_params=pltpu.CompilerParams(collective_id=3, has_side_effects=True),
         name="tail",
-    )(rows, early, late, weight)
+    )(rows, early, late, weight, weight_far, grad_values)
 
 
 def ahead(x, d):
@@ -533,22 +554,11 @@
 
 
 def product(feat, state):
-    fh, fl = split(feat)
-    sh, sl = split(state)
-    left = jnp.concatenate([fh, fl, fh], axis=0)
-    right = jnp.concatenate([sh, sh, sl], axis=0)
-    return dot(left, right, 0, 0)
-
-
-def pulled(state, rows, fine=None):
-    high, low = split(state)
-    both = dot(jnp.concatenate([high, low], axis=0), rows, 1, 1)
-    both = both[:EP] + both[EP:]
-    return both if fine is None else both + dot(high, fine, 1, 1)
+    return dot(jnp.concatenate(split(feat), axis=0), jnp.concatenate([state, state], axis=0), 0, 0)
 
 
 def causal():
-    shape = (128, 128)
+    shape = (256, 256)
     return lax.broadcasted_iota(jnp.int32, shape, 0) >= lax.broadcasted_iota(jnp.int32, shape, 1)
 
 
@@ -561,27 +571,27 @@
 
 
 def slot(h):
-    return h // 8, h % 2, (h // 2) % 4
+    return h % 2, h // 2
 
 
 def project_kernel(tok_ref, w_ref, v_ref, proj_ref, state_ref):
     proj = dot(tok_ref[...], w_ref[...], 1, 0)
     proj_ref[...] = proj.T
     for h in range(H):
-        keys = proj_ref[256 + h * F : 256 + (h + 1) * F, :]
+        keys = proj_ref[HF + h * F : HF + (h + 1) * F, :]
         high, low = split(features(keys, False))
         v = v_ref[:, head_cols(h)]
         state = dot(
             jnp.concatenate([high, low], axis=1), jnp.concatenate([v, v], axis=0), 1, 0
         )
-        state_ref[slot(h)] = state
+        state_ref[slot(h)] = state.astype(BF16)
 
 
 def forward_kernel(proj_ref, v_ref, g_ref, prefix_ref, att_ref, gn_ref, state_ref):
     mask = causal()
     for h in range(H):
         q = proj_ref[head_rows(h), :]
-        k = proj_ref[256 + h * F : 256 + (h + 1) * F, :]
+        k = proj_ref[HF + h * F : HF + (h + 1) * F, :]
         a = scores(q, k)
         kernel = jnp.where(mask, 1.0 + a + 0.5 * a * a, 0.0)
         feat = features(q, False)
@@ -603,14 +613,14 @@
             jnp.concatenate([gh, gh, gl], axis=0),
             1,
             0,
-        )
+        ).astype(BF16)
 
 
 def backward_kernel(proj_ref, v_ref, gn_ref, prefix_ref, suffix_ref, gv_ref, rows_ref, acc):
     mask = causal()
     for h in range(H):
         q = proj_ref[head_rows(h), :]
-        k = proj_ref[256 + h * F : 256 + (h + 1) * F, :]
+        k = proj_ref[HF + h * F : HF + (h + 1) * F, :]
         v = v_ref[:, head_cols(h)]
         gh, gl = split(gn_ref[:, head_cols(h)])
         a = scores(q, k)
@@ -627,8 +637,8 @@
         dk = dk[:F] + dk[F:] + dot(qh, sl, 1, 0)
         pre = prefix_ref[slot(h)]
         suf = suffix_ref[slot(h)]
-        acc[head_rows(h), :] = dq + pull_features(q, pulled(pre, gh, gl))
-        acc[256 + h * F : 256 + (h + 1) * F, :] = dk + pull_features(k, pulled(suf, v))
+        acc[head_rows(h), :] = dq + pull_features(q, dot(jnp.concatenate([pre, pre], axis=1), jnp.concatenate([gh, gl], axis=1), 1, 1))
+        acc[HF + h * F : HF + (h + 1) * F, :] = dk + pull_features(k, dot(suf, v, 1, 1))
         gv = dot(
             jnp.concatenate([mh, ml, mh], axis=0), jnp.concatenate([gh, gh, gl], axis=0), 0, 0
         )
@@ -652,33 +662,47 @@
     return jax.ShapeDtypeStruct(shape, dtype)
 
 
+def joined(c, mine, far):
+    pair = jnp.where(c == 0, jnp.concatenate([mine, far], axis=1), jnp.concatenate([far, mine], axis=1))
+    return pair[None]
+
+
 def local(tokens, proj_weight, values, grad_out):
-    tok, val, up = tokens[0], values[0], grad_out[0]
-    rows = tok.shape[0]
-    packed = shaped((2, NC, NY, RC, DH), F32)
-    weight = gather_weight(proj_weight)
+    c = lax.axis_index("ctx") % 2
+    tok = tokens[0]
+    count = tok.shape[0]
+    packed = shaped((NC, NY, RC, DH), BF16)
+    weight, tok2, val, up = gather(proj_weight, tok, values[0], grad_out[0])
     proj, state = plain(
-        project_kernel, (shaped((2 * H * F, rows), F32), packed), (tok, weight, val), name="project"
+        project_kernel, (shaped((2 * HF, 2 * count), F32), packed), (tok2, weight, val), name="project"
     )
     early = ((0, 0), (0, 1), (0, 3), (1, 0), (1, 2))
     late = ((0, 2), (1, 1), (1, 3))
-    prefix, cols_early = scan(state, False, 1, tok, early)
+    prefix, cols_early, weight_far = scan(
+        state, False, 1, tok, early, weight, shaped(weight.shape, BF16), whole
+    )
     attended, grad_num, carried = plain(
         forward_kernel,
         (shaped(val.shape, BF16), shaped(val.shape, F32), packed),
         (proj, val, up, prefix),
         name="forward",
     )
-    suffix, cols_late = scan(carried, True, 2, tok, late)
+    suffix, cols_late, attended_far = scan(
+        carried, True, 2, tok, late, attended, shaped((count, HD), BF16), their_rows
+    )
     grad_values, grad_rows = plain(
         backward_kernel,
-        (shaped(val.shape, BF16), shaped((rows, 2 * H * F), BF16)),
+        (shaped(val.shape, BF16), shaped((2 * count, 2 * HF), BF16)),
         (proj, val, grad_num, prefix, suffix),
-        scratch=[pltpu.VMEM((2 * H * F, rows), F32)],
+        scratch=[pltpu.VMEM((2 * HF, 2 * count), F32)],
         name="backward",
     )
-    grad_tokens, grad_proj = tail(grad_rows, cols_early, cols_late, early + late, weight)
-    return (attended[None], grad_tokens[None], grad_values[None], grad_proj)
+    grad_tokens, grad_proj, values_far = tail(
+        grad_rows, cols_early, cols_late, early + late, weight, weight_far, grad_values
+    )
+    attended = joined(c, lax.dynamic_slice_in_dim(attended, c * count, count), attended_far)
+    grad_values = joined(c, lax.dynamic_slice_in_dim(grad_values, c * count, count), values_far)
+    return (attended, grad_tokens[None], grad_values, grad_proj)
 
 
 def solution(mesh):

time: 157 us -> 146 us (0.930)
  Pallas kernels: 153 us -> 140 us
  other arithmetic: 0 us -> 2.95 us
    pallas_call x3, Pallas kernels: 95.4 us -> 80.2 us  [the longest x2 55.8 us: scan(): pl.pallas_call(functools.partial(scan_kernel, later, slots, across_chip),...]
    pallas_call x1, Pallas kernels: 33 us -> 40.6 us  [tail(): pl.pallas_call(functools.partial(tail_kernel, order), out_shape=(jax.Shap...]
    pallas_call x3, Pallas kernels: 24.8 us -> 19.1 us  [plain(): pl.pallas_call(kernel, out_shape=outs, in_specs=[VMEM] * len(args), out_s...]
    select_n x0 -> x2, other arithmetic: none -> 2.95 us  [joined(): jnp.where(c == 0, jnp.concatenate([mine, far], axis=1), jnp.concatenate([...]
where the time goes in v4:
time: 146 us; the launch traced here: 145 us
  Pallas kernels  140 us (96%)
  other arithmetic  2.95 us (2%)
  local copies, waits for them, and re-layouts  1.65 us (1%)
    pallas_call x2, Pallas kernels, scan(): pl.pallas_call(functools.partial(scan_kernel, later, slots, across_chip),...  55.8 us
    pallas_call x1, Pallas kernels, tail(): pl.pallas_call(functools.partial(tail_kernel, order), out_shape=(jax.Shap...  40.6 us
    pallas_call x1, Pallas kernels, gather(): pl.pallas_call(gather_kernel, out_shape=(jax.ShapeDtypeStruct((NDP * w.sh...  24.4 us
    pallas_call x3, Pallas kernels, plain(): pl.pallas_call(kernel, out_shape=outs, in_specs=[VMEM] * len(args), out_s...  19.1 us
    select_n x2, other arithmetic, joined(): jnp.where(c == 0, jnp.concatenate([mine, far], axis=1), jnp.concatenate([...  2.95 us

profile of v4, /device:TPU:1, one launch (start us, length us, event | category | flops | bytes accessed | tf_op | source)
XLA Modules:
  0.0 145.3 jit_solution(18433483394969436827)
XLA Ops:
  0.6 24.4 %gather.1 = (bf16[4096,256]{1,0:T(8,128)(2,1)}, bf16[256,4096]{1,0:T(8,128)(2,1)}, bf16[256,1024]{1,0:T(8,128)(2,1)}, bf16[256,1024]{1,0:T(8,128)(2,1)}) custom-call(bf16[512,512]{1,0:T(8,128)(2,1)} %w_ref.1, bf16[128,4096]{1,0:T(8,128)(2,1)} %bitcast.10, bf16[128,2048]{1,0:T(8,128)(2,1)} %bitcast.14, bf16[128,2048]{1,0:T(8,128)(2,1)} %bitcast.15), custom_call_target="tpu_custom_call" | custom-call | tf_op jit(solution)/shard_map/gather/pallas_call | solution.py:193
  25.0 4.9 %project.1 = (f32[256,256]{1,0:T(8,128)}, bf16[2,4,160,128]{3,2,1,0:T(8,128)(2,1)}) custom-call(bf16[256,4096]{1,0:T(8,128)(2,1)} %get-tuple-element.24.tok_ref, bf16[4096,256]{1,0:T(8,128)(2,1)} %get-tuple-element.25.w_ref.side_ref.w_hbm, bf16[256,1024]{1,0:T(8,128)(2,1)} %get-tuple-element.26.v_ref), custom_call_target="tpu_custom_call" | custom-call | tf_op jit(solution)/shard_map/project/pallas_call | solution.py:651
  29.9 27.8 %scan_earlier.1 = (bf16[2,4,160,128]{3,2,1,0:T(8,128)(2,1)}, bf16[5,128,512]{2,1,0:T(8,128)(2,1)}, bf16[4096,256]{1,0:T(8,128)(2,1)}) custom-call(bf16[2,4,160,128]{3,2,1,0:T(8,128)(2,1)} %get-tuple-element.29.s_ref, bf16[128,4096]{1,0:T(8,128)(2,1)} %bitcast.11, bf16[4096,256]{1,0:T(8,128)(2,1)} %get-tuple-element.25.w_ref.side_ref.w_hbm), custom_call_target="tpu_custom_call" | custom-call | tf_op jit(solution)/shard_map/scan_earlier/pallas_call | solution.py:319
  57.8 7.1 %forward.1 = (bf16[256,1024]{1,0:T(8,128)(2,1)}, f32[256,1024]{1,0:T(8,128)}, bf16[2,4,160,128]{3,2,1,0:T(8,128)(2,1)}) custom-call(f32[256,256]{1,0:T(8,128)} %get-tuple-element.27.proj_ref, bf16[256,1024]{1,0:T(8,128)(2,1)} %get-tuple-element.26.v_ref, bf16[256,1024]{1,0:T(8,128)(2,1)} %get-tuple-element.28.g_ref, ...), custom_call_target="tpu_custom_call" | custom-call | tf_op jit(solution)/shard_map/forward/pallas_call | solution.py:651
  64.9 28.0 %scan_later.1 = (bf16[2,4,160,128]{3,2,1,0:T(8,128)(2,1)}, bf16[3,128,512]{2,1,0:T(8,128)(2,1)}, bf16[128,1024]{1,0:T(8,128)(2,1)}) custom-call(bf16[2,4,160,128]{3,2,1,0:T(8,128)(2,1)} %get-tuple-element.32.s_ref, bf16[128,4096]{1,0:T(8,128)(2,1)} %bitcast.12, bf16[256,1024]{1,0:T(8,128)(2,1)} %get-tuple-element.31.side_ref), custom_call_target="tpu_custom_call" | custom-call | tf_op jit(solution)/shard_map/scan_later/pallas_call | solution.py:319
  92.8 7.1 %backward.1 = (bf16[256,1024]{1,0:T(8,128)(2,1)}, bf16[256,256]{1,0:T(8,128)(2,1)}) custom-call(f32[256,256]{1,0:T(8,128)} %get-tuple-element.27.proj_ref, bf16[256,1024]{1,0:T(8,128)(2,1)} %get-tuple-element.26.v_ref, f32[256,1024]{1,0:T(8,128)} %get-tuple-element.34.gn_ref, bf16[2,4,160,128]{3,2,1,0:T(8,128)(2,1)} %get-tuple-element.30.prefix_ref, ...), custom_call_target="tpu_custom_call" | custom-call | tf_op jit(solution)/shard_map/backward/pallas_call | solution.py:651
  99.9 0.0 copy-start
  99.9 0.0 copy-start.1
  99.9 40.6 %tail.1 = (bf16[128,4096]{1,0:T(8,128)(2,1)}, f32[16,512]{1,0:T(8,128)}, bf16[128,1024]{1,0:T(8,128)(2,1)}) custom-call(bf16[256,256]{1,0:T(8,128)(2,1)} %get-tuple-element.36.rows_ref, bf16[5,128,512]{2,1,0:T(8,128)(2,1)} %get-tuple-element.37.early_ref, bf16[3,128,512]{2,1,0:T(8,128)(2,1)} %get-tuple-element.38.late_ref, ...), custom_call_target="tpu_custom_call" | custom-call | tf_op jit(solution)/shard_map/tail/pallas_call | solution.py:484
  140.6 0.0 copy-start.3
  140.6 0.0 copy-start.2
  140.6 0.0 copy-done
  140.6 0.0 copy-done.1
  140.7 0.0 copy-start.4
  140.7 2.0 %maximum_select_fusion.1 = bf16[1,128,2048]{2,1,0:T(8,128)(2,1)} fusion(bf16[1,128,1024]{2,1,0:T(8,128)(2,1)} %bitcast.17, bf16[1,128,1024]{2,1,0:T(8,128)(2,1)S(1)} %get-tuple-element.44, pred[]{:T(512)S(6)} %eq.6), kind=kLoop, calls=%fused_computation.1 | loop fusion | flops 2359296 | bytes 1048577 | tf_op jit(solution)/shard_map/jit(_where)/select_n | solution.py:666
  142.7 0.0 copy-done.3
  142.7 0.9 maximum_select_fusion
  143.7 0.0 copy-done.2
  143.7 1.0 copy.10
  144.6 0.0 copy-done.4
  144.6 0.6 copy.11
  (1 shorter events, 0.0 us)
Async XLA Ops:
  99.9 40.7 %copy-start = (bf16[256,1024]{1,0:T(8,128)(2,1)S(1)}, bf16[256,1024]{1,0:T(8,128)(2,1)}, u32[]{:S(2)}) copy-start(bf16[256,1024]{1,0:T(8,128)(2,1)} %get-tuple-element.40.gv_ref) | copy-start | bytes 1572868
  99.9 40.7 %copy-start.1 = (bf16[256,1024]{1,0:T(8,128)(2,1)S(1)}, bf16[256,1024]{1,0:T(8,128)(2,1)}, u32[]{:S(2)}) copy-start(bf16[256,1024]{1,0:T(8,128)(2,1)} %get-tuple-element.31.side_ref) | copy-start | bytes 1572868
  140.6 2.2 %copy-start.3 = (bf16[128,1024]{1,0:T(8,128)(2,1)S(1)}, bf16[128,1024]{1,0:T(8,128)(2,1)}, u32[]{:S(2)}) copy-start(bf16[128,1024]{1,0:T(8,128)(2,1)} %get-tuple-element.33) | copy-start | bytes 786436
  140.6 3.1 %copy-start.2 = (bf16[128,4096]{1,0:T(8,128)(2,1)S(1)}, bf16[128,4096]{1,0:T(8,128)(2,1)}, u32[]{:S(2)}) copy-start(bf16[128,4096]{1,0:T(8,128)(2,1)} %get-tuple-element.41) | copy-start | bytes 3145732
  140.7 3.9 %copy-start.4 = (f32[16,512]{1,0:T(8,128)S(1)}, f32[16,512]{1,0:T(8,128)}, u32[]{:S(2)}) copy-start(f32[16,512]{1,0:T(8,128)} %get-tuple-element.53) | copy-start | bytes 98308

commit v5 on v0

v5 whole, which is shorter than its diff:
```python
import jax
import jax.numpy as jnp
from jax import lax
from jax.experimental import pallas as pl
from jax.experimental.pallas import tpu as pltpu
from jax.sharding import PartitionSpec as P

H = 8
F = 16
DH = 128
EP = 160
QUAD = 1.0 / 32.0
EPSILON = 1e-05
MESH = pl.DeviceIdType.MESH
F32 = jnp.float32
BF16 = jnp.bfloat16
VMEM = pl.BlockSpec(memory_space=pltpu.VMEM)
NY = 4
NZ = 4
NDP = 8
RC = 2 * EP
HF = H * F
HD = H * DH


def dot(lhs, rhs, left, right):
    return lax.dot_general(lhs, rhs, (((left,), (right,)), ((), ())), preferred_element_type=F32)


def remote(src, dst, send, recv, **where):
    return pltpu.make_async_remote_copy(
        src_ref=src, dst_ref=dst, send_sem=send, recv_sem=recv, device_id=where, device_id_type=MESH
    )


def greet(peers):
    barrier = pltpu.get_barrier_semaphore()
    for where in peers:
        pl.semaphore_signal(barrier, inc=1, device_id=where, device_id_type=MESH)
    pl.semaphore_wait(barrier, len(peers))


def across(dp, dz, dx):
    return (dp // 4 + dz) % 2 * 4 + (dp % 4 + dx + 4) % 4


def place():
    ctx = lax.axis_index("ctx")
    return ctx // 8, (ctx // 2) % 4, ctx % 2


def at(z, y, c):
    return z * 8 + y * 2 + c


class Wires:
    def __init__(self, send, recv):
        self.send, self.recv, self.copies = send, recv, []

    def push(self, src, dst, **where):
        n = len(self.copies)
        copy = remote(src, dst, self.send.at[n], self.recv.at[n], **where)
        copy.start()
        self.copies.append(copy)
        return copy

    def drain(self):
        for copy in self.copies:
            copy.wait_send()


def ahead(x, d):
    return pltpu.roll(x, F - d, 0)


def behind(x, d):
    return pltpu.roll(x, d, 0)


def features(x, weighted):
    quad, linear = (QUAD, 0.25) if weighted else (1.0, 1.0)
    twice = 2.0 * quad if weighted else 1.0
    parts = [x * x * quad] + [x * ahead(x, d) * twice for d in range(1, 8)]
    parts += [x[:8] * x[8:] * twice, x * linear]
    row = lax.broadcasted_iota(jnp.int32, (8, x.shape[1]), 0)
    parts.append(jnp.where(row == 0, 1.0, 0.0))
    return jnp.concatenate(parts, axis=0)


def pull_features(x, cot):
    out = 2.0 * QUAD * cot[:F] * x
    for d in range(1, 8):
        part = 2.0 * QUAD * cot[F * d : F * (d + 1)]
        out = out + part * ahead(x, d) + behind(part * x, d)
    half = 2.0 * QUAD * cot[128:136]
    out = out + jnp.concatenate([half * x[8:], half * x[:8]], axis=0)
    return out + 0.25 * cot[136:152]


def split(x):
    high = x.astype(BF16)
    return high, (x - high.astype(F32)).astype(BF16)


def scores(q, k):
    qh, ql = split(q)
    kh, kl = split(k)
    left = jnp.concatenate([qh, qh, ql, ql], axis=0)
    right = jnp.concatenate([kh, kl, kh, kl], axis=0)
    return dot(left, right, 0, 0) * 0.25


def product(feat, state):
    return dot(jnp.concatenate(split(feat), axis=0), jnp.concatenate([state, state], axis=0), 0, 0)


def causal():
    shape = (256, 256)
    return lax.broadcasted_iota(jnp.int32, shape, 0) >= lax.broadcasted_iota(jnp.int32, shape, 1)


def head_cols(h):
    return slice(h * DH, (h + 1) * DH)


def head_rows(h):
    return slice(h * F, (h + 1) * F)


def rows_of(h):
    return h // 2, slice(h % 2 * EP, (h % 2 + 1) * EP)


def aligned(start, size, step=None):
    return pl.ds(pl.multiple_of(start, step or size), size)


def layer_kernel(
    w_ref, tok_ref, v_ref, g_ref, att_ref, gt_ref, gv_ref, gp_ref,
    wc, w_far, tok2, v2, g2, proj, projt, state, yin, tz, zin, yout, pre, prefix, suffix,
    carried, yin_b, zin_b, yout_b, tz_b, work, gn, att2, gv2, acc, rows2, r_far, r_all, cols,
    all_ref, grad, sib, pair, yred, ysum, zred, send, recv, local_sem,
):
    dp = lax.axis_index("dp")
    z, y, c = place()
    partner = at(z, y, 1 - c)
    up, down = at(z, (y + 1) % NY, c), at(z, (y + 3) % NY, c)
    right, left, other = across(dp, 0, 1), across(dp, 0, 3), across(dp, 1, 0)
    count = tok_ref.shape[0]
    rows = w_ref.shape[0]
    ours = aligned(c * count, count)
    theirs = aligned((1 - c) * count, count)
    own_half = aligned(c * HD, HD)
    their_half = aligned((1 - c) * HD, HD)
    wires = Wires(send, recv)
    locals_ = []

    def copy_here(src, dst):
        copy = pltpu.make_async_copy(src, dst, local_sem.at[len(locals_)])
        copy.start()
        locals_.append(copy)
        return copy

    own_rows = aligned(dp * rows, rows)
    for n in range(2):
        wc[own_rows, n * HF : (n + 1) * HF] = w_ref[:, aligned(n * 2 * HF + c * HF, HF)]
    greet(
        [{"ctx": partner}]
        + [{"ctx": at(z, (y + d) % NY, c)} for d in range(1, NY)]
        + [{"ctx": at((z + d) % NZ, y, c)} for d in range(1, NZ)]
        + [{"dp": across(dp, n // 4, n % 4)} for n in range(1, NDP)]
    )

    wide = rows // 2
    thin = wide // NY
    base_a, base_b = 0, wide

    def part(owner, start, size):
        return wc.at[aligned(owner * rows + start, size, thin // 2)]

    def own_sends(start, size):
        piece = part(dp, start, size)
        return [wires.push(piece, piece, dp=to) for to in (other, right, left)]

    def pass_on(owner, start, size):
        piece = part(owner, start, size)
        return wires.push(piece, piece, dp=right), wires.push(piece, piece, dp=left)

    def relay(near, far, start, size):
        one = part(near, start, size // 2)
        two = part(far, start + size // 2, size // 2)
        return wires.push(one, one, dp=right), wires.push(two, two, dp=left)

    def over_y(owner):
        piece = part(owner, base_b + y * thin, thin)
        return wires.push(piece, piece, ctx=up), wires.push(piece, piece, ctx=down)

    mine_b = base_b + y * thin
    b_over, b_right, b_left = own_sends(mine_b, thin)
    a_over, a_right, a_left = own_sends(base_a, wide)
    from_partner = [
        wires.push(tok_ref, tok2.at[ours], ctx=partner),
        wires.push(v_ref.at[:, their_half], v2.at[ours], ctx=partner),
        wires.push(g_ref.at[:, their_half], g2.at[ours], ctx=partner),
    ]
    here = [
        copy_here(tok_ref, tok2.at[ours]),
        copy_here(v_ref.at[:, own_half], v2.at[ours]),
        copy_here(g_ref.at[:, own_half], g2.at[ours]),
    ]
    owners = [other, left, right] + [across(dp, dz, dx) for dz, dx in ((1, 3), (1, 1), (0, 2), (1, 2))]
    chain_y = []
    b_over.wait_recv()
    b_right2, b_left2 = pass_on(other, mine_b, thin)
    chain_y.append(over_y(owners[0]))
    b_right.wait_recv()
    b_left.wait_recv()
    b_ends = relay(left, right, mine_b, thin)
    chain_y.append(over_y(owners[1]))
    chain_y.append(over_y(owners[2]))
    a_over.wait_recv()
    a_right2, a_left2 = pass_on(other, base_a, wide)
    b_right2.wait_recv()
    b_left2.wait_recv()
    b_ends2 = relay(owners[3], owners[4], mine_b, thin)
    chain_y.append(over_y(owners[3]))
    chain_y.append(over_y(owners[4]))
    a_right.wait_recv()
    a_left.wait_recv()
    a_ends = relay(left, right, base_a, wide)
    for copy in b_ends:
        copy.wait_recv()
    chain_y.append(over_y(owners[5]))
    for copy in b_ends2:
        copy.wait_recv()
    chain_y.append(over_y(owners[6]))
    ends_y = []
    below = base_b + (y + 3) % NY * thin
    above = base_b + (y + 1) % NY * thin + thin // 2

    def relay_y(n):
        chain_y[n][0].wait_recv()
        one = part(owners[n], below, thin // 2)
        ends_y.append([wires.push(one, one, ctx=up)])
        chain_y[n][1].wait_recv()
        two = part(owners[n], above, thin // 2)
        ends_y[-1].append(wires.push(two, two, ctx=down))

    for n in range(3):
        relay_y(n)
    a_right2.wait_recv()
    a_left2.wait_recv()
    a_ends2 = relay(owners[3], owners[4], base_a, wide)
    for n in range(3, 7):
        relay_y(n)

    def project(owner):
        return dot(
            tok2[:, aligned(owner * rows, rows)], wc[aligned(owner * rows, rows), :], 1, 0
        )

    for copy in from_partner:
        copy.wait_recv()
    for copy in here:
        copy.wait()
    proj[...] = project(dp)
    for n in range(7):
        for copy in ends_y[n]:
            copy.wait_recv()
        if n == 5:
            for copy in a_ends:
                copy.wait_recv()
        if n == 6:
            for copy in a_ends2:
                copy.wait_recv()
        proj[...] += project(owners[n])
    far_weight = wires.push(wc, w_far, ctx=partner)
    width = cols.shape[2]
    token_copies = []

    def send_tokens(slots):
        for n in slots:
            peer = across(dp, n // 4, n % 4)
            token_copies.append(
                wires.push(tok_ref.at[:, aligned(peer * width, width)], cols.at[n], dp=peer)
            )

    projt[...] = proj[...].T

    def query(h):
        return projt[h * F : (h + 1) * F, :]

    def key(h):
        return projt[HF + h * F : HF + (h + 1) * F, :]

    def head(h):
        return slice(h * DH, (h + 1) * DH)

    for h in range(H):
        high, low = split(features(key(h), False))
        v = v2[:, head(h)]
        new = dot(jnp.concatenate([high, low], axis=1), jnp.concatenate([v, v], axis=0), 1, 0)
        j, at_rows = rows_of(h)
        state[j, at_rows, :] = new.astype(BF16)

    def scan(later, src, land, total_ref, planes, out, result, fill_y, fill_z):
        copies = []
        for d in (2, 1, 3):
            to = (y + d) % NY
            copies.append(wires.push(src.at[to], land.at[y], ctx=at(z, to, c)))
        fill_y()
        for copy in copies:
            copy.wait_recv()
        total = jnp.zeros(pre.shape[1:], F32)
        for j in list(range(NY))[::-1] if later else range(NY):
            pre[j] = total
            total = total + jnp.where(j == y, src[j], land[j]).astype(F32)
        total_ref[...] = total.astype(BF16)
        copies = []
        for d in (2, 1, 3):
            to = (z + d) % NZ
            copies.append(wires.push(total_ref, planes.at[z], ctx=at(to, y, c)))
        fill_z()
        for copy in copies:
            copy.wait_recv()
        base = jnp.zeros(pre.shape[1:], F32)
        for j in range(NZ):
            wanted = (j > z) if later else (j < z)
            base = base + jnp.where(wanted, planes[j].astype(F32), 0.0)
        for j in range(NY):
            out[j] = (base + pre[j]).astype(BF16)
        copies = []
        for d in (2, 1, 3):
            to = (y + d) % NY
            copies.append(wires.push(out.at[to], result.at[y], ctx=at(z, to, c)))
        result[y] = out[y]
        for copy in copies:
            copy.wait_recv()

    mask = causal()

    def local_numerator(h):
        a = scores(query(h), key(h))
        kernel = jnp.where(mask, 1.0 + a + 0.5 * a * a, 0.0)
        v = v2[:, head(h)]
        work[:, head(h)] = dot(
            jnp.concatenate(split(kernel), axis=1), jnp.concatenate([v, v], axis=0), 1, 0
        )

    def first_fill():
        send_tokens((1, 2, 3))
        for h in range(3):
            local_numerator(h)

    def second_fill():
        send_tokens((4, 5, 6, 7))
        for h in range(3, H):
            local_numerator(h)

    scan(False, state, yin, tz, zin, yout, prefix, first_fill, second_fill)

    for h in range(H):
        j, at_rows = rows_of(h)
        q = query(h)
        numerator = work[:, head(h)] + product(features(q, True), prefix[j, at_rows, :])
        inv = lax.rsqrt(jnp.mean(numerator * numerator, axis=1, keepdims=True) + EPSILON)
        normed = numerator * inv
        att2[:, head(h)] = normed.astype(BF16)
        g = g2[:, head(h)].astype(F32)
        grad_num = inv * (g - normed * jnp.mean(normed * g, axis=1, keepdims=True))
        gn[:, head(h)] = grad_num
        high, low = split(features(q, False))
        gh, gl = split(grad_num)
        new = dot(
            jnp.concatenate([high, low, high], axis=1), jnp.concatenate([gh, gh, gl], axis=0), 1, 0
        )
        carried[j, at_rows, :] = new.astype(BF16)

    def local_grads(h):
        q, k = query(h), key(h)
        v = v2[:, head(h)]
        gh, gl = split(gn[:, head(h)])
        a = scores(q, k)
        mh, ml = split(jnp.where(mask, 1.0 + a + 0.5 * a * a, 0.0))
        mixing = dot(
            jnp.concatenate([gh, gl], axis=1), jnp.concatenate([v, v], axis=1), 1, 1
        )
        sh, sl = split(jnp.where(mask, mixing * (1.0 + a) * 0.25, 0.0))
        qh, ql = split(q)
        kh, kl = split(k)
        dq = dot(jnp.concatenate([kh, kl], axis=0), sh, 1, 1)
        dq = dq[:F] + dq[F:] + dot(kh, sl, 1, 1)
        dk = dot(jnp.concatenate([qh, ql], axis=0), sh, 1, 0)
        dk = dk[:F] + dk[F:] + dot(qh, sl, 1, 0)
        j, at_rows = rows_of(h)
        before = prefix[j, at_rows, :]
        pulled = dot(
            jnp.concatenate([before, before], axis=1), jnp.concatenate([gh, gl], axis=1), 1, 1
        )
        acc[h * F : (h + 1) * F, :] = dq + pull_features(q, pulled)
        acc[HF + h * F : HF + (h + 1) * F, :] = dk
        work[:, head(h)] = dot(
            jnp.concatenate([mh, ml, mh], axis=0), jnp.concatenate([gh, gh, gl], axis=0), 0, 0
        )

    outs = []

    def third_fill():
        outs.append(wires.push(att2.at[theirs], att_ref.at[:, own_half], ctx=partner))
        copy_here(att2.at[ours], att_ref.at[:, own_half])
        for h in range(3):
            local_grads(h)

    def fourth_fill():
        for h in range(3, H):
            local_grads(h)

    scan(True, carried, yin_b, tz_b, zin_b, yout_b, suffix, third_fill, fourth_fill)

    for h in range(H):
        j, at_rows = rows_of(h)
        after = suffix[j, at_rows, :]
        k = key(h)
        span = slice(HF + h * F, HF + (h + 1) * F)
        acc[span, :] = acc[span, :] + pull_features(k, dot(after, v2[:, head(h)], 1, 1))
    rows2[...] = acc[...].T.astype(BF16)

    swap = wires.push(rows2.at[theirs], r_far, ctx=partner)
    for h in range(H):
        j, at_rows = rows_of(h)
        total = work[:, head(h)] + product(features(key(h), True), suffix[j, at_rows, :])
        gv2[:, head(h)] = total.astype(BF16)
    for n in range(2):
        r_all[:, aligned(n * 2 * HF + c * HF, HF)] = rows2[ours, n * HF : (n + 1) * HF]
    swap.wait_recv()
    for n in range(2):
        r_all[:, aligned(n * 2 * HF + (1 - c) * HF, HF)] = r_far[:, n * HF : (n + 1) * HF]
    half = count // 2
    low_rows, high_rows = pl.ds(0, half), pl.ds(half, half)
    over = wires.push(r_all, all_ref.at[4], dp=other)
    rights = [wires.push(r_all, all_ref.at[1], dp=right)]
    lefts = [wires.push(r_all, all_ref.at[3], dp=left)]
    outs.append(wires.push(gv2.at[theirs], gv_ref.at[:, own_half], ctx=partner))
    copy_here(gv2.at[ours], gv_ref.at[:, own_half])
    far_weight.wait_recv()
    for copy in token_copies:
        copy.wait_recv()

    def tokens_of(n):
        if n == 0:
            return tok2[ours, aligned(dp * width, width)]
        return cols[n]

    def product_of(slots):
        left_rows = jnp.concatenate([tokens_of(n) for n in slots], axis=0)
        right_rows = jnp.concatenate([r_all[...] if n == 0 else all_ref[n] for n in slots], axis=0)
        return dot(left_rows, right_rows, 0, 0).reshape(grad.shape)

    block = wc.shape[0] // 4

    def input_grad(n):
        span = slice(n * block, (n + 1) * block)
        piece = dot(rows2[ours, :], wc[span, :], 1, 1)
        piece += dot(r_far[...], w_far[span, :], 1, 1)
        gt_ref[:, span] = piece.astype(BF16)

    over.wait_recv()
    rights.append(wires.push(all_ref.at[4], all_ref.at[5], dp=right))
    lefts.append(wires.push(all_ref.at[4], all_ref.at[7], dp=left))
    input_grad(0)
    ends = []
    for n in range(2):
        rights[n].wait_recv()
        ends.append(
            wires.push(all_ref.at[4 * n + 1, low_rows], all_ref.at[4 * n + 2, low_rows], dp=right)
        )
        lefts[n].wait_recv()
        ends.append(
            wires.push(all_ref.at[4 * n + 3, high_rows], all_ref.at[4 * n + 2, high_rows], dp=left)
        )
        input_grad(2 * n + 1)
        if n == 0:
            grad[...] = product_of((0, 1, 3, 4))
            input_grad(2)
    for copy in ends:
        copy.wait_recv()
    grad[...] += product_of((2, 5, 6, 7))

    copies_c = {}
    for d in (2, 1, 3, 0):
        to = (y + d) % NY
        copies_c[d] = wires.push(grad.at[:, to, 1 - c], sib.at[to], ctx=partner)
    near = []
    for d in (2, 1, 3, 0):
        to = (y + d) % NY
        copies_c[d].wait_recv()
        both = grad[:, to, c] + sib[to]
        if d == 0:
            ysum[...] = both
        else:
            pair[to] = both.astype(BF16)
            near.append(wires.push(pair.at[to], yred.at[y], ctx=at(z, to, c)))
    for copy in near:
        copy.wait_recv()
    for j in range(NY):
        ysum[...] += jnp.where(j == y, 0.0, yred[j].astype(F32))
    copies_z = []
    for d in (2, 1, 3):
        to = (z + d) % NZ
        copies_z.append(wires.push(ysum.at[to], zred.at[z], ctx=at(to, y, c)))
    for copy in copies_z:
        copy.wait_recv()
    total = ysum[z]
    for j in range(NZ):
        total = total + jnp.where(j == z, 0.0, zred[j])
    gp_ref[...] = total
    for copy in outs:
        copy.wait_recv()
    for copy in locals_[3:]:
        copy.wait()
    wires.drain()


def local(tokens, proj_weight, values, grad_out):
    tok, val, up = tokens[0], values[0], grad_out[0]
    count, model = tok.shape
    shard, width = proj_weight.shape
    both = 2 * count
    own = shard // (2 * NY * NZ)
    parts = (NY, RC, DH)
    dma = pltpu.SemaphoreType.DMA
    hbm = pl.BlockSpec(memory_space=pl.ANY)

    def half(*shape):
        return pltpu.VMEM(shape, BF16)

    def full(*shape):
        return pltpu.VMEM(shape, F32)

    attended, grad_tokens, grad_values, grad_proj = pl.pallas_call(
        layer_kernel,
        out_shape=(
            jax.ShapeDtypeStruct(val.shape, BF16),
            jax.ShapeDtypeStruct(tok.shape, BF16),
            jax.ShapeDtypeStruct(val.shape, BF16),
            jax.ShapeDtypeStruct((own, width), F32),
        ),
        in_specs=[VMEM, hbm, hbm, hbm],
        out_specs=(VMEM,) * 4,
        scratch_shapes=[
            half(model, 2 * HF),
            half(model, 2 * HF),
            half(both, model),
            half(both, HD),
            half(both, HD),
            full(both, 2 * HF),
            full(2 * HF, both),
            half(*parts),
            half(*parts),
            half(RC, DH),
            half(NZ, RC, DH),
            half(*parts),
            full(*parts),
            half(*parts),
            half(*parts),
            half(*parts),
            half(*parts),
            half(NZ, RC, DH),
            half(*parts),
            half(RC, DH),
            full(both, HD),
            full(both, HD),
            half(both, HD),
            half(both, HD),
            full(2 * HF, both),
            half(both, 2 * HF),
            half(count, 2 * HF),
            half(count, width),
            half(NDP, count, shard),
            half(NDP, count, width),
            full(NZ, NY, 2, own, width),
            full(NY, NZ, own, width),
            half(NY, NZ, own, width),
            half(NY, NZ, own, width),
            full(NZ, own, width),
            full(NZ, own, width),
            dma((112,)),
            dma((112,)),
            dma((5,)),
        ],
        compiler_params=pltpu.CompilerParams(collective_id=0, has_side_effects=True),
        name="layer",
    )(proj_weight, tok, val, up)
    return (attended[None], grad_tokens[None], grad_values[None], grad_proj)


def solution(mesh):
    return jax.shard_map(
        local,
        mesh=mesh,
        in_specs=(P("dp", "ctx", None), P("dp", None), P("dp", "ctx", None), P("dp", "ctx", None)),
        out_specs=(
            P("dp", "ctx", None),
            P("dp", "ctx", None),
            P("dp", "ctx", None),
            P(("dp", "ctx"), None),
        ),
        check_vma=False,
    )
```

time: 2050 us -> 106 us (0.05)
  the two profiles are of different devices: /device:TPU:32 before, /device:TPU:1 now
where the time goes in v5:
time: 106 us
  Pallas kernels  100 us (94%)
  local copies, waits for them, and re-layouts  4.78 us (5%)
    pallas_call x1, Pallas kernels, local(): pl.pallas_call(layer_kernel, out_shape=(jax.ShapeDtypeStruct(val.shape, B...  100 us
    unnamed x10, local copies, waits for them, and re-layouts  4.78 us

profile of v5, /device:TPU:1, one launch (start us, length us, event | category | flops | bytes accessed | tf_op | source)
XLA Modules:
  0.0 105.6 jit_solution(18306546456845226558)
XLA Ops:
  0.6 100.2 %layer.1 = (bf16[128,2048]{1,0:T(8,128)(2,1)}, bf16[128,4096]{1,0:T(8,128)(2,1)}, bf16[128,2048]{1,0:T(8,128)(2,1)}, f32[16,512]{1,0:T(8,128)}) custom-call(bf16[512,512]{1,0:T(8,128)(2,1)} %w_ref.1, bf16[128,4096]{1,0:T(8,128)(2,1)} %bitcast.6, bf16[128,2048]{1,0:T(8,128)(2,1)} %bitcast.8, bf16[128,2048]{1,0:T(8,128)(2,1)} %bitcast.9), custom_call_target="tpu_custom_call" | custom-call | tf_op jit(solution)/shard_map/layer/pallas_call | solution.py:540
  100.9 0.0 copy-start
  100.9 2.0 %copy.12 = bf16[1,128,2048]{2,1,0:T(8,128)(2,1)} copy(bf16[1,128,2048]{2,1,0:T(8,128)(2,1)} %bitcast.11) | data formatting | bytes 1048576
  102.8 0.0 copy-done
  102.8 0.0 copy-start.1
  102.8 1.0 copy.13
  103.8 0.4 copy-done.1
  104.2 0.0 copy-start.2
  104.2 0.8 copy.14
  105.0 0.0 copy-done.2
  105.0 0.6 copy.15
Async XLA Ops:
  100.9 2.0 %copy-start = (bf16[128,4096]{1,0:T(8,128)(2,1)S(1)}, bf16[128,4096]{1,0:T(8,128)(2,1)}, u32[]{:S(2)}) copy-start(bf16[128,4096]{1,0:T(8,128)(2,1)} %get-tuple-element.9) | copy-start | bytes 3145732
  102.8 1.4 %copy-start.1 = (bf16[128,2048]{1,0:T(8,128)(2,1)S(1)}, bf16[128,2048]{1,0:T(8,128)(2,1)}, u32[]{:S(2)}) copy-start(bf16[128,2048]{1,0:T(8,128)(2,1)} %get-tuple-element.10) | copy-start | bytes 1572868
  104.2 0.8 copy-start.2

commit v6 on v5

--- a/solution.py
+++ b/solution.py
@@ -33,11 +33,15 @@
     )
 
 
-def greet(peers):
-    barrier = pltpu.get_barrier_semaphore()
+def meet(peers):
     for where in peers:
-        pl.semaphore_signal(barrier, inc=1, device_id=where, device_id_type=MESH)
-    pl.semaphore_wait(barrier, len(peers))
+        pl.semaphore_signal(
+            pltpu.get_barrier_semaphore(), inc=1, device_id=where, device_id_type=MESH
+        )
+
+
+def met(count):
+    pl.semaphore_wait(pltpu.get_barrier_semaphore(), count)
 
 
 def across(dp, dz, dx):
@@ -137,9 +141,10 @@
 
 def layer_kernel(
     w_ref, tok_ref, v_ref, g_ref, att_ref, gt_ref, gv_ref, gp_ref,
-    wc, w_far, tok2, v2, g2, proj, projt, state, yin, tz, zin, yout, pre, prefix, suffix,
-    carried, yin_b, zin_b, yout_b, tz_b, work, gn, att2, gv2, acc, rows2, r_far, r_all, cols,
-    all_ref, grad, sib, pair, yred, ysum, zred, send, recv, local_sem,
+    wq, wk, wq_far, wk_far, tok2, v2, g2, proj, projt, state, yin, tz, zin, yout, pre, prefix,
+    suffix, carried, yin_b, zin_b, yout_b, tz_b, work, gn, att2, gv2, acc, rows_q, rows_k, rq_far,
+    rk_far, rq_all, rk_all, cols, all_q, all_k, grad_q, grad_k, sib, pair, yred, ysum, zred,
+    send, recv, local_sem,
 ):
     dp = lax.axis_index("dp")
     z, y, c = place()
@@ -162,21 +167,27 @@
         return copy
 
     own_rows = aligned(dp * rows, rows)
-    for n in range(2):
-        wc[own_rows, n * HF : (n + 1) * HF] = w_ref[:, aligned(n * 2 * HF + c * HF, HF)]
-    greet(
+    meet(
         [{"ctx": partner}]
         + [{"ctx": at(z, (y + d) % NY, c)} for d in range(1, NY)]
         + [{"ctx": at((z + d) % NZ, y, c)} for d in range(1, NZ)]
         + [{"dp": across(dp, n // 4, n % 4)} for n in range(1, NDP)]
     )
+    here = [
+        copy_here(tok_ref, tok2.at[ours]),
+        copy_here(v_ref.at[:, own_half], v2.at[ours]),
+        copy_here(g_ref.at[:, own_half], g2.at[ours]),
+    ]
+    wk[own_rows, :] = w_ref[:, aligned(2 * HF + c * HF, HF)]
+    wq[own_rows, :] = w_ref[:, aligned(c * HF, HF)]
+    met(NY + NZ + NDP - 2)
 
     wide = rows // 2
     thin = wide // NY
     base_a, base_b = 0, wide
 
     def part(owner, start, size):
-        return wc.at[aligned(owner * rows + start, size, thin // 2)]
+        return wk.at[aligned(owner * rows + start, size, thin // 2)]
 
     def own_sends(start, size):
         piece = part(dp, start, size)
@@ -202,11 +213,6 @@
         wires.push(tok_ref, tok2.at[ours], ctx=partner),
         wires.push(v_ref.at[:, their_half], v2.at[ours], ctx=partner),
         wires.push(g_ref.at[:, their_half], g2.at[ours], ctx=partner),
-    ]
-    here = [
-        copy_here(tok_ref, tok2.at[ours]),
-        copy_here(v_ref.at[:, own_half], v2.at[ours]),
-        copy_here(g_ref.at[:, own_half], g2.at[ours]),
     ]
     owners = [other, left, right] + [across(dp, dz, dx) for dz, dx in ((1, 3), (1, 1), (0, 2), (1, 2))]
     chain_y = []
@@ -251,19 +257,31 @@
     a_right2.wait_recv()
     a_left2.wait_recv()
     a_ends2 = relay(owners[3], owners[4], base_a, wide)
+
+    def query_part(owner):
+        return wq.at[aligned(owner * rows, rows)]
+
+    def query_halves(near, far):
+        one = wq.at[aligned(near * rows, wide)]
+        two = wq.at[aligned(far * rows + wide, wide)]
+        return wires.push(one, one, dp=right), wires.push(two, two, dp=left)
+
+    q_over, q_right, q_left = [
+        wires.push(query_part(dp), query_part(dp), dp=to) for to in (other, right, left)
+    ]
     for n in range(3, 7):
         relay_y(n)
 
-    def project(owner):
+    def project(weight, owner):
         return dot(
-            tok2[:, aligned(owner * rows, rows)], wc[aligned(owner * rows, rows), :], 1, 0
+            tok2[:, aligned(owner * rows, rows)], weight[aligned(owner * rows, rows), :], 1, 0
         )
 
     for copy in from_partner:
         copy.wait_recv()
     for copy in here:
         copy.wait()
-    proj[...] = project(dp)
+    proj[...] = project(wk, dp)
     for n in range(7):
         for copy in ends_y[n]:
             copy.wait_recv()
@@ -273,8 +291,8 @@
         if n == 6:
             for copy in a_ends2:
                 copy.wait_recv()
-        proj[...] += project(owners[n])
-    far_weight = wires.push(wc, w_far, ctx=partner)
+        proj[...] += project(wk, owners[n])
+    far_weight = [wires.push(wk, wk_far, ctx=partner)]
     width = cols.shape[2]
     token_copies = []
 
@@ -285,7 +303,10 @@
                 wires.push(tok_ref.at[:, aligned(peer * width, width)], cols.at[n], dp=peer)
             )
 
-    projt[...] = proj[...].T
+    q_over.wait_recv()
+    q_passed = [wires.push(query_part(other), query_part(other), dp=to) for to in (right, left)]
+
+    projt[HF:, :] = proj[...].T
 
     def query(h):
         return projt[h * F : (h + 1) * F, :]
@@ -303,7 +324,7 @@
         j, at_rows = rows_of(h)
         state[j, at_rows, :] = new.astype(BF16)
 
-    def scan(later, src, land, total_ref, planes, out, result, fill_y, fill_z):
+    def scan(later, src, land, total_ref, planes, out, result, fill_y, fill_z, fill_b):
         copies = []
         for d in (2, 1, 3):
             to = (y + d) % NY
@@ -334,6 +355,7 @@
             to = (y + d) % NY
             copies.append(wires.push(out.at[to], result.at[y], ctx=at(z, to, c)))
         result[y] = out[y]
+        fill_b()
         for copy in copies:
             copy.wait_recv()
 
@@ -347,17 +369,34 @@
             jnp.concatenate(split(kernel), axis=1), jnp.concatenate([v, v], axis=0), 1, 0
         )
 
+    q_ends = []
+
     def first_fill():
+        q_right.wait_recv()
+        q_left.wait_recv()
+        q_ends.append(query_halves(left, right))
+
+    def second_fill():
+        for copy in q_passed:
+            copy.wait_recv()
+        q_ends.append(query_halves(owners[3], owners[4]))
+        proj[...] = project(wq, dp)
+        for n in range(5):
+            proj[...] += project(wq, owners[n])
+        for n in range(2):
+            for copy in q_ends[n]:
+                copy.wait_recv()
+            proj[...] += project(wq, owners[5 + n])
+        projt[:HF, :] = proj[...].T
+        far_weight.append(wires.push(wq, wq_far, ctx=partner))
         send_tokens((1, 2, 3))
-        for h in range(3):
+        for h in range(H):
             local_numerator(h)
 
-    def second_fill():
+    def send_rest():
         send_tokens((4, 5, 6, 7))
-        for h in range(3, H):
-            local_numerator(h)
-
-    scan(False, state, yin, tz, zin, yout, prefix, first_fill, second_fill)
+
+    scan(False, state, yin, tz, zin, yout, prefix, first_fill, second_fill, send_rest)
 
     for h in range(H):
         j, at_rows = rows_of(h)
@@ -404,18 +443,82 @@
         )
 
     outs = []
+    half = count // 2
+    low_rows, high_rows = pl.ds(0, half), pl.ds(half, half)
+
+    class Gathered:
+        def __init__(self, mine, far, both, land):
+            self.mine, self.far, self.both, self.land = mine, far, both, land
+
+        def swap(self):
+            self.swapped = wires.push(self.mine.at[theirs], self.far, ctx=partner)
+
+        def start(self):
+            self.both[:, aligned(c * HF, HF)] = self.mine[ours, :]
+            self.swapped.wait_recv()
+            self.both[:, aligned((1 - c) * HF, HF)] = self.far[...]
+            self.over = wires.push(self.both, self.land.at[4], dp=other)
+            self.near = [
+                (
+                    wires.push(self.both, self.land.at[1], dp=right),
+                    wires.push(self.both, self.land.at[3], dp=left),
+                )
+            ]
+            self.ends = []
+
+        def pass_on(self):
+            self.over.wait_recv()
+            self.near.append(
+                (
+                    wires.push(self.land.at[4], self.land.at[5], dp=right),
+                    wires.push(self.land.at[4], self.land.at[7], dp=left),
+                )
+            )
+
+        def relay(self, n):
+            at_slot = 4 * n
+            self.near[n][0].wait_recv()
+            self.ends.append(
+                wires.push(
+                    self.land.at[at_slot + 1, low_rows], self.land.at[at_slot + 2, low_rows],
+                    dp=right,
+                )
+            )
+            self.near[n][1].wait_recv()
+            self.ends.append(
+                wires.push(
+                    self.land.at[at_slot + 3, high_rows], self.land.at[at_slot + 2, high_rows],
+                    dp=left,
+                )
+            )
+
+        def finish(self):
+            for copy in self.ends:
+                copy.wait_recv()
+
+    queries = Gathered(rows_q, rq_far, rq_all, all_q)
+    keys = Gathered(rows_k, rk_far, rk_all, all_k)
 
     def third_fill():
         outs.append(wires.push(att2.at[theirs], att_ref.at[:, own_half], ctx=partner))
         copy_here(att2.at[ours], att_ref.at[:, own_half])
-        for h in range(3):
+        for h in range(4):
             local_grads(h)
 
     def fourth_fill():
-        for h in range(3, H):
+        for h in range(4, H):
             local_grads(h)
-
-    scan(True, carried, yin_b, tz_b, zin_b, yout_b, suffix, third_fill, fourth_fill)
+        rows_q[...] = acc[:HF, :].T.astype(BF16)
+        queries.swap()
+        queries.start()
+
+    def fifth_fill():
+        queries.pass_on()
+        queries.relay(0)
+
+    scan(
+        True, carried, yin_b, tz_b, zin_b, yout_b, suffix, third_fill, fourth_fill, fifth_fill
+    )
 
     for h in range(H):
         j, at_rows = rows_of(h)
@@ -423,27 +526,17 @@
         k = key(h)
         span = slice(HF + h * F, HF + (h + 1) * F)
         acc[span, :] = acc[span, :] + pull_features(k, dot(after, v2[:, head(h)], 1, 1))
-    rows2[...] = acc[...].T.astype(BF16)
-
-    swap = wires.push(rows2.at[theirs], r_far, ctx=partner)
+    rows_k[...] = acc[HF:, :].T.astype(BF16)
+    keys.swap()
+    queries.relay(1)
+    keys.start()
     for h in range(H):
         j, at_rows = rows_of(h)
         total = work[:, head(h)] + product(features(key(h), True), suffix[j, at_rows, :])
         gv2[:, head(h)] = total.astype(BF16)
-    for n in range(2):
-        r_all[:, aligned(n * 2 * HF + c * HF, HF)] = rows2[ours, n * HF : (n + 1) * HF]
-    swap.wait_recv()
-    for n in range(2):
-        r_all[:, aligned(n * 2 * HF + (1 - c) * HF, HF)] = r_far[:, n * HF : (n + 1) * HF]
-    half = count // 2
-    low_rows, high_rows = pl.ds(0, half), pl.ds(half, half)
-    over = wires.push(r_all, all_ref.at[4], dp=other)
-    rights = [wires.push(r_all, all_ref.at[1], dp=right)]
-    lefts = [wires.push(r_all, all_ref.at[3], dp=left)]
     outs.append(wires.push(gv2.at[theirs], gv_ref.at[:, own_half], ctx=partner))
     copy_here(gv2.at[ours], gv_ref.at[:, own_half])
-    far_weight.wait_recv()
-    for copy in token_copies:
+    for copy in token_copies + far_weight:
         copy.wait_recv()
 
     def tokens_of(n):
@@ -451,74 +544,118 @@
             return tok2[ours, aligned(dp * width, width)]
         return cols[n]
 
-    def product_of(slots):
+    def product_of(part_rows, slots):
         left_rows = jnp.concatenate([tokens_of(n) for n in slots], axis=0)
-        right_rows = jnp.concatenate([r_all[...] if n == 0 else all_ref[n] for n in slots], axis=0)
-        return dot(left_rows, right_rows, 0, 0).reshape(grad.shape)
-
-    block = wc.shape[0] // 4
+        right_rows = jnp.concatenate(
+            [part_rows.both[...] if n == 0 else part_rows.land[n] for n in slots], axis=0
+        )
+        return dot(left_rows, right_rows, 0, 0).reshape(grad_q.shape)
+
+    block = wq.shape[0] // 4
 
     def input_grad(n):
         span = slice(n * block, (n + 1) * block)
-        piece = dot(rows2[ours, :], wc[span, :], 1, 1)
-        piece += dot(r_far[...], w_far[span, :], 1, 1)
+        near_rows = jnp.concatenate([rows_q[ours, :], rows_k[ours, :]], axis=1)
+        far_rows = jnp.concatenate([rq_far[...], rk_far[...]], axis=1)
+        piece = dot(near_rows, jnp.concatenate([wq[span, :], wk[span, :]], axis=1), 1, 1)
+        piece += dot(far_rows, jnp.concatenate([wq_far[span, :], wk_far[span, :]], axis=1), 1, 1)
         gt_ref[:, span] = piece.astype(BF16)
 
-    over.wait_recv()
-    rights.append(wires.push(all_ref.at[4], all_ref.at[5], dp=right))
-    lefts.append(wires.push(all_ref.at[4], all_ref.at[7], dp=left))
+    class Reduced:
+        def __init__(self, n, grad):
+            self.n, self.grad = n, grad
+
+        def chip(self):
+            n = self.n
+            self.halves = {
+                d: wires.push(
+                    self.grad.at[:, (y + d) % NY, 1 - c], sib.at[n, (y + d) % NY], ctx=partner
+                )
+                for d in (2, 1, 3, 0)
+            }
+
+        def over_y(self):
+            n = self.n
+            self.near = []
+            for d in (2, 1, 3, 0):
+                to = (y + d) % NY
+                self.halves[d].wait_recv()
+                both = self.grad[:, to, c] + sib[n, to]
+                if d == 0:
+                    ysum[n] = both
+                else:
+                    pair[n, to] = both.astype(BF16)
+                    self.near.append(
+                        wires.push(pair.at[n, to], yred.at[n, y], ctx=at(z, to, c))
+                    )
+
+        def over_z(self):
+            n = self.n
+            for copy in self.near:
+                copy.wait_recv()
+            for j in range(NY):
+                ysum[n] += jnp.where(j == y, 0.0, yred[n, j].astype(F32))
+            self.planes = [
+                wires.push(ysum.at[n, (z + d) % NZ], zred.at[n, z], ctx=at((z + d) % NZ, y, c))
+                for d in (2, 1, 3)
+            ]
+
+        def finish(self):
+            n = self.n
+            for copy in self.planes:
+                copy.wait_recv()
+            total = ysum[n, z]
+            for j in range(NZ):
+                total = total + jnp.where(j == z, 0.0, zred[n, j])
+            span = total.shape[1]
+            gp_ref[:, n * span : (n + 1) * span] = total
+
+    first, second = Reduced(0, grad_q), Reduced(1, grad_k)
+    queries.finish()
+    grad_q[...] = product_of(queries, range(NDP))
+    first.chip()
+    keys.pass_on()
+    keys.relay(0)
+    first.over_y()
     input_grad(0)
-    ends = []
-    for n in range(2):
-        rights[n].wait_recv()
-        ends.append(
-            wires.push(all_ref.at[4 * n + 1, low_rows], all_ref.at[4 * n + 2, low_rows], dp=right)
-        )
-        lefts[n].wait_recv()
-        ends.append(
-            wires.push(all_ref.at[4 * n + 3, high_rows], all_ref.at[4 * n + 2, high_rows], dp=left)
-        )
-        input_grad(2 * n + 1)
-        if n == 0:
-            grad[...] = product_of((0, 1, 3, 4))
-            input_grad(2)
-    for copy in ends:
-        copy.wait_recv()
-    grad[...] += product_of((2, 5, 6, 7))
-
-    copies_c = {}
-    for d in (2, 1, 3, 0):
-        to = (y + d) % NY
-        copies_c[d] = wires.push(grad.at[:, to, 1 - c], sib.at[to], ctx=partner)
-    near = []
-    for d in (2, 1, 3, 0):
-        to = (y + d) % NY
-        copies_c[d].wait_recv()
-        both = grad[:, to, c] + sib[to]
-        if d == 0:
-            ysum[...] = both
-        else:
-            pair[to] = both.astype(BF16)
-            near.append(wires.push(pair.at[to], yred.at[y], ctx=at(z, to, c)))
-    for copy in near:
-        copy.wait_recv()
-    for j in range(NY):
-        ysum[...] += jnp.where(j == y, 0.0, yred[j].astype(F32))
-    copies_z = []
-    for d in (2, 1, 3):
-        to = (z + d) % NZ
-        copies_z.append(wires.push(ysum.at[to], zred.at[z], ctx=at(to, y, c)))
-    for copy in copies_z:
-        copy.wait_recv()
-    total = ysum[z]
-    for j in range(NZ):
-        total = total + jnp.where(j == z, 0.0, zred[j])
-    gp_ref[...] = total
+    grad_k[...] = product_of(keys, (0, 1, 3, 4))
+    keys.relay(1)
+    input_grad(1)
+    first.over_z()
+    keys.finish()
+    grad_k[...] += product_of(keys, (2, 5, 6, 7))
+    second.chip()
+    input_grad(2)
+    second.over_y()
+    input_grad(3)
+    first.finish()
+    second.over_z()
+    second.finish()
     for copy in outs:
         copy.wait_recv()
     for copy in locals_[3:]:
         copy.wait()
     wires.drain()
+
+
+def hand_over_kernel(*refs):
+    for src, dst in zip(refs[:3], refs[3:]):
+        dst[...] = src[...]
+
+
+def hand_over(*arrays):
+    steps = 4
+    specs = [
+        pl.BlockSpec((a.shape[0], a.shape[1] // steps), lambda i: (0, i)) for a in arrays
+    ]
+    return pl.pallas_call(
+        hand_over_kernel,
+        grid=(steps,),
+        out_shape=[jax.ShapeDtypeStruct(a.shape, a.dtype) for a in arrays],
+        in_specs=specs,
+        out_specs=specs,
+        name="hand_over",
+    )(*arrays)
 
 
 def local(tokens, proj_weight, values, grad_out):
@@ -548,12 +685,14 @@
         in_specs=[VMEM, hbm, hbm, hbm],
         out_specs=(VMEM,) * 4,
         scratch_shapes=[
-            half(model, 2 * HF),
-            half(model, 2 * HF),
+            half(model, HF),
+            half(model, HF),
+            half(model, HF),
+            half(model, HF),
             half(both, model),
             half(both, HD),
             half(both, HD),
-            full(both, 2 * HF),
+            full(both, HF),
             full(2 * HF, both),
             half(*parts),
             half(*parts),
@@ -573,24 +712,30 @@
             half(both, HD),
             half(both, HD),
             full(2 * HF, both),
-            half(both, 2 * HF),
+            half(both, HF),
+            half(both, HF),
+            half(count, HF),
+            half(count, HF),
             half(count, 2 * HF),
-            half(count, width),
+            half(count, 2 * HF),
             half(NDP, count, shard),
-            half(NDP, count, width),
-            full(NZ, NY, 2, own, width),
-            full(NY, NZ, own, width),
-            half(NY, NZ, own, width),
-            half(NY, NZ, own, width),
-            full(NZ, own, width),
-            full(NZ, own, width),
-            dma((112,)),
-            dma((112,)),
+            half(NDP, count, 2 * HF),
+            half(NDP, count, 2 * HF),
+            full(NZ, NY, 2, own, 2 * HF),
+            full(NZ, NY, 2, own, 2 * HF),
+            full(2, NY, NZ, own, 2 * HF),
+            half(2, NY, NZ, own, 2 * HF),
+            half(2, NY, NZ, own, 2 * HF),
+            full(2, NZ, own, 2 * HF),
+            full(2, NZ, own, 2 * HF),
+            dma((144,)),
+            dma((144,)),
             dma((5,)),
         ],
         compiler_params=pltpu.CompilerParams(collective_id=0, has_side_effects=True),
         name="layer",
     )(proj_weight, tok, val, up)
+    attended, grad_tokens, grad_values = hand_over(attended, grad_tokens, grad_values)
     return (attended[None], grad_tokens[None], grad_values[None], grad_proj)
 
 

time: 106 us -> 98.4 us (0.928)
  local copies, waits for them, and re-layouts: 4.78 us -> 0.62 us
  Pallas kernels: 100 us -> 96.9 us
    pallas_call x1, Pallas kernels: 100 us -> 93.2 us  [local(): pl.pallas_call(layer_kernel, out_shape=(jax.ShapeDtypeStruct(val.shape, B...]
    unnamed x10 -> x3, local copies, waits for them, and re-layouts: 4.78 us -> 0.62 us
    pallas_call x0 -> x1, Pallas kernels: none -> 3.76 us  [hand_over(): pl.pallas_call(hand_over_kernel, grid=(steps,), out_shape=[jax.ShapeDtype...]
where the time goes in v6:
time: 98.4 us; the launch traced here: 98.2 us
  Pallas kernels  96.9 us (98%)
    pallas_call x1, Pallas kernels, local(): pl.pallas_call(layer_kernel, out_shape=(jax.ShapeDtypeStruct(val.shape, B...  93.2 us
    pallas_call x1, Pallas kernels, hand_over(): pl.pallas_call(hand_over_kernel, grid=(steps,), out_shape=[jax.ShapeDtype...  3.76 us

profile of v6, /device:TPU:1, one launch (start us, length us, event | category | flops | bytes accessed | tf_op | source)
XLA Modules:
  0.0 98.2 jit_solution(15478578264918949565)
XLA Ops:
  0.6 93.2 %layer.1 = (bf16[128,2048]{1,0:T(8,128)(2,1)}, bf16[128,4096]{1,0:T(8,128)(2,1)}, bf16[128,2048]{1,0:T(8,128)(2,1)}, f32[16,512]{1,0:T(8,128)}) custom-call(bf16[512,512]{1,0:T(8,128)(2,1)} %w_ref.1, bf16[128,4096]{1,0:T(8,128)(2,1)} %bitcast.6, bf16[128,2048]{1,0:T(8,128)(2,1)} %bitcast.7, bf16[128,2048]{1,0:T(8,128)(2,1)} %bitcast.8), custom_call_target="tpu_custom_call" | custom-call | tf_op jit(solution)/shard_map/layer/pallas_call | solution.py:677
  93.8 0.0 copy-start
  93.8 3.8 %hand_over.1 = (bf16[128,2048]{1,0:T(8,128)(2,1)}, bf16[128,4096]{1,0:T(8,128)(2,1)}, bf16[128,2048]{1,0:T(8,128)(2,1)}) custom-call(bf16[128,2048]{1,0:T(8,128)(2,1)} %get-tuple-element.11.refs_0_, bf16[128,4096]{1,0:T(8,128)(2,1)} %get-tuple-element.12.refs_1_, bf16[128,2048]{1,0:T(8,128)(2,1)} %get-tuple-element.13.refs_2_), custom_call_target="tpu_custom_call" | custom-call | tf_op jit(solution)/shard_map/hand_over/pallas_call | solution.py:651
  97.6 0.0 copy-done
  97.6 0.6 copy.9
Async XLA Ops:
  93.8 3.8 %copy-start = (f32[16,512]{1,0:T(8,128)S(1)}, f32[16,512]{1,0:T(8,128)}, u32[]{:S(2)}) copy-start(f32[16,512]{1,0:T(8,128)} %get-tuple-element.25) | copy-start | bytes 98308

commit v7 on v6

--- a/solution.py
+++ b/solution.py
@@ -390,11 +390,13 @@
         projt[:HF, :] = proj[...].T
         far_weight.append(wires.push(wq, wq_far, ctx=partner))
         send_tokens((1, 2, 3))
-        for h in range(H):
+        for h in range(2):
             local_numerator(h)
 
     def send_rest():
         send_tokens((4, 5, 6, 7))
+        for h in range(2, H):
+            local_numerator(h)
 
     scan(False, state, yin, tz, zin, yout, prefix, first_fill, second_fill, send_rest)
 
@@ -502,11 +504,11 @@
     def third_fill():
         outs.append(wires.push(att2.at[theirs], att_ref.at[:, own_half], ctx=partner))
         copy_here(att2.at[ours], att_ref.at[:, own_half])
-        for h in range(4):
+        for h in range(5):
             local_grads(h)
 
     def fourth_fill():
-        for h in range(4, H):
+        for h in range(5, H):
             local_grads(h)
         rows_q[...] = acc[:HF, :].T.astype(BF16)
         queries.swap()
@@ -530,12 +532,21 @@
     keys.swap()
     queries.relay(1)
     keys.start()
-    for h in range(H):
+
+    def value_grad(h):
         j, at_rows = rows_of(h)
         total = work[:, head(h)] + product(features(key(h), True), suffix[j, at_rows, :])
         gv2[:, head(h)] = total.astype(BF16)
+
+    for h in range(4):
+        value_grad(h)
+    keys.pass_on()
+    for h in range(4, H):
+        value_grad(h)
     outs.append(wires.push(gv2.at[theirs], gv_ref.at[:, own_half], ctx=partner))
     copy_here(gv2.at[ours], gv_ref.at[:, own_half])
+    keys.relay(0)
+    keys.relay(1)
     for copy in token_copies + far_weight:
         copy.wait_recv()
 
@@ -614,22 +625,19 @@
     queries.finish()
     grad_q[...] = product_of(queries, range(NDP))
     first.chip()
-    keys.pass_on()
-    keys.relay(0)
+    grad_k[...] = product_of(keys, (0, 1, 3, 4, 5, 7))
     first.over_y()
+    keys.finish()
+    grad_k[...] += product_of(keys, (2, 6))
+    second.chip()
     input_grad(0)
-    grad_k[...] = product_of(keys, (0, 1, 3, 4))
-    keys.relay(1)
+    second.over_y()
+    first.over_z()
     input_grad(1)
-    first.over_z()
-    keys.finish()
-    grad_k[...] += product_of(keys, (2, 5, 6, 7))
-    second.chip()
     input_grad(2)
-    second.over_y()
+    second.over_z()
     input_grad(3)
     first.finish()
-    second.over_z()
     second.finish()
     for copy in outs:
         copy.wait_recv()
@@ -639,21 +647,36 @@
 
 
 def hand_over_kernel(*refs):
-    for src, dst in zip(refs[:3], refs[3:]):
-        dst[...] = src[...]
+    srcs, dsts, holds, sems = refs[:3], refs[3:6], refs[6:9], refs[9]
+    pieces = [(n, at_half) for at_half in range(2) for n in range(3)]
+    reads, writes = [], []
+    for i, (n, at_half) in enumerate(pieces):
+        size = holds[n].shape[0] // 2
+        rows = pl.ds(at_half * size, size)
+        reads.append(
+            pltpu.make_async_copy(srcs[n].at[rows], holds[n].at[rows], sems.at[0, i])
+        )
+        writes.append(
+            pltpu.make_async_copy(holds[n].at[rows], dsts[n].at[rows], sems.at[1, i])
+        )
+    for copy in reads:
+        copy.start()
+    for read, write in zip(reads, writes):
+        read.wait()
+        write.start()
+    for copy in writes:
+        copy.wait()
 
 
 def hand_over(*arrays):
-    steps = 4
-    specs = [
-        pl.BlockSpec((a.shape[0], a.shape[1] // steps), lambda i: (0, i)) for a in arrays
-    ]
+    hbm = pl.BlockSpec(memory_space=pl.ANY)
     return pl.pallas_call(
         hand_over_kernel,
-        grid=(steps,),
         out_shape=[jax.ShapeDtypeStruct(a.shape, a.dtype) for a in arrays],
-        in_specs=specs,
-        out_specs=specs,
+        in_specs=[hbm] * 3,
+        out_specs=[hbm] * 3,
+        scratch_shapes=[pltpu.VMEM(a.shape, a.dtype) for a in arrays]
+        + [pltpu.SemaphoreType.DMA((2, 6))],
         name="hand_over",
     )(*arrays)
 

time: 98.4 us -> 96.4 us (0.980)
  Pallas kernels: 96.9 us -> 94.9 us
    pallas_call x1, Pallas kernels: 3.76 us -> 2.45 us  [hand_over(): pl.pallas_call(hand_over_kernel, out_shape=[jax.ShapeDtypeStruct(a.shape,...]
where the time goes in v7:
time: 96.4 us; the launch traced here: 96.2 us
  Pallas kernels  94.9 us (98%)
    pallas_call x1, Pallas kernels, local(): pl.pallas_call(layer_kernel, out_shape=(jax.ShapeDtypeStruct(val.shape, B...  92.4 us
    pallas_call x1, Pallas kernels, hand_over(): pl.pallas_call(hand_over_kernel, out_shape=[jax.ShapeDtypeStruct(a.shape,...  2.45 us

profile of v7, /device:TPU:1, one launch (start us, length us, event | category | flops | bytes accessed | tf_op | source)
XLA Modules:
  0.0 96.2 jit_solution(861284743031295367)
XLA Ops:
  0.6 92.4 %layer.1 = (bf16[128,2048]{1,0:T(8,128)(2,1)}, bf16[128,4096]{1,0:T(8,128)(2,1)}, bf16[128,2048]{1,0:T(8,128)(2,1)}, f32[16,512]{1,0:T(8,128)}) custom-call(bf16[512,512]{1,0:T(8,128)(2,1)} %w_ref.1, bf16[128,4096]{1,0:T(8,128)(2,1)} %bitcast.6, bf16[128,2048]{1,0:T(8,128)(2,1)} %bitcast.7, bf16[128,2048]{1,0:T(8,128)(2,1)} %bitcast.8), custom_call_target="tpu_custom_call" | custom-call | tf_op jit(solution)/shard_map/layer/pallas_call | solution.py:700
  93.1 0.0 copy-start
  93.1 2.5 %hand_over.1 = (bf16[128,2048]{1,0:T(8,128)(2,1)}, bf16[128,4096]{1,0:T(8,128)(2,1)}, bf16[128,2048]{1,0:T(8,128)(2,1)}) custom-call(bf16[128,2048]{1,0:T(8,128)(2,1)} %get-tuple-element.11.refs_0_, bf16[128,4096]{1,0:T(8,128)(2,1)} %get-tuple-element.12.refs_1_, bf16[128,2048]{1,0:T(8,128)(2,1)} %get-tuple-element.13.refs_2_), custom_call_target="tpu_custom_call" | custom-call | tf_op jit(solution)/shard_map/hand_over/pallas_call | solution.py:673
  95.5 0.0 copy-done
  95.5 0.6 copy.9
Async XLA Ops:
  93.1 2.5 %copy-start = (f32[16,512]{1,0:T(8,128)S(1)}, f32[16,512]{1,0:T(8,128)}, u32[]{:S(2)}) copy-start(f32[16,512]{1,0:T(8,128)} %get-tuple-element.25) | copy-start | bytes 98308

commit v8 on v7

--- a/solution.py
+++ b/solution.py
@@ -149,7 +149,6 @@
     dp = lax.axis_index("dp")
     z, y, c = place()
     partner = at(z, y, 1 - c)
-    up, down = at(z, (y + 1) % NY, c), at(z, (y + 3) % NY, c)
     right, left, other = across(dp, 0, 1), across(dp, 0, 3), across(dp, 1, 0)
     count = tok_ref.shape[0]
     rows = w_ref.shape[0]
@@ -182,8 +181,9 @@
     wq[own_rows, :] = w_ref[:, aligned(c * HF, HF)]
     met(NY + NZ + NDP - 2)
 
-    wide = rows // 2
-    thin = wide // NY
+    wide = 3 * rows // 4
+    thin = (rows - wide) // NY
+    half_rows = rows // 2
     base_a, base_b = 0, wide
 
     def part(owner, start, size):
@@ -204,7 +204,9 @@
 
     def over_y(owner):
         piece = part(owner, base_b + y * thin, thin)
-        return wires.push(piece, piece, ctx=up), wires.push(piece, piece, ctx=down)
+        return [
+            wires.push(piece, piece, ctx=at(z, (y + d) % NY, c)) for d in (2, 1, 3)
+        ]
 
     mine_b = base_b + y * thin
     b_over, b_right, b_left = own_sends(mine_b, thin)
@@ -240,20 +242,6 @@
     for copy in b_ends2:
         copy.wait_recv()
     chain_y.append(over_y(owners[6]))
-    ends_y = []
-    below = base_b + (y + 3) % NY * thin
-    above = base_b + (y + 1) % NY * thin + thin // 2
-
-    def relay_y(n):
-        chain_y[n][0].wait_recv()
-        one = part(owners[n], below, thin // 2)
-        ends_y.append([wires.push(one, one, ctx=up)])
-        chain_y[n][1].wait_recv()
-        two = part(owners[n], above, thin // 2)
-        ends_y[-1].append(wires.push(two, two, ctx=down))
-
-    for n in range(3):
-        relay_y(n)
     a_right2.wait_recv()
     a_left2.wait_recv()
     a_ends2 = relay(owners[3], owners[4], base_a, wide)
@@ -262,15 +250,13 @@
         return wq.at[aligned(owner * rows, rows)]
 
     def query_halves(near, far):
-        one = wq.at[aligned(near * rows, wide)]
-        two = wq.at[aligned(far * rows + wide, wide)]
+        one = wq.at[aligned(near * rows, half_rows)]
+        two = wq.at[aligned(far * rows + half_rows, half_rows)]
         return wires.push(one, one, dp=right), wires.push(two, two, dp=left)
 
     q_over, q_right, q_left = [
         wires.push(query_part(dp), query_part(dp), dp=to) for to in (other, right, left)
     ]
-    for n in range(3, 7):
-        relay_y(n)
 
     def project(weight, owner):
         return dot(
@@ -283,7 +269,7 @@
         copy.wait()
     proj[...] = project(wk, dp)
     for n in range(7):
-        for copy in ends_y[n]:
+        for copy in chain_y[n]:
             copy.wait_recv()
         if n == 5:
             for copy in a_ends:
@@ -309,28 +295,35 @@
     projt[HF:, :] = proj[...].T
 
     def query(h):
-        return projt[h * F : (h + 1) * F, :]
+        return projt[aligned(h * F, F), :]
 
     def key(h):
-        return projt[HF + h * F : HF + (h + 1) * F, :]
+        return projt[aligned(HF + h * F, F), :]
 
     def head(h):
-        return slice(h * DH, (h + 1) * DH)
-
-    for h in range(H):
-        high, low = split(features(key(h), False))
-        v = v2[:, head(h)]
-        new = dot(jnp.concatenate([high, low], axis=1), jnp.concatenate([v, v], axis=0), 1, 0)
-        j, at_rows = rows_of(h)
-        state[j, at_rows, :] = new.astype(BF16)
-
-    def scan(later, src, land, total_ref, planes, out, result, fill_y, fill_z, fill_b):
-        copies = []
-        for d in (2, 1, 3):
-            to = (y + d) % NY
-            copies.append(wires.push(src.at[to], land.at[y], ctx=at(z, to, c)))
+        return aligned(h * DH, DH)
+
+    def send_part(src, land, j):
+        return wires.push(src.at[j], land.at[y], ctx=at(z, j, c))
+
+    def arrived(copies, d):
+        copies[NY - d].wait_recv()
+
+    sent = {}
+    for d in (2, 1, 3, 0):
+        j = (y + d) % NY
+        for e in range(2):
+            h = 2 * j + e
+            high, low = split(features(key(h), False))
+            v = v2[:, head(h)]
+            new = dot(jnp.concatenate([high, low], axis=1), jnp.concatenate([v, v], axis=0), 1, 0)
+            state[j, e * EP : (e + 1) * EP, :] = new.astype(BF16)
+        if d:
+            sent[d] = send_part(state, yin, j)
+
+    def scan(later, sent, src, land, total_ref, planes, out, result, fill_y, fill_z, fill_b):
         fill_y()
-        for copy in copies:
+        for copy in sent.values():
             copy.wait_recv()
         total = jnp.zeros(pre.shape[1:], F32)
         for j in list(range(NY))[::-1] if later else range(NY):
@@ -350,14 +343,10 @@
             base = base + jnp.where(wanted, planes[j].astype(F32), 0.0)
         for j in range(NY):
             out[j] = (base + pre[j]).astype(BF16)
-        copies = []
-        for d in (2, 1, 3):
-            to = (y + d) % NY
-            copies.append(wires.push(out.at[to], result.at[y], ctx=at(z, to, c)))
+        copies = {d: send_part(out, result, (y + d) % NY) for d in (2, 1, 3)}
         result[y] = out[y]
         fill_b()
-        for copy in copies:
-            copy.wait_recv()
+        return copies
 
     mask = causal()
 
@@ -375,11 +364,11 @@
         q_right.wait_recv()
         q_left.wait_recv()
         q_ends.append(query_halves(left, right))
-
-    def second_fill():
         for copy in q_passed:
             copy.wait_recv()
         q_ends.append(query_halves(owners[3], owners[4]))
+
+    def second_fill():
         proj[...] = project(wq, dp)
         for n in range(5):
             proj[...] += project(wq, owners[n])
@@ -398,10 +387,10 @@
         for h in range(2, H):
             local_numerator(h)
 
-    scan(False, state, yin, tz, zin, yout, prefix, first_fill, second_fill, send_rest)
-
-    for h in range(H):
-        j, at_rows = rows_of(h)
+    back = scan(False, sent, state, yin, tz, zin, yout, prefix, first_fill, second_fill, send_rest)
+
+    def forward_head(j, e):
+        h, at_rows = 2 * j + e, slice(e * EP, (e + 1) * EP)
         q = query(h)
         numerator = work[:, head(h)] + product(features(q, True), prefix[j, at_rows, :])
         inv = lax.rsqrt(jnp.mean(numerator * numerator, axis=1, keepdims=True) + EPSILON)
@@ -416,6 +405,16 @@
             jnp.concatenate([high, low, high], axis=1), jnp.concatenate([gh, gh, gl], axis=0), 1, 0
         )
         carried[j, at_rows, :] = new.astype(BF16)
+
+    sent = {}
+    for d in (0, 1, 3, 2):
+        j = (y + d) % NY
+        if d:
+            arrived(back, d)
+        for e in range(2):
+            forward_head(j, e)
+        if d:
+            sent[d] = send_part(carried, yin_b, j)
 
     def local_grads(h):
         q, k = query(h), key(h)
@@ -518,16 +517,20 @@
         queries.pass_on()
         queries.relay(0)
 
-    scan(
-        True, carried, yin_b, tz_b, zin_b, yout_b, suffix, third_fill, fourth_fill, fifth_fill
+    back = scan(
+        True, sent, carried, yin_b, tz_b, zin_b, yout_b, suffix, third_fill, fourth_fill, fifth_fill
     )
 
-    for h in range(H):
-        j, at_rows = rows_of(h)
-        after = suffix[j, at_rows, :]
-        k = key(h)
-        span = slice(HF + h * F, HF + (h + 1) * F)
-        acc[span, :] = acc[span, :] + pull_features(k, dot(after, v2[:, head(h)], 1, 1))
+    for d in (0, 1, 3, 2):
+        j = (y + d) % NY
+        if d:
+            arrived(back, d)
+        for e in range(2):
+            h = 2 * j + e
+            after = suffix[j, e * EP : (e + 1) * EP, :]
+            span = aligned(HF + h * F, F)
+            pulled = dot(after, v2[:, head(h)], 1, 1)
+            acc[span, :] = acc[span, :] + pull_features(key(h), pulled)
     rows_k[...] = acc[HF:, :].T.astype(BF16)
     keys.swap()
     queries.relay(1)

time: 96.4 us -> 91.6 us (0.950)
  Pallas kernels: 94.9 us -> 90.1 us
    pallas_call x1, Pallas kernels: 92.4 us -> 87.7 us  [local(): pl.pallas_call(layer_kernel, out_shape=(jax.ShapeDtypeStruct(val.shape, B...]
where the time goes in v8:
time: 91.6 us; the launch traced here: 91.4 us
  Pallas kernels  90.1 us (98%)
    pallas_call x1, Pallas kernels, local(): pl.pallas_call(layer_kernel, out_shape=(jax.ShapeDtypeStruct(val.shape, B...  87.7 us
    pallas_call x1, Pallas kernels, hand_over(): pl.pallas_call(hand_over_kernel, out_shape=[jax.ShapeDtypeStruct(a.shape,...  2.45 us

profile of v8, /device:TPU:1, one launch (start us, length us, event | category | flops | bytes accessed | tf_op | source)
XLA Modules:
  0.0 91.4 jit_solution(5257736281597082905)
XLA Ops:
  0.6 87.7 %layer.1 = (bf16[128,2048]{1,0:T(8,128)(2,1)}, bf16[128,4096]{1,0:T(8,128)(2,1)}, bf16[128,2048]{1,0:T(8,128)(2,1)}, f32[16,512]{1,0:T(8,128)}) custom-call(bf16[512,512]{1,0:T(8,128)(2,1)} %w_ref.1, bf16[128,4096]{1,0:T(8,128)(2,1)} %bitcast.6, bf16[128,2048]{1,0:T(8,128)(2,1)} %bitcast.7, bf16[128,2048]{1,0:T(8,128)(2,1)} %bitcast.8), custom_call_target="tpu_custom_call" | custom-call | tf_op jit(solution)/shard_map/layer/pallas_call | solution.py:703
  88.3 0.0 copy-start
  88.3 2.5 %hand_over.1 = (bf16[128,2048]{1,0:T(8,128)(2,1)}, bf16[128,4096]{1,0:T(8,128)(2,1)}, bf16[128,2048]{1,0:T(8,128)(2,1)}) custom-call(bf16[128,2048]{1,0:T(8,128)(2,1)} %get-tuple-element.11.refs_0_, bf16[128,4096]{1,0:T(8,128)(2,1)} %get-tuple-element.12.refs_1_, bf16[128,2048]{1,0:T(8,128)(2,1)} %get-tuple-element.13.refs_2_), custom_call_target="tpu_custom_call" | custom-call | tf_op jit(solution)/shard_map/hand_over/pallas_call | solution.py:676
  90.8 0.0 copy-done
  90.8 0.6 copy.9
Async XLA Ops:
  88.3 2.5 %copy-start = (f32[16,512]{1,0:T(8,128)S(1)}, f32[16,512]{1,0:T(8,128)}, u32[]{:S(2)}) copy-start(f32[16,512]{1,0:T(8,128)} %get-tuple-element.25) | copy-start | bytes 98308

commit v9 on v8

--- a/solution.py
+++ b/solution.py
@@ -353,10 +353,7 @@
     def local_numerator(h):
         a = scores(query(h), key(h))
         kernel = jnp.where(mask, 1.0 + a + 0.5 * a * a, 0.0)
-        v = v2[:, head(h)]
-        work[:, head(h)] = dot(
-            jnp.concatenate(split(kernel), axis=1), jnp.concatenate([v, v], axis=0), 1, 0
-        )
+        work[:, head(h)] = dot(kernel.astype(BF16), v2[:, head(h)], 1, 0)
 
     q_ends = []
 
@@ -379,12 +376,12 @@
         projt[:HF, :] = proj[...].T
         far_weight.append(wires.push(wq, wq_far, ctx=partner))
         send_tokens((1, 2, 3))
-        for h in range(2):
+        for h in range(4):
             local_numerator(h)
 
     def send_rest():
         send_tokens((4, 5, 6, 7))
-        for h in range(2, H):
+        for h in range(4, H):
             local_numerator(h)
 
     back = scan(False, sent, state, yin, tz, zin, yout, prefix, first_fill, second_fill, send_rest)
@@ -421,17 +418,17 @@
         v = v2[:, head(h)]
         gh, gl = split(gn[:, head(h)])
         a = scores(q, k)
-        mh, ml = split(jnp.where(mask, 1.0 + a + 0.5 * a * a, 0.0))
+        kernel = jnp.where(mask, 1.0 + a + 0.5 * a * a, 0.0).astype(BF16)
         mixing = dot(
             jnp.concatenate([gh, gl], axis=1), jnp.concatenate([v, v], axis=1), 1, 1
         )
-        sh, sl = split(jnp.where(mask, mixing * (1.0 + a) * 0.25, 0.0))
+        slope = jnp.where(mask, mixing * (1.0 + a) * 0.25, 0.0).astype(BF16)
         qh, ql = split(q)
         kh, kl = split(k)
-        dq = dot(jnp.concatenate([kh, kl], axis=0), sh, 1, 1)
-        dq = dq[:F] + dq[F:] + dot(kh, sl, 1, 1)
-        dk = dot(jnp.concatenate([qh, ql], axis=0), sh, 1, 0)
-        dk = dk[:F] + dk[F:] + dot(qh, sl, 1, 0)
+        dq = dot(jnp.concatenate([kh, kl], axis=0), slope, 1, 1)
+        dq = dq[:F] + dq[F:]
+        dk = dot(jnp.concatenate([qh, ql], axis=0), slope, 1, 0)
+        dk = dk[:F] + dk[F:]
         j, at_rows = rows_of(h)
         before = prefix[j, at_rows, :]
         pulled = dot(
@@ -439,9 +436,7 @@
         )
         acc[h * F : (h + 1) * F, :] = dq + pull_features(q, pulled)
         acc[HF + h * F : HF + (h + 1) * F, :] = dk
-        work[:, head(h)] = dot(
-            jnp.concatenate([mh, ml, mh], axis=0), jnp.concatenate([gh, gh, gl], axis=0), 0, 0
-        )
+        work[:, head(h)] = dot(kernel, gh, 0, 0)
 
     outs = []
     half = count // 2
@@ -503,19 +498,17 @@
     def third_fill():
         outs.append(wires.push(att2.at[theirs], att_ref.at[:, own_half], ctx=partner))
         copy_here(att2.at[ours], att_ref.at[:, own_half])
-        for h in range(5):
+        for h in range(4):
             local_grads(h)
 
     def fourth_fill():
-        for h in range(5, H):
+        for h in range(4, H):
             local_grads(h)
         rows_q[...] = acc[:HF, :].T.astype(BF16)
         queries.swap()
+
+    def fifth_fill():
         queries.start()
-
-    def fifth_fill():
-        queries.pass_on()
-        queries.relay(0)
 
     back = scan(
         True, sent, carried, yin_b, tz_b, zin_b, yout_b, suffix, third_fill, fourth_fill, fifth_fill
@@ -533,7 +526,8 @@
             acc[span, :] = acc[span, :] + pull_features(key(h), pulled)
     rows_k[...] = acc[HF:, :].T.astype(BF16)
     keys.swap()
-    queries.relay(1)
+    queries.pass_on()
+    queries.relay(0)
     keys.start()
 
     def value_grad(h):
@@ -548,6 +542,7 @@
         value_grad(h)
     outs.append(wires.push(gv2.at[theirs], gv_ref.at[:, own_half], ctx=partner))
     copy_here(gv2.at[ours], gv_ref.at[:, own_half])
+    queries.relay(1)
     keys.relay(0)
     keys.relay(1)
     for copy in token_copies + far_weight:
@@ -650,8 +645,9 @@
 
 
 def hand_over_kernel(*refs):
-    srcs, dsts, holds, sems = refs[:3], refs[3:6], refs[6:9], refs[9]
-    pieces = [(n, at_half) for at_half in range(2) for n in range(3)]
+    count = len(refs) // 3
+    srcs, dsts, holds, sems = refs[:count], refs[count : 2 * count], refs[2 * count : -1], refs[-1]
+    pieces = [(n, at_half) for at_half in range(2) for n in range(count)]
     reads, writes = [], []
     for i, (n, at_half) in enumerate(pieces):
         size = holds[n].shape[0] // 2
@@ -676,10 +672,10 @@
     return pl.pallas_call(
         hand_over_kernel,
         out_shape=[jax.ShapeDtypeStruct(a.shape, a.dtype) for a in arrays],
-        in_specs=[hbm] * 3,
-        out_specs=[hbm] * 3,
+        in_specs=[hbm] * len(arrays),
+        out_specs=[hbm] * len(arrays),
         scratch_shapes=[pltpu.VMEM(a.shape, a.dtype) for a in arrays]
-        + [pltpu.SemaphoreType.DMA((2, 6))],
+        + [pltpu.SemaphoreType.DMA((2, 2 * len(arrays)))],
         name="hand_over",
     )(*arrays)
 
@@ -761,7 +757,9 @@
         compiler_params=pltpu.CompilerParams(collective_id=0, has_side_effects=True),
         name="layer",
     )(proj_weight, tok, val, up)
-    attended, grad_tokens, grad_values = hand_over(attended, grad_tokens, grad_values)
+    attended, grad_tokens, grad_values, grad_proj = hand_over(
+        attended, grad_tokens, grad_values, grad_proj
+    )
     return (attended[None], grad_tokens[None], grad_values[None], grad_proj)
 
 

time: 91.6 us -> 91.7 us (level)
  no operation moved by 1% of the time
where the time goes in v9:
time: 91.7 us; the launch traced here: 91.6 us
  Pallas kernels  90.8 us (99%)
    pallas_call x1, Pallas kernels, local(): pl.pallas_call(layer_kernel, out_shape=(jax.ShapeDtypeStruct(val.shape, B...  88.3 us
    pallas_call x1, Pallas kernels, hand_over(): pl.pallas_call(hand_over_kernel, out_shape=[jax.ShapeDtypeStruct(a.shape,...  2.49 us

profile of v9, /device:TPU:1, one launch (start us, length us, event | category | flops | bytes accessed | tf_op | source)
XLA Modules:
  0.0 91.6 jit_solution(7335237296597649062)
XLA Ops:
  0.6 88.3 %layer.1 = (bf16[128,2048]{1,0:T(8,128)(2,1)}, bf16[128,4096]{1,0:T(8,128)(2,1)}, bf16[128,2048]{1,0:T(8,128)(2,1)}, f32[16,512]{1,0:T(8,128)}) custom-call(bf16[512,512]{1,0:T(8,128)(2,1)} %w_ref.1, bf16[128,4096]{1,0:T(8,128)(2,1)} %bitcast.6, bf16[128,2048]{1,0:T(8,128)(2,1)} %bitcast.7, bf16[128,2048]{1,0:T(8,128)(2,1)} %bitcast.8), custom_call_target="tpu_custom_call" | custom-call | tf_op jit(solution)/shard_map/layer/pallas_call | solution.py:699
  88.9 2.5 %hand_over.1 = (bf16[128,2048]{1,0:T(8,128)(2,1)}, bf16[128,4096]{1,0:T(8,128)(2,1)}, bf16[128,2048]{1,0:T(8,128)(2,1)}, f32[16,512]{1,0:T(8,128)}) custom-call(bf16[128,2048]{1,0:T(8,128)(2,1)} %get-tuple-element.12.refs_0_, bf16[128,4096]{1,0:T(8,128)(2,1)} %get-tuple-element.13.refs_1_, bf16[128,2048]{1,0:T(8,128)(2,1)} %get-tuple-element.14.refs_2_, ...), custom_call_target="tpu_custom_call" | custom-call | tf_op jit(solution)/shard_map/hand_over/pallas_call | solution.py:672
